TPU v7x, 32 devices: a whole 2x2x4 slice. The times are simulated.
32 devices in a mesh: fsdp: 8 (over z, x), ctx: 4 (over y, core).
Axes of the slice: x: 2, y: 2, z: 4, core: 2. Of those that a mesh axis runs over, the one named last changes fastest.
Arguments:
- tokens: bfloat16 [16, 592, 1024], P('fsdp', 'ctx'), may hold values from -6 to 6
- out_grad: bfloat16 [16, 592, 1024], P('fsdp', 'ctx'), may hold values from -6 to 6
- key_mask: int32 [16, 592], P('fsdp', 'ctx'), may hold values from 0 to 1, as said below
- slot_valid: int32 [16], P('fsdp'), may hold values 0 or 1
- norm_gains: bfloat16 [2, 1024], P(None, 'fsdp'), may hold values from 0.25 to 1.75
- norm_shifts: bfloat16 [2, 1024], P(None, 'fsdp'), may hold values from -2 to 2
- qkv_weight: bfloat16 [1024, 3072], P('fsdp'), may hold values from -0.1875 to 0.1875
- qv_bias: bfloat16 [2, 1024], P(None, 'fsdp'), may hold values from -3 to 3
- out_weight: bfloat16 [1024, 1024], P('fsdp'), may hold values from -1.5 to 1.5
- out_bias: bfloat16 [1024], P('fsdp'), may hold values from -2 to 2
- fc1_weight: bfloat16 [1024, 4096], P('fsdp'), may hold values from -0.1875 to 0.1875
- fc1_bias: bfloat16 [4096], P('fsdp'), may hold values from -3 to 3
- fc2_weight: bfloat16 [4096, 1024], P('fsdp'), may hold values from -0.125 to 0.125
- fc2_bias: bfloat16 [1024], P('fsdp'), may hold values from -2 to 2
Outputs:
- result: bfloat16 [16, 592, 1024], P('fsdp', 'ctx')
- token_gradient: bfloat16 [16, 592, 1024], P('fsdp', 'ctx')
- gain_grads: float32 [2, 1024], P(None, 'fsdp')
- shift_grads: float32 [2, 1024], P(None, 'fsdp')
- qkv_grad: float32 [1024, 3072], P('fsdp')
- qv_bias_grad: float32 [2, 1024], P(None, 'fsdp')
- out_weight_grad: float32 [1024, 1024], P('fsdp')
- out_bias_grad: float32 [1024], P('fsdp')
- fc1_grad: float32 [1024, 4096], P('fsdp')
- fc1_bias_grad: float32 [4096], P('fsdp')
- fc2_grad: float32 [4096, 1024], P('fsdp')
- fc2_bias_grad: float32 [1024], P('fsdp')
Inputs may be any that keep to these rules, and one draw needn't show every extreme that they name: key_mask is 1 at position 0 of every image and 0 at positions 577 and beyond.
All inputs are finite; a program needn't handle non-finite values. No bound on the sum of `slot_valid` on one device may be relied on, other than what follows from the above.
Results may differ from a plain program's by a relative error of at most 0.017.
Values may be sent and summed in bfloat16 or wider, within the bound.
No kernel may reach another device: no remote copies, remote signals or barrier semaphores. Data moves between devices by JAX's collectives and lax.ppermute only.
A program may use at most 192 MiB of HBM per device.

v0:
```python
import jax
import jax.numpy as jnp
from jax import lax
from jax.sharding import PartitionSpec as P

D = 1024
HEADS = 16
HEAD_DIM = 64
LIVE = 577


def across_rows(left_side, right_side):
    return lax.dot_general(
        left_side, right_side, (((0,), (0,)), ((), ())), preferred_element_type=jnp.float32
    )


def against(left_side, right_side):
    return lax.dot_general(
        left_side, right_side, (((1,), (1,)), ((), ())), preferred_element_type=jnp.float32
    )


def apply_layer_norm(values, gain_row, shift_row):
    centred = values - jnp.mean(values, axis=-1, keepdims=True)
    inverse_std = lax.rsqrt(jnp.mean(centred * centred, axis=-1, keepdims=True) + 1e-05)
    normed = centred * inverse_std
    return (normed * gain_row + shift_row, normed, inverse_std)


def norm_reverse_pass(grad_normed, normed, inverse_std):
    first_mean = jnp.mean(grad_normed, axis=-1, keepdims=True)
    second_mean = jnp.mean(grad_normed * normed, axis=-1, keepdims=True)
    return inverse_std * (grad_normed - first_mean - normed * second_mean)


def head_slice(source, head_index, offset):
    return lax.dynamic_slice_in_dim(source, offset + head_index * HEAD_DIM, HEAD_DIM, 2)


def body(
    tokens,
    out_grad,
    key_mask,
    slot_valid,
    norm_gains,
    norm_shifts,
    qkv_weight,
    qv_bias,
    out_weight,
    out_bias,
    fc1_weight,
    fc1_bias,
    fc2_weight,
    fc2_bias,
):
    full_params = (
        lax.all_gather(norm_gains, "fsdp", axis=1, tiled=True),
        lax.all_gather(norm_shifts, "fsdp", axis=1, tiled=True),
        lax.all_gather(qkv_weight, "fsdp", axis=0, tiled=True),
        lax.all_gather(qv_bias, "fsdp", axis=1, tiled=True),
        lax.all_gather(out_weight, "fsdp", axis=0, tiled=True),
        lax.all_gather(out_bias, "fsdp", axis=0, tiled=True),
        lax.all_gather(fc1_weight, "fsdp", axis=0, tiled=True),
        lax.all_gather(fc1_bias, "fsdp", axis=0, tiled=True),
        lax.all_gather(fc2_weight, "fsdp", axis=0, tiled=True),
        lax.all_gather(fc2_bias, "fsdp", axis=0, tiled=True),
    )
    norm_gain_vector = full_params[0].astype(jnp.float32)
    norm_bias_vector = full_params[1].astype(jnp.float32)
    qkv_matrix = full_params[2]
    qv_shift = full_params[3].astype(jnp.float32)
    out_matrix = full_params[4]
    out_shift = full_params[5].astype(jnp.float32)
    fc1_matrix = full_params[6]
    fc1_shift = full_params[7].astype(jnp.float32)
    fc2_matrix = full_params[8]
    fc2_shift = full_params[9].astype(jnp.float32)
    image_count = tokens.shape[0]
    local_len = tokens.shape[1]
    row_count = image_count * local_len
    flattened_rows = tokens.reshape(row_count, D).astype(jnp.float32)
    normalized_input, first_centred_scaled, first_inverse_deviation = apply_layer_norm(
        flattened_rows, norm_gain_vector[0], norm_bias_vector[0]
    )
    normed_low = normalized_input.astype(jnp.bfloat16)
    raw_proj = jnp.dot(normed_low, qkv_matrix, preferred_element_type=jnp.float32)
    queries = (
        (raw_proj[:, :D] + qv_shift[0]).astype(jnp.bfloat16).reshape(image_count, local_len, D)
    )
    key_value = jnp.concatenate(
        [raw_proj[:, D : 2 * D], raw_proj[:, 2 * D :] + qv_shift[1]], axis=1
    )
    key_value = key_value.astype(jnp.bfloat16).reshape(image_count, local_len, 2 * D)
    key_all, mask_all = (
        lax.all_gather(key_value, "ctx", axis=1, tiled=True),
        lax.all_gather(key_mask.astype(jnp.bfloat16), "ctx", axis=1, tiled=True),
    )
    visible = (mask_all > 0)[:, None, :]

    def head_forward(head_index):
        head_queries = head_slice(queries, head_index, 0)
        head_keys = head_slice(key_all, head_index, 0)
        head_value_rows = head_slice(key_all, head_index, D)
        scores = (
            jnp.einsum("jgz,jaz->jga", head_queries, head_keys, preferred_element_type=jnp.float32)
            * 0.125
        )
        scores = jnp.where(visible, scores, -1e30)
        row_max = jnp.max(scores, axis=-1, keepdims=True)
        exponent = jnp.exp(scores - row_max)
        row_sum = jnp.sum(exponent, axis=-1, keepdims=True)
        attention_weights = (exponent / row_sum).astype(jnp.bfloat16)
        context = jnp.einsum(
            "ans,ash->anh", attention_weights, head_value_rows, preferred_element_type=jnp.float32
        )
        return (context.astype(jnp.bfloat16), (row_max + jnp.log(row_sum))[:, :, 0])

    contexts, log_norm = lax.map(head_forward, jnp.arange(HEADS))
    context_low = contexts.transpose(1, 2, 0, 3).reshape(row_count, D)
    residual_state = (
        flattened_rows
        + jnp.dot(context_low, out_matrix, preferred_element_type=jnp.float32)
        + out_shift
    )
    normalized_residual, second_centred_scaled, second_inverse_deviation = apply_layer_norm(
        residual_state, norm_gain_vector[1], norm_bias_vector[1]
    )
    middle_low = normalized_residual.astype(jnp.bfloat16)
    pre_act = jnp.dot(middle_low, fc1_matrix, preferred_element_type=jnp.float32) + fc1_shift
    sigmoid_gate = jax.nn.sigmoid(1.702 * pre_act)
    hidden = (pre_act * sigmoid_gate).astype(jnp.bfloat16)
    output = (
        residual_state + jnp.dot(hidden, fc2_matrix, preferred_element_type=jnp.float32) + fc2_shift
    )
    result = output.astype(jnp.bfloat16).reshape(image_count, local_len, D)
    position = lax.axis_index("ctx") * local_len + jnp.arange(local_len)
    keep_row = (position < LIVE)[None, :] & (slot_valid[:, None] > 0)
    grad_out = jnp.where(keep_row[:, :, None], out_grad, jnp.zeros_like(out_grad)).reshape(
        row_count, D
    )
    held = lax.optimization_barrier(
        ((norm_gains, qkv_weight, out_weight, fc1_weight, fc2_weight), grad_out)
    )
    held_gain, held_qkv, held_out, held_fc1, held_fc2 = held[0]
    again_params = (
        lax.all_gather(held_gain, "fsdp", axis=1, tiled=True),
        lax.all_gather(held_qkv, "fsdp", axis=0, tiled=True),
        lax.all_gather(held_out, "fsdp", axis=0, tiled=True),
        lax.all_gather(held_fc1, "fsdp", axis=0, tiled=True),
        lax.all_gather(held_fc2, "fsdp", axis=0, tiled=True),
    )
    reverse_gain_pass = again_params[0].astype(jnp.float32)
    back_qkv = again_params[1]
    back_out = again_params[2]
    back_fc1 = again_params[3]
    back_fc2 = again_params[4]
    grad_fc2 = across_rows(hidden, grad_out)
    grad_fc2_shift = jnp.sum(grad_out.astype(jnp.float32), axis=0)
    grad_hidden = against(grad_out, back_fc2)
    grad_pre = grad_hidden * (sigmoid_gate + 1.702 * pre_act * sigmoid_gate * (1.0 - sigmoid_gate))
    grad_fc1_shift = jnp.sum(grad_pre, axis=0)
    grad_pre_low = grad_pre.astype(jnp.bfloat16)
    grad_fc1 = across_rows(middle_low, grad_pre_low)
    middle_norm_gradient = against(grad_pre_low, back_fc1)
    second_gain_gradient = jnp.sum(middle_norm_gradient * second_centred_scaled, axis=0)
    grad_shift_two = jnp.sum(middle_norm_gradient, axis=0)
    residual_gradient = grad_out.astype(jnp.float32) + norm_reverse_pass(
        middle_norm_gradient * reverse_gain_pass[1], second_centred_scaled, second_inverse_deviation
    )
    grad_out_shift = jnp.sum(residual_gradient, axis=0)
    grad_middle_low = residual_gradient.astype(jnp.bfloat16)
    grad_out_matrix = across_rows(context_low, grad_middle_low)
    grad_context = (
        against(grad_middle_low, back_out).astype(jnp.bfloat16).reshape(image_count, local_len, D)
    )

    def head_backward(head_inputs):
        head_index, head_norm = head_inputs
        head_queries = head_slice(queries, head_index, 0)
        head_keys = head_slice(key_all, head_index, 0)
        head_value_rows = head_slice(key_all, head_index, D)
        head_gradient = head_slice(grad_context, head_index, 0)
        scores = (
            jnp.einsum("jgz,jaz->jga", head_queries, head_keys, preferred_element_type=jnp.float32)
            * 0.125
        )
        attention_weights = jnp.where(visible, jnp.exp(scores - head_norm[:, :, None]), 0.0)
        grad_probs = jnp.einsum(
            "jgz,jaz->jga", head_gradient, head_value_rows, preferred_element_type=jnp.float32
        )
        row_delta = jnp.sum(attention_weights * grad_probs, axis=-1, keepdims=True)
        score_gradient = (attention_weights * (grad_probs - row_delta)).astype(jnp.bfloat16)
        grad_query = (
            jnp.einsum(
                "ans,ash->anh", score_gradient, head_keys, preferred_element_type=jnp.float32
            )
            * 0.125
        )
        grad_key = (
            jnp.einsum(
                "isl,isc->ilc", score_gradient, head_queries, preferred_element_type=jnp.float32
            )
            * 0.125
        )
        grad_value = jnp.einsum(
            "isl,isc->ilc",
            attention_weights.astype(jnp.bfloat16),
            head_gradient,
            preferred_element_type=jnp.float32,
        )
        return (grad_query, grad_key, grad_value)

    grad_queries, grad_keys, grad_values = lax.map(head_backward, (jnp.arange(HEADS), log_norm))
    grad_keys_all = grad_keys.transpose(1, 2, 0, 3).reshape(image_count, -1, D)
    grad_values_all = grad_values.transpose(1, 2, 0, 3).reshape(image_count, -1, D)
    own_keys, own_values = (
        lax.psum_scatter(
            grad_keys_all.astype(jnp.bfloat16), "ctx", scatter_dimension=1, tiled=True
        ).astype(jnp.float32),
        lax.psum_scatter(
            grad_values_all.astype(jnp.bfloat16), "ctx", scatter_dimension=1, tiled=True
        ).astype(jnp.float32),
    )
    grad_query_rows = grad_queries.transpose(1, 2, 0, 3).reshape(row_count, D)
    own_value_rows = own_values.reshape(row_count, D)
    grad_qv_shift = jnp.stack([jnp.sum(grad_query_rows, axis=0), jnp.sum(own_value_rows, axis=0)])
    grad_raw = jnp.concatenate(
        [grad_query_rows, own_keys.reshape(row_count, D), own_value_rows], axis=1
    ).astype(jnp.bfloat16)
    grad_qkv = across_rows(normed_low, grad_raw)
    input_norm_gradient = against(grad_raw, back_qkv)
    first_gain_gradient = jnp.sum(input_norm_gradient * first_centred_scaled, axis=0)
    grad_shift_one = jnp.sum(input_norm_gradient, axis=0)
    token_gradient = residual_gradient + norm_reverse_pass(
        input_norm_gradient * reverse_gain_pass[0], first_centred_scaled, first_inverse_deviation
    )
    token_gradient = token_gradient.astype(jnp.bfloat16).reshape(image_count, local_len, D)
    grad_gains = jnp.stack([first_gain_gradient, second_gain_gradient])
    grad_shifts = jnp.stack([grad_shift_one, grad_shift_two])
    (
        gain_part,
        shift_part,
        qkv_part,
        qv_part,
        out_part,
        out_shift_part,
        fc1_part,
        fc1_shift_part,
        fc2_part,
        fc2_shift_part,
    ) = (
        lax.psum_scatter(grad_gains, "fsdp", scatter_dimension=1, tiled=True),
        lax.psum_scatter(grad_shifts, "fsdp", scatter_dimension=1, tiled=True),
        lax.psum_scatter(grad_qkv, "fsdp", scatter_dimension=0, tiled=True),
        lax.psum_scatter(grad_qv_shift, "fsdp", scatter_dimension=1, tiled=True),
        lax.psum_scatter(grad_out_matrix, "fsdp", scatter_dimension=0, tiled=True),
        lax.psum_scatter(grad_out_shift, "fsdp", scatter_dimension=0, tiled=True),
        lax.psum_scatter(grad_fc1, "fsdp", scatter_dimension=0, tiled=True),
        lax.psum_scatter(grad_fc1_shift, "fsdp", scatter_dimension=0, tiled=True),
        lax.psum_scatter(grad_fc2, "fsdp", scatter_dimension=0, tiled=True),
        lax.psum_scatter(grad_fc2_shift, "fsdp", scatter_dimension=0, tiled=True),
    )
    finished = (
        lax.psum(gain_part.astype(jnp.bfloat16), "ctx").astype(jnp.float32),
        lax.psum(shift_part.astype(jnp.bfloat16), "ctx").astype(jnp.float32),
        lax.psum(qkv_part.astype(jnp.bfloat16), "ctx").astype(jnp.float32),
        lax.psum(qv_part.astype(jnp.bfloat16), "ctx").astype(jnp.float32),
        lax.psum(out_part.astype(jnp.bfloat16), "ctx").astype(jnp.float32),
        lax.psum(out_shift_part.astype(jnp.bfloat16), "ctx").astype(jnp.float32),
        lax.psum(fc1_part.astype(jnp.bfloat16), "ctx").astype(jnp.float32),
        lax.psum(fc1_shift_part.astype(jnp.bfloat16), "ctx").astype(jnp.float32),
        lax.psum(fc2_part.astype(jnp.bfloat16), "ctx").astype(jnp.float32),
        lax.psum(fc2_shift_part.astype(jnp.bfloat16), "ctx").astype(jnp.float32),
    )
    return (
        result,
        token_gradient,
        finished[0],
        finished[1],
        finished[2],
        finished[3],
        finished[4],
        finished[5],
        finished[6],
        finished[7],
        finished[8],
        finished[9],
    )


def solution(mesh):
    in_specs = (
        P("fsdp", "ctx", None),
        P("fsdp", "ctx", None),
        P("fsdp", "ctx"),
        P("fsdp"),
        P(None, "fsdp"),
        P(None, "fsdp"),
        P("fsdp", None),
        P(None, "fsdp"),
        P("fsdp", None),
        P("fsdp"),
        P("fsdp", None),
        P("fsdp"),
        P("fsdp", None),
        P("fsdp"),
    )
    out_specs = (
        P("fsdp", "ctx", None),
        P("fsdp", "ctx", None),
        P(None, "fsdp"),
        P(None, "fsdp"),
        P("fsdp", None),
        P(None, "fsdp"),
        P("fsdp", None),
        P("fsdp"),
        P("fsdp", None),
        P("fsdp"),
        P("fsdp", None),
        P("fsdp"),
    )
    return jax.shard_map(body, mesh=mesh, in_specs=in_specs, out_specs=out_specs, check_vma=False)
```

profile of v0, /device:TPU:0, one launch (start us, length us, event | category | flops | bytes accessed | tf_op | source)
XLA Modules:
  0.0 2302.0 jit_solution(17001615898816371938)
XLA Ops:
  8.0 2.3 copy.94
  13.6 22.3 all_gather.53
  36.0 16.5 all_gather.52
  52.4 18.4 all_gather.55
  70.8 41.2 %all-gather.14.cloned.1.call-done = bf16[1024,3072]{1,0:T(8,128)(2,1)} async-done(((bf16[128,3072]{1,0:T(8,128)(2,1)}), bf16[1024,3072]{1,0:T(8,128)(2,1)}) %all-gather.14.cloned.1.call-update) | async-done | bytes 6291472 | tf_op jit(solution)/shard_map/all_gather | solution.py:60
  112.0 5.0 fusion.46
  120.5 2.3 copy.99
  127.8 17.6 all-gather.1
  145.4 5.1 all-gather
  150.7 26.1 %all-gather.2 = bf16[8,1,512]{2,1,0:T(2,128)(2,1)S(1)} all-gather(bf16[1,1,512]{2,1,0:T(2,128)(2,1)S(1)} %reshape.215), channel_id=1, replica_groups=mesh['fsdp'=8,'ctx'=4] {'fsdp'}, dimensions={0}, use_global_device_ids=true | all-gather | bytes 9216 | tf_op jit(solution)/shard_map/all_gather | solution.py:65
  176.8 16.4 all_gather.65
  193.9 11.7 copy.101
  205.7 88.4 %while.30 = (s32[]{:T(128)}, bf16[16,2,148,64]{2,3,1,0:T(8,128)(2,1)}, f32[16,2,148]{2,1,0:T(2,128)}, pred[2,1,592]{2,0,1:T(4,128)(4,1)S(1)}, s32[16]{0:T(128)S(...) while((s32[]{:T(128)}, ...), condition=%wide.region_5.6_spmd, body=%wide.region_2.5_spmd.sunk | while | flops 46279904 | bytes 2574702 | solution.py:119
  214.1 2.0 fusion.93
  219.7 2.0 fusion.93
  230.7 2.0 fusion.93
  236.2 2.0 fusion.93
  241.7 2.0 fusion.93
  252.8 2.0 fusion.93
  263.9 2.0 fusion.93
  269.4 2.0 fusion.93
  286.0 2.0 fusion.93
  294.1 2.2 copy.102
  298.0 2.7 fusion.54
  301.0 35.4 %all-gather.20.cloned.1.call-done = bf16[1024,4096]{1,0:T(8,128)(2,1)} async-done(((bf16[128,4096]{1,0:T(8,128)(2,1)}), bf16[1024,4096]{1,0:T(8,128)(2,1)}) %all-gather.20.cloned.1.call-update) | async-done | bytes 8388624 | tf_op jit(solution)/shard_map/all_gather | solution.py:64
  336.3 8.5 convolution_add_fusion
  344.8 116.7 %all-gather.24.cloned.1.call-done = bf16[4096,1024]{1,0:T(8,128)(2,1)} async-done(((bf16[512,1024]{1,0:T(8,128)(2,1)}), bf16[4096,1024]{1,0:T(8,128)(2,1)}) %all-gather.24.cloned.1.call-update) | async-done | bytes 8388624 | tf_op jit(solution)/shard_map/all_gather | solution.py:151
  461.5 10.3 fusion.55
  471.7 114.9 %all-gather.26.cloned.1.call-done = bf16[1024,4096]{1,0:T(8,128)(2,1)} async-done(((bf16[128,4096]{1,0:T(8,128)(2,1)}), bf16[1024,4096]{1,0:T(8,128)(2,1)}) %all-gather.26.cloned.1.call-update) | async-done | bytes 8388624 | tf_op jit(solution)/shard_map/all_gather | solution.py:150
  586.6 6.6 multiply_reduce_fusion.1
  594.7 41.5 %all-gather.28.cloned.1.call-done = bf16[1024,1024]{1,0:T(8,128)(2,1)} async-done(((bf16[128,1024]{1,0:T(8,128)(2,1)}), bf16[1024,1024]{1,0:T(8,128)(2,1)}) %all-gather.28.cloned.1.call-update) | async-done | bytes 2097168 | tf_op jit(solution)/shard_map/all_gather | solution.py:149
  636.2 3.6 convolution_convert_fusion.1
  639.8 2.0 reshape.205
  641.9 2.2 copy.106
  644.1 165.1 %while.31 = (s32[]{:T(128)}, f32[16,2,148,64]{2,3,1,0:T(8,128)}, bf16[16,2,592,64]{2,3,1,0:T(8,128)(2,1)}, bf16[16,2,592,64]{2,3,1,0:T(8,128)(2,1)}, pred[2,1,59...) while((s32[]{:T(128)}, f32[16,2,148,64]{2,3,1,0:T(8,128)}, ...), condition=%wide.region_12.13_spmd, body=%wide.region_10.12_spmd.sunk | while | flops 113820000 | bytes 11654198 | solution.py:214
  809.2 3.5 copy.108
  812.7 6.6 copy.109
  819.3 3.5 copy.111
  822.9 6.6 copy.112
  830.5 4.6 fusion.42
  840.7 2.1 reshape.206
  843.6 80.8 %all-reduce.14.cloned.1.call-done = (bf16[2,592,1024]{2,0,1:T(2,128)(2,1)}, bf16[2,592,1024]{2,0,1:T(2,128)(2,1)}) async-done(((bf16[2,592,1024]{2,0,1:T(2,128)(2,1)}, bf16[2,592,1024]{2,0,1:T(2,128)(2,1)}), (bf16[2,592,1024]{2,0,1:T(2,128)(2,1)}, bf16[2,592,1024]{2,0,1:T(2,128)(2,1)})) %all-reduce.14.cloned.1.call-update) | async-done | bytes 4849680
  933.9 8.3 fusion.45
  942.3 10.3 fusion.38
  953.7 10.7 fusion.47
  967.0 58.9 %all-gather.30.cloned.1.call-done = bf16[1024,3072]{1,0:T(8,128)(2,1)} async-done(((bf16[128,3072]{1,0:T(8,128)(2,1)}), bf16[1024,3072]{1,0:T(8,128)(2,1)}) %all-gather.30.cloned.1.call-update) | async-done | bytes 6291472 | tf_op jit(solution)/shard_map/all_gather | solution.py:148
  1025.8 6.7 multiply_reduce_fusion.2
  1035.9 18.2 all-gather.3
  1056.0 59.5 %reduce-scatter.16.cloned.1.call-done = f32[128,1024]{1,0:T(8,128)} async-done(((f32[1024,1024]{1,0:T(8,128)}), f32[128,1024]{1,0:T(8,128)}) %reduce-scatter.16.cloned.1.call-update) | async-done | bytes 524304 | tf_op jit(solution)/shard_map/reduce_scatter | solution.py:257
  1117.3 209.3 %reduce-scatter.14.cloned.1.call-done = f32[128,3072]{1,0:T(8,128)} async-done(((f32[1024,3072]{1,0:T(8,128)}), f32[128,3072]{1,0:T(8,128)}) %reduce-scatter.14.cloned.1.call-update) | async-done | bytes 1572880 | tf_op jit(solution)/shard_map/reduce_scatter | solution.py:255
  1326.5 2.4 convert_element_type.208
  1328.9 283.5 %reduce-scatter.18.cloned.1.call-done = f32[128,4096]{1,0:T(8,128)} async-done(((f32[1024,4096]{1,0:T(8,128)}), f32[128,4096]{1,0:T(8,128)}) %reduce-scatter.18.cloned.1.call-update) | async-done | bytes 2097168 | tf_op jit(solution)/shard_map/reduce_scatter | solution.py:259
  1612.4 2.7 convert_element_type.217
  1615.1 282.9 %reduce-scatter.20.cloned.1.call-done = f32[512,1024]{1,0:T(8,128)} async-done(((f32[4096,1024]{1,0:T(8,128)}), f32[512,1024]{1,0:T(8,128)}) %reduce-scatter.20.cloned.1.call-update) | async-done | bytes 2097168 | tf_op jit(solution)/shard_map/reduce_scatter | solution.py:261
  1898.0 2.8 convert_element_type.221
  1900.8 123.4 %all-gather.22.cloned.1.call-done = bf16[4096,1024]{1,0:T(8,128)(2,1)} async-done(((bf16[512,1024]{1,0:T(8,128)(2,1)}), bf16[4096,1024]{1,0:T(8,128)(2,1)}) %all-gather.22.cloned.1.call-update) | async-done | bytes 8388624 | tf_op jit(solution)/shard_map/all_gather | solution.py:66
  2024.2 8.5 fusion.35
  2035.5 34.2 %all-reduce.5 = (bf16[1024]{0:T(1024)(128)(2,1)S(1)}, bf16[4096]{0:T(1024)(128)(2,1)S(1)}, bf16[1024]{0:T(1024)(128)(2,1)S(1)}) all-reduce(f32[1024]{0:T(1024)S(1)} %get-tuple-element.448, f32[4096]{0:T(1024)S(1)} %get-tuple-element.470, f32[1024]{0:T(1024)S(1)} %get-tuple-element.446), channel_id=9, replica_groups=mesh['fsdp'=8,'ctx'=4] {'fsdp'}, use_global_device_ids=true, to_apply=%region_34.35.clone | all-reduce | flops 6144 | bytes 36864
  2073.2 15.2 reduce-scatter.22.cloned.1.call-done
  2089.3 63.3 %reduce-scatter.24.cloned.1.call-done = f32[128,2]{1,0:T(8,128)} async-done(((f32[1024,2]{1,0:T(8,128)}), f32[128,2]{1,0:T(8,128)}) %reduce-scatter.24.cloned.1.call-update) | async-done | bytes 1040
  2153.5 63.5 %reduce-scatter.26.cloned.1.call-done = f32[128,2]{1,0:T(8,128)} async-done(((f32[1024,2]{1,0:T(8,128)}), f32[128,2]{1,0:T(8,128)}) %reduce-scatter.26.cloned.1.call-update) | async-done | bytes 1040
  2218.0 5.7 all-reduce.6
  2226.9 61.3 %all-reduce.12.cloned.1.call-done = (bf16[128,3072]{1,0:T(8,128)(2,1)}, bf16[128,1024]{1,0:T(8,128)(2,1)}, bf16[128,4096]{1,0:T(8,128)(2,1)}, bf16[512,1024]{1,0:T(8,128)(2,1)}) async-done(((bf16[128,3072]{1,0:T(8,128)(2,1)}, bf16[128,1024]{1,0:T(8,128)(2,1)}, bf16[128,4096]{1,0:T(8,128)(2,1)}, bf16[512,1024]{1,0:T(8,128)(2,1)}), (bf16[128,3072]{1,0:T(8,128)(2,1)}, bf16[128,1024]{1,0:T(8,128)(2,1)}, ...) | async-done | bytes 3145744 | tf_op jit(solution)/shard_map/psum | solution.py:267
  2288.2 2.5 convert_element_type.209
  (432 shorter events, 272.1 us)
Async XLA Ops:
  7.2 104.9 %all-gather.14.cloned.1.call-start = ((), (), s32[]{:S(2)}) async-start(), calls=%async_computation.7 | async-start | bytes 7077888 | tf_op jit(solution)/shard_map/all_gather | solution.py:60
  7.9 3.9 copy-start.1
  7.9 186.0 %all-gather.16.cloned.1.call-start = ((), (), s32[]{:S(2)}) async-start(), calls=%async_computation.8 | async-start | bytes 6062080 | tf_op jit(solution)/shard_map/all_gather | solution.py:96
  10.3 3.3 copy-start.15
  10.3 25.7 %copy-start.12 = (bf16[2,128]{1,0:T(2,128)(2,1)S(1)}, bf16[2,128]{1,0:T(2,128)(2,1)}, u32[]{:S(2)}) copy-start(bf16[2,128]{1,0:T(2,128)(2,1)} %param.22) | copy-start | bytes 1540
  10.3 42.1 %copy-start.16 = (bf16[2,128]{1,0:T(2,128)(2,1)S(1)}, bf16[2,128]{1,0:T(2,128)(2,1)}, u32[]{:S(2)}) copy-start(bf16[2,128]{1,0:T(2,128)(2,1)} %param.25) | copy-start | bytes 1540
  122.8 1.4 copy-start.19
  122.8 1.5 copy-start.10
  122.8 175.1 %all-gather.18.cloned.1.call-start = ((), (), s32[]{:S(2)}) async-start(), calls=%async_computation.9 | async-start | bytes 2359296 | tf_op jit(solution)/shard_map/all_gather | solution.py:62
  123.6 212.8 %all-gather.20.cloned.1.call-start = ((), (), s32[]{:S(2)}) async-start(), calls=%async_computation.10 | async-start | bytes 9437184 | tf_op jit(solution)/shard_map/all_gather | solution.py:64
  124.1 337.3 %all-gather.24.cloned.1.call-start = ((), (), s32[]{:S(2)}) async-start(), calls=%async_computation.12 | async-start | bytes 9437184 | tf_op jit(solution)/shard_map/all_gather | solution.py:151
  125.4 2.4 copy-start.17
  125.4 20.1 copy-start.13
  125.4 25.3 %copy-start.14 = (bf16[512]{0:T(512)(128)(2,1)S(1)}, bf16[512]{0:T(512)(128)(2,1)}, u32[]{:S(2)}) copy-start(bf16[512]{0:T(512)(128)(2,1)} %param.29) | copy-start | bytes 3076
  125.4 67.8 %copy-start.5 = (bf16[296,1024]{1,0:T(8,128)(2,1)S(1)}, bf16[296,1024]{1,0:T(8,128)(2,1)}, u32[]{:S(2)}) copy-start(bf16[296,1024]{1,0:T(8,128)(2,1)} %get-tuple-element.457) | copy-start | bytes 1818628
  126.4 460.2 %all-gather.26.cloned.1.call-start = ((), (), s32[]{:S(2)}) async-start(), calls=%async_computation.13 | async-start | bytes 9437184 | tf_op jit(solution)/shard_map/all_gather | solution.py:150
  127.0 509.3 %all-gather.28.cloned.1.call-start = ((), (), s32[]{:S(2)}) async-start(), calls=%async_computation.14 | async-start | bytes 2359296 | tf_op jit(solution)/shard_map/all_gather | solution.py:149
  127.7 796.7 %all-reduce.14.cloned.1.call-start = ((), (), s32[]{:S(2)}) async-start(), calls=%async_computation.24 | async-start | bytes 9699328
  586.6 6.6 copy-start.6
  649.0 5.4 copy-start.3
  654.4 1.3 copy-start.2
  659.3 5.4 copy-start.3
  664.7 1.3 copy-start.2
  669.6 5.4 copy-start.3
  679.9 5.4 copy-start.3
  685.4 1.3 copy-start.2
  690.3 5.4 copy-start.3
  695.7 1.3 copy-start.2
  700.6 5.4 copy-start.3
  706.0 1.3 copy-start.2
  710.9 5.4 copy-start.3
  716.3 1.3 copy-start.2
  721.2 5.4 copy-start.3
  726.6 1.3 copy-start.2
  731.6 5.4 copy-start.3
  736.9 1.3 copy-start.2
  741.9 5.4 copy-start.3
  747.2 1.3 copy-start.2
  752.2 5.4 copy-start.3
  762.5 5.4 copy-start.3
  767.9 1.3 copy-start.2
  772.8 5.4 copy-start.3
  778.2 1.3 copy-start.2
  783.1 5.4 copy-start.3
  788.5 1.3 copy-start.2
  793.5 5.4 copy-start.3
  798.9 1.3 copy-start.2
  803.8 5.4 copy-start.3
  829.4 196.4 %all-gather.30.cloned.1.call-start = ((), (), s32[]{:S(2)}) async-start(), calls=%async_computation.15 | async-start | bytes 7077888 | tf_op jit(solution)/shard_map/all_gather | solution.py:148
  830.2 285.3 %reduce-scatter.16.cloned.1.call-start = ((), (), s32[]{:S(2)}) async-start(), calls=%async_computation.17 | async-start | bytes 4718592 | tf_op jit(solution)/shard_map/reduce_scatter | solution.py:257
  835.1 491.5 %reduce-scatter.14.cloned.1.call-start = ((), (), s32[]{:S(2)}) async-start(), calls=%async_computation.16 | async-start | bytes 14155776 | tf_op jit(solution)/shard_map/reduce_scatter | solution.py:255
  942.2 670.2 %reduce-scatter.18.cloned.1.call-start = ((), (), s32[]{:S(2)}) async-start(), calls=%async_computation.18 | async-start | bytes 18874368 | tf_op jit(solution)/shard_map/reduce_scatter | solution.py:259
  952.6 945.4 %reduce-scatter.20.cloned.1.call-start = ((), (), s32[]{:S(2)}) async-start(), calls=%async_computation.19 | async-start | bytes 18874368 | tf_op jit(solution)/shard_map/reduce_scatter | solution.py:261
  964.5 1059.8 %all-gather.22.cloned.1.call-start = ((), (), s32[]{:S(2)}) async-start(), calls=%async_computation.11 | async-start | bytes 9437184 | tf_op jit(solution)/shard_map/all_gather | solution.py:66
  965.0 1123.4 %reduce-scatter.22.cloned.1.call-start = ((), (), s32[]{:S(2)}) async-start(), calls=%async_computation.20 | async-start | bytes 589824
  1032.5 3.4 copy-start.18
  1032.5 21.6 copy-start.20
  1033.6 1119.1 %reduce-scatter.24.cloned.1.call-start = ((), (), s32[]{:S(2)}) async-start(), calls=%async_computation.21 | async-start | bytes 589824
  1034.7 1182.4 %reduce-scatter.26.cloned.1.call-start = ((), (), s32[]{:S(2)}) async-start(), calls=%async_computation.22 | async-start | bytes 589824
  1035.8 1252.4 %all-reduce.12.cloned.1.call-start = ((), (), s32[]{:S(2)}) async-start(), calls=%async_computation.23 | async-start | bytes 6291456 | tf_op jit(solution)/shard_map/psum | solution.py:267
  2032.7 37.2 %copy-start = (f32[296,1024]{1,0:T(8,128)S(1)}, f32[296,1024]{1,0:T(8,128)}, u32[]{:S(2)}) copy-start(f32[296,1024]{1,0:T(8,128)} %get-tuple-element.449) | copy-start | bytes 3637252
  2288.2 2.5 copy-start.11
  2288.2 3.4 copy-start.9
  2290.7 2.4 copy-start.8
  (6 other events, 6.8 us)
Sparse Core Ops, SparseCore 0:
  10.2 101.8 all-gather.13
  122.9 36.4 all-gather.15
  161.5 49.2 all-gather.17
  212.8 123.4 all-gather.19
  338.3 123.1 all-gather.23
  463.5 123.1 all-gather.25
  588.7 47.4 all-gather.27
  829.6 94.8 all-reduce.13
  926.6 99.1 all-gather.29
  1029.3 86.1 reduce-scatter.15
  1119.5 207.0 reduce-scatter.13
  1330.6 281.7 reduce-scatter.17
  1616.2 281.7 reduce-scatter.19
  1900.2 123.9 all-gather.21
  2028.3 60.0 reduce-scatter.21
  2091.6 60.9 reduce-scatter.23
  2156.2 60.8 reduce-scatter.25
  2220.1 68.0 all-reduce.11
where the time goes:
time: 2310 us; the launch traced here: 2300 us
  waiting for transfers between devices  1660 us (72%)
  matrix products  270 us (12%)
  blocking collectives  180 us (8%)
  local copies, waits for them, and re-layouts  108 us (5%)
  other arithmetic  49 us (2%)
    reduce_scatter x1, waiting for transfers between devices, body(): lax.psum_scatter(grad_fc1, 'fsdp', scatter_dimension=0, tiled=True)  284 us
    reduce_scatter x1, waiting for transfers between devices, body(): lax.psum_scatter(grad_fc2, 'fsdp', scatter_dimension=0, tiled=True)  283 us
    unnamed x22, waiting for transfers between devices  227 us
    reduce_scatter x1, waiting for transfers between devices, body(): lax.psum_scatter(grad_qkv, 'fsdp', scatter_dimension=0, tiled=True)  209 us
    all_gather x1, waiting for transfers between devices, body(): lax.all_gather(fc2_weight, 'fsdp', axis=0, tiled=True)  123 us
    all_gather x1, waiting for transfers between devices, body(): lax.all_gather(held_fc2, 'fsdp', axis=0, tiled=True)  117 us
    all_gather x1, waiting for transfers between devices, body(): lax.all_gather(held_fc1, 'fsdp', axis=0, tiled=True)  115 us
    psum x1, waiting for transfers between devices, body(): lax.psum(qkv_part.astype(jnp.bfloat16), 'ctx').astype(jnp.float32)  61.3 us
  transfers between devices with their start and end apart: 18, of which 16 were waited for; matrix products, arithmetic and copies ran while one was open for 10% of the time, Pallas kernels for 0%

commit v1 on v0

v1 whole, which is shorter than its diff:
```python
import functools

import jax
import jax.numpy as jnp
from jax import lax
from jax.experimental import pallas as pl
from jax.experimental.pallas import tpu as pltpu
from jax.sharding import PartitionSpec as P

D = 1024
HEADS = 16
HEAD_DIM = 64
LIVE = 577
PAD = 160
MASK_ROW = 148
NEG = -1e30
F32 = jnp.float32
BF16 = jnp.bfloat16


def dot(a, b):
    return lax.dot_general(a, b, (((1,), (0,)), ((), ())), preferred_element_type=F32)


def dot_nt(a, b):
    return lax.dot_general(a, b, (((1,), (1,)), ((), ())), preferred_element_type=F32)


def dot_tn(a, b):
    return lax.dot_general(a, b, (((0,), (0,)), ((), ())), preferred_element_type=F32)


def layer_norm(values):
    centred = values - jnp.mean(values, axis=-1, keepdims=True)
    inverse = lax.rsqrt(jnp.mean(centred * centred, axis=-1, keepdims=True) + 1e-05)
    return centred * inverse, inverse


def norm_reverse(grad, normed, inverse):
    first = jnp.mean(grad, axis=-1, keepdims=True)
    second = jnp.mean(grad * normed, axis=-1, keepdims=True)
    return inverse * (grad - first - normed * second)


def attn_fwd_kernel(q_ref, k_ref, v_ref, bias_ref, o_ref):
    rows = q_ref.shape[0]
    lane = lax.broadcasted_iota(jnp.int32, (1, 128), 1)
    k = k_ref[...]
    v = v_ref[...]
    bias = bias_ref[...]
    for start in range(0, rows, 128):
        q = q_ref[start : start + 128, :] * 0.125
        outs = []
        for h in range(2):
            qh = jnp.where((lane // 64) == h, q, jnp.zeros_like(q))
            s = dot_nt(qh, k) + bias
            top = jnp.max(s, axis=-1, keepdims=True)
            e = jnp.exp(s - top)
            total = jnp.sum(e, axis=-1, keepdims=True)
            p = (e * (1.0 / total)).astype(BF16)
            outs.append(dot(p, v))
        o_ref[start : start + 128, :] = jnp.where(lane < 64, outs[0], outs[1]).astype(BF16)


def attn_bwd_kernel(q_ref, k_ref, v_ref, g_ref, bias_ref, dq_ref, dk_ref, dv_ref, sum_ref, dk_acc, dv_acc):
    rows = q_ref.shape[0]
    lane = lax.broadcasted_iota(jnp.int32, (1, 128), 1)
    k = k_ref[...]
    v = v_ref[...]
    bias = bias_ref[:, 0:1]
    qsum = jnp.zeros((1, 128), F32)
    for start in range(0, rows, 128):
        q = q_ref[start : start + 128, :] * 0.125
        g = g_ref[start : start + 128, :]
        dqs, dks, dvs = [], [], []
        for h in range(2):
            mine = (lane // 64) == h
            qh = jnp.where(mine, q, jnp.zeros_like(q))
            gh = jnp.where(mine, g, jnp.zeros_like(g))
            s = dot_nt(k, qh) + bias
            top = jnp.max(s, axis=0, keepdims=True)
            e = jnp.exp(s - top)
            total = jnp.sum(e, axis=0, keepdims=True)
            p = e * (1.0 / total)
            dp = dot_nt(v, gh)
            delta = jnp.sum(p * dp, axis=0, keepdims=True)
            ds = (p * (dp - delta)).astype(BF16)
            dvs.append(dot(p.astype(BF16), gh))
            dks.append(dot(ds, qh))
            dqs.append(dot_tn(ds, k))
        dq = jnp.where(lane < 64, dqs[0], dqs[1]) * 0.125
        qsum = qsum + jnp.sum(dq, axis=0, keepdims=True)
        dq_ref[start : start + 128, :] = dq.astype(BF16)
        dk = dks[0] + dks[1]
        dv = dvs[0] + dvs[1]
        if start == 0:
            dk_acc[...] = dk
            dv_acc[...] = dv
        else:
            dk_acc[...] += dk
            dv_acc[...] += dv
    dk_ref[...] = dk_acc[...].astype(BF16)
    dv = dv_acc[...]
    dv_ref[...] = dv.astype(BF16)
    vsum = jnp.sum(dv, axis=0, keepdims=True)
    sum_ref[...] = jnp.concatenate([qsum, vsum, jnp.zeros((6, 128), F32)], axis=0)


def attention(qkv, bias_row):
    rows, width = qkv.shape[0], qkv.shape[1] // 3
    pairs = width // 128
    spec = lambda off: pl.BlockSpec((rows, 128), lambda i: (0, off * pairs + i))
    return pl.pallas_call(
        attn_fwd_kernel,
        grid=(pairs,),
        in_specs=[spec(0), spec(1), spec(2), pl.BlockSpec((1, rows), lambda i: (0, 0))],
        out_specs=pl.BlockSpec((rows, 128), lambda i: (0, i)),
        out_shape=jax.ShapeDtypeStruct((rows, width), BF16),
        compiler_params=pltpu.CompilerParams(vmem_limit_bytes=40 << 20),
        cost_estimate=pl.CostEstimate(
            flops=4 * rows * rows * width * 4,
            bytes_accessed=4 * rows * width * 2,
            transcendentals=rows * rows * pairs * 2,
        ),
        name="attn_fwd",
    )(qkv, qkv, qkv, bias_row)


def attention_back(qkv, grad, bias_col):
    rows, width = grad.shape
    pairs = width // 128
    spec = lambda off: pl.BlockSpec((rows, 128), lambda i: (0, off * pairs + i))
    out = pl.BlockSpec((rows, 128), lambda i: (0, i))
    return pl.pallas_call(
        attn_bwd_kernel,
        grid=(pairs,),
        in_specs=[
            spec(0),
            spec(1),
            spec(2),
            pl.BlockSpec((rows, 128), lambda i: (0, i)),
            pl.BlockSpec((rows, 128), lambda i: (0, 0)),
        ],
        out_specs=[out, out, out, pl.BlockSpec((8, 128), lambda i: (0, i))],
        out_shape=[jax.ShapeDtypeStruct((rows, width), BF16)] * 3
        + [jax.ShapeDtypeStruct((8, width), F32)],
        scratch_shapes=[pltpu.VMEM((rows, 128), F32)] * 2,
        compiler_params=pltpu.CompilerParams(vmem_limit_bytes=48 << 20),
        cost_estimate=pl.CostEstimate(
            flops=10 * rows * rows * width * 4,
            bytes_accessed=8 * rows * width * 2,
            transcendentals=rows * rows * pairs * 2,
        ),
        name="attn_bwd",
    )(qkv, qkv, qkv, grad, bias_col)


def body(
    nf,
    nc,
    tokens,
    out_grad,
    key_mask,
    slot_valid,
    norm_gains,
    norm_shifts,
    qkv_weight,
    qv_bias,
    out_weight,
    out_bias,
    fc1_weight,
    fc1_bias,
    fc2_weight,
    fc2_bias,
):
    f = lax.axis_index("fsdp")
    c = lax.axis_index("ctx")
    axes = ("fsdp", "ctx")
    bits = []
    while (1 << len(bits)) < nf:
        bits.append(1 << len(bits))

    def swap(v, df, dc):
        pairs = [(i * nc + j, (i ^ df) * nc + (j ^ dc)) for i in range(nf) for j in range(nc)]
        return lax.ppermute(v, axes, pairs)

    def core(v):
        return swap(v, 0, 1)

    def across(v):
        return swap(v, 0, 2)

    def gather(shard, axis=0):
        buf = shard[None]
        for b in reversed(bits):
            other = swap(buf, b, 0)
            up = (f // b) % 2 == 1
            low, high = jnp.where(up, other, buf), jnp.where(up, buf, other)
            buf = jnp.stack([low, high], axis=1).reshape((2 * buf.shape[0],) + shard.shape)
        if axis == 0:
            return buf.reshape((-1,) + shard.shape[1:])
        return buf.transpose(1, 0, 2).reshape(shard.shape[0], -1)

    def scatter(full, low):
        for b in bits:
            v = full.reshape((full.shape[0] // 2, 2) + full.shape[1:])
            up = (f // b) % 2
            send = lax.dynamic_index_in_dim(v, 1 - up, 1, keepdims=False).astype(low)
            keep = lax.dynamic_index_in_dim(v, up, 1, keepdims=False)
            full = keep + swap(send, b, 0).astype(F32)
        return full[0]

    def ctx_all(v):
        other = across(v)
        up = c // 2 == 1
        v = jnp.stack([jnp.where(up, other, v), jnp.where(up, v, other)])
        other = core(v)
        up = c % 2 == 1
        v = jnp.stack([jnp.where(up, other, v), jnp.where(up, v, other)], axis=1)
        return v.reshape((4,) + v.shape[2:])

    n_img, length = tokens.shape[0], tokens.shape[1]
    quarter = D // nc
    wide = 4 * D // nf // nc

    def spread(v):
        v = jnp.concatenate([v, across(v)], axis=0)
        return jnp.concatenate([v, core(v)], axis=0)

    def all_rows(part):
        half = 2 * PAD
        mine = part[:half] + core(part[half:].astype(BF16)).astype(F32)
        got = across(mine.astype(BF16)).astype(F32)
        mine = mine + jnp.concatenate([got[PAD:], got[:PAD]], axis=0)
        rest = core(mine.astype(BF16)).astype(F32)
        return jnp.concatenate([mine, rest], axis=0)

    def own_rows(part):
        half = 2 * PAD
        mine = part[:half] + core(part[half:].astype(BF16)).astype(F32)
        return mine[:PAD] + across(mine[PAD:].astype(BF16)).astype(F32)

    x_all = []
    for i in range(n_img):
        mask_row = jnp.pad(key_mask[i : i + 1].astype(BF16), ((0, 0), (0, D - length)))
        x = jnp.concatenate(
            [tokens[i], mask_row, jnp.zeros((PAD - length - 1, D), BF16)], axis=0
        )
        x_all.append(spread(x))

    small = jnp.concatenate(
        [
            norm_gains,
            norm_shifts,
            qv_bias,
            out_bias[None],
            fc2_bias[None],
            fc1_bias.reshape(4, D // nf),
        ],
        axis=0,
    )
    small = gather(small, axis=1).astype(F32)
    gain1, gain2, shift1, shift2 = small[0:1], small[1:2], small[2:3], small[3:4]
    out_shift, fc2_shift = small[6:7], small[7:8]
    fc1_shift = lax.dynamic_slice_in_dim(small, 8 + c, 1, 0)
    q_shift = lax.dynamic_slice(small, (4, c * quarter), (1, quarter))
    v_shift = lax.dynamic_slice(small, (5, c * quarter), (1, quarter))
    qkv_shift = jnp.concatenate([q_shift, jnp.zeros_like(q_shift), v_shift], axis=1)

    rows_w = D // nf
    part_qkv = lax.dynamic_index_in_dim(
        qkv_weight.reshape(rows_w, 3, nc, quarter), c, 2, keepdims=False
    ).reshape(rows_w, 3 * quarter)
    w_qkv = gather(part_qkv)
    piece = rows_w // 4
    out_pairs = []
    for fs in range(nf):
        for j in range(nc):
            dst_c = fs // (nf // 4)
            dst_f = (fs % (nf // 4)) * 4 + j
            out_pairs.append((fs * nc + j, dst_f * nc + dst_c))
    out_back = [(b, a) for a, b in out_pairs]
    part_out = lax.ppermute(
        lax.dynamic_slice_in_dim(out_weight, c * piece, piece, 0), axes, out_pairs
    )
    w_out = gather(part_out)
    part_fc1 = lax.dynamic_index_in_dim(
        fc1_weight.reshape(rows_w, nf, 4, wide), c, 2, keepdims=False
    ).reshape(rows_w, D)
    w_fc1 = gather(part_fc1)
    part_fc2 = lax.dynamic_slice_in_dim(fc2_weight, c * wide, wide, 0)
    w_fc2 = gather(part_fc2)

    position = c * length + jnp.arange(length)
    g_all = []
    for i in range(n_img):
        keep = ((position < LIVE) & (slot_valid[i] > 0))[:, None]
        g = jnp.where(keep, out_grad[i], jnp.zeros((), BF16))
        g_all.append(spread(jnp.pad(g, ((0, PAD - length), (0, 0)))))

    saved = []
    for i in range(n_img):
        x = x_all[i].astype(F32)
        xhat1, inv1 = layer_norm(x)
        normed = (xhat1 * gain1 + shift1).astype(BF16)
        qkv = (dot(normed, w_qkv) + qkv_shift).astype(BF16)
        mask = x_all[i].reshape(4, PAD, D)[:, MASK_ROW, :PAD].reshape(1, 4 * PAD)
        bias = (1.0 - mask.astype(F32)) * NEG
        context = attention(qkv, bias)
        middle = x + all_rows(dot(context, w_out)) + out_shift
        xhat2, inv2 = layer_norm(middle)
        normed_mid = (xhat2 * gain2 + shift2).astype(BF16)
        pre = dot(normed_mid, w_fc1) + fc1_shift
        sig = jax.nn.sigmoid(1.702 * pre)
        hidden = (pre * sig).astype(BF16)
        res = own_rows(dot(hidden, w_fc2))
        result = (middle[:PAD] + res + fc2_shift).astype(BF16)[:length]
        saved.append((xhat1, inv1, normed, qkv, bias, context, middle, xhat2, inv2, normed_mid, pre, sig, hidden, result))

    grads = []
    for i in range(n_img):
        (xhat1, inv1, normed, qkv, bias, context, middle, xhat2, inv2, normed_mid, pre, sig, hidden, result) = saved[i]
        g = g_all[i]
        d_hidden = dot_nt(g, w_fc2)
        d_pre = d_hidden * (sig + 1.702 * pre * sig * (1.0 - sig))
        fc1_sum = jnp.sum(d_pre, axis=0, keepdims=True)
        d_pre_low = d_pre.astype(BF16)
        d_norm = all_rows(dot_nt(d_pre_low, w_fc1))
        d_mid = g.astype(F32) + norm_reverse(d_norm * gain2, xhat2, inv2)
        d_mid_low = d_mid.astype(BF16)
        d_context = dot_nt(d_mid_low, w_out).astype(BF16)
        bias_col = jnp.broadcast_to(bias.reshape(-1, 1), (4 * PAD, 128))
        dq, dk, dv, qv_sum = attention_back(qkv, d_context, bias_col)
        d_raw = jnp.concatenate([dq, dk, dv], axis=1)
        d_normed = own_rows(dot_nt(d_raw, w_qkv))
        d_tok = d_mid[:PAD] + norm_reverse(d_normed * gain1, xhat1[:PAD], inv1[:PAD])
        d_tok = d_tok.astype(BF16)[:length]
        own_norm = d_norm[:PAD]
        vectors = [
            jnp.sum(d_normed * xhat1[:PAD], axis=0, keepdims=True),
            jnp.sum(own_norm * xhat2[:PAD], axis=0, keepdims=True),
            jnp.sum(d_normed, axis=0, keepdims=True),
            jnp.sum(own_norm, axis=0, keepdims=True),
            jnp.sum(d_mid[:PAD], axis=0, keepdims=True),
            jnp.sum(g[:PAD].astype(F32), axis=0, keepdims=True),
        ]
        grads.append((d_pre_low, d_mid_low, d_raw, d_tok, vectors, fc1_sum, qv_sum))

    def over_images(lefts, rights):
        total = dot_tn(lefts[0], rights[0])
        for a, b in zip(lefts[1:], rights[1:]):
            total = total + dot_tn(a, b)
        return total

    p_fc2 = over_images([s[12] for s in saved], g_all)
    p_fc1 = over_images([s[9] for s in saved], [r[0] for r in grads])
    p_out = over_images([s[5] for s in saved], [r[1] for r in grads])
    p_qkv = over_images([s[2] for s in saved], [r[2] for r in grads])

    fc2_g = scatter(p_fc2.reshape(nf, -1, D), BF16)
    fc1_g = scatter(p_fc1.reshape(nf, -1, D), BF16)
    out_g = scatter(p_out.reshape(nf, -1, D), BF16)
    qkv_g = scatter(p_qkv.reshape(nf, -1, 3 * quarter), BF16)
    out_g = lax.ppermute(out_g.astype(BF16), axes, out_back)
    fc2_full = ctx_all(fc2_g.astype(BF16)).reshape(-1, D).astype(F32)
    fc1_full = (
        ctx_all(fc1_g.astype(BF16))
        .reshape(nc, rows_w, nf, wide)
        .transpose(1, 2, 0, 3)
        .reshape(rows_w, 4 * D)
        .astype(F32)
    )
    out_full = ctx_all(out_g).reshape(rows_w, D).astype(F32)
    qkv_full = (
        ctx_all(qkv_g.astype(BF16))
        .reshape(nc, rows_w, 3, quarter)
        .transpose(1, 2, 0, 3)
        .reshape(rows_w, 3 * D)
        .astype(F32)
    )

    vec = [sum(r[4][k] for r in grads) for k in range(6)]
    fc1_sum = sum(r[5] for r in grads)
    qv_sum = sum(r[6] for r in grads)
    here = (jnp.arange(D) // quarter == c)[None]
    qv_rows = jnp.where(here, jnp.tile(qv_sum[0:2], (1, nc)), 0.0)
    fc1_rows = jnp.where((jnp.arange(4) == c)[:, None], fc1_sum, 0.0)
    packed = jnp.concatenate(vec[0:4] + [qv_rows] + vec[4:6] + [fc1_rows], axis=0)
    packed = packed.reshape(12, nf, D // nf).transpose(1, 0, 2)
    packed = scatter(packed, F32)
    packed = packed + across(packed)
    packed = packed + core(packed)

    return (
        jnp.stack([s[13] for s in saved]),
        jnp.stack([r[3] for r in grads]),
        packed[0:2],
        packed[2:4],
        qkv_full,
        packed[4:6],
        out_full,
        packed[6],
        fc1_full,
        packed[8:12].reshape(-1),
        fc2_full,
        packed[7],
    )


def solution(mesh):
    in_specs = (
        P("fsdp", "ctx", None),
        P("fsdp", "ctx", None),
        P("fsdp", "ctx"),
        P("fsdp"),
        P(None, "fsdp"),
        P(None, "fsdp"),
        P("fsdp", None),
        P(None, "fsdp"),
        P("fsdp", None),
        P("fsdp"),
        P("fsdp", None),
        P("fsdp"),
        P("fsdp", None),
        P("fsdp"),
    )
    out_specs = (
        P("fsdp", "ctx", None),
        P("fsdp", "ctx", None),
        P(None, "fsdp"),
        P(None, "fsdp"),
        P("fsdp", None),
        P(None, "fsdp"),
        P("fsdp", None),
        P("fsdp"),
        P("fsdp", None),
        P("fsdp"),
        P("fsdp", None),
        P("fsdp"),
    )
    step = functools.partial(body, mesh.shape["fsdp"], mesh.shape["ctx"])
    return jax.shard_map(step, mesh=mesh, in_specs=in_specs, out_specs=out_specs, check_vma=False)
```

time: 2310 us -> 455 us (0.20)
  waiting for transfers between devices: 1660 us -> 141 us
  matrix products: 270 us -> 49.3 us
  blocking collectives: 180 us -> 0 us
  starting transfers between devices: 0.72 us -> 81.3 us
  local copies, waits for them, and re-layouts: 108 us -> 63.4 us
  Pallas kernels: 0 us -> 42.7 us
    reduce_scatter x4 -> x0, waiting for transfers between devices: 835 us -> none  [the longest x1 284 us: body(): lax.psum_scatter(grad_fc1, 'fsdp', scatter_dimension=0, tiled=True)]
    all_gather x9 -> x0, waiting for transfers between devices: 532 us -> none  [the longest x1 123 us: body(): lax.all_gather(fc2_weight, 'fsdp', axis=0, tiled=True)]
    unnamed x22 -> x0, waiting for transfers between devices: 227 us -> none
    dot_general x124 -> x24, matrix products: 270 us -> 49.3 us  [the longest x8 22.6 us: dot_tn(): lax.dot_general(a, b, (((0,), (0,)), ((), ())), preferred_element_type=F32)]
    ppermute x0 -> x70, waiting for transfers between devices: none -> 141 us  [the longest x68 141 us: swap(): return lax.ppermute(v, axes, pairs)]
    all_gather x8 -> x0, blocking collectives: 141 us -> none  [the longest x1 26.1 us: body(): lax.all_gather(fc1_bias, 'fsdp', axis=0, tiled=True)]
    ppermute x0 -> x70, starting transfers between devices: none -> 81.3 us  [the longest x68 80 us: swap(): return lax.ppermute(v, axes, pairs)]
    psum x1 -> x0, waiting for transfers between devices: 61.3 us -> none  [body(): lax.psum(qkv_part.astype(jnp.bfloat16), 'ctx').astype(jnp.float32)]
  transfers between devices with their start and end apart: 18 -> 70, of which waited for: 16 -> 27; matrix products, arithmetic and copies ran while one was open for 10% -> 37% of each run, Pallas kernels for 0% -> 10%
where the time goes in v1:
time: 455 us; the launch traced here: 449 us
  waiting for transfers between devices  141 us (31%)
  starting transfers between devices  81.3 us (18%)
  other arithmetic  65.3 us (14%)
  local copies, waits for them, and re-layouts  63.4 us (14%)
  matrix products  49.3 us (11%)
  Pallas kernels  42.7 us (9%)
  between operations  5.16 us (1%)
    ppermute x68, waiting for transfers between devices, swap(): return lax.ppermute(v, axes, pairs)  141 us
    ppermute x68, starting transfers between devices, swap(): return lax.ppermute(v, axes, pairs)  80 us
    pallas_call x2, Pallas kernels, attention_back(): pl.pallas_call(attn_bwd_kernel, grid=(pairs,), in_specs=[spec(0), spec(1)...  25.6 us
    dot_general x8, matrix products, dot_tn(): lax.dot_general(a, b, (((0,), (0,)), ((), ())), preferred_element_type=F32)  22.6 us
    pallas_call x2, Pallas kernels, attention(): pl.pallas_call(attn_fwd_kernel, grid=(pairs,), in_specs=[spec(0), spec(1)...  17.1 us
    unnamed x211, local copies, waits for them, and re-layouts  16.9 us
    dot_general x8, matrix products, dot_nt(): lax.dot_general(a, b, (((1,), (1,)), ((), ())), preferred_element_type=F32)  15.2 us
    dot_general x8, matrix products, dot(): lax.dot_general(a, b, (((1,), (0,)), ((), ())), preferred_element_type=F32)  11.4 us
  transfers between devices with their start and end apart: 70, of which 27 were waited for; matrix products, arithmetic and copies ran while one was open for 37% of the time, Pallas kernels for 10%

profile of v1, /device:TPU:0, one launch (start us, length us, event | category | flops | bytes accessed | tf_op | source)
XLA Modules:
  0.0 448.5 jit_solution(9675332339367896126)
XLA Ops:
  2.8 4.0 collective-permute-start.18
  8.7 2.9 collective-permute-start.2
  21.1 14.3 %collective-permute-done.2 = bf16[1,12,128]{2,1,0:T(8,128)(2,1)S(1)} collective-permute-done((bf16[1,12,128]{2,1,0:T(8,128)(2,1)S(1)}, bf16[1,12,128]{2,1,0:T(8,128)(2,1)S(1)}, u32[]{:S(2)}, u32[]{:S(2)}) %collective-permute-start.2) | collective-permute-done | bytes 3104 | tf_op jit(solution)/shard_map/ppermute | solution.py:185
  36.2 2.9 collective-permute-done.3
  39.2 1.9 collective-permute-start.4
  45.0 7.7 %collective-permute-start.9 = (bf16[1,32,1024]{2,1,0:T(8,128)(2,1)S(1)}, bf16[1,32,1024]{2,1,0:T(8,128)(2,1)S(1)}, u32[]{:S(2)}, u32[]{:S(2)}) collective-permute-start(bf16[1,32,1024]{2,1,0:T(8,128)(2,1)S(1)} %bitcast.415), channel_id=1, source_target_pairs={{0,16},{1,17},{2,18},{3,19},{4,20},{5,21},{6,22},{7,23},{8,24},{9,... | collective-permute-start | bytes 196616 | tf_op jit(solution)/shard_map/ppermute | solution.py:185
  53.3 2.1 collective-permute-done.9
  55.4 3.0 collective-permute-start
  59.6 2.1 collective-permute-start.37
  62.8 1.9 collective-permute-start.10
  65.7 3.2 collective-permute-done.10
  68.9 2.1 collective-permute-start.6
  72.8 2.5 collective-permute-start.11
  75.3 2.2 fusion.17
  82.5 9.9 %collective-permute-done.19 = bf16[2,128,1024]{1,2,0:T(8,128)(2,1)} collective-permute-done((bf16[2,128,1024]{1,2,0:T(8,128)(2,1)}, bf16[2,128,1024]{1,2,0:T(8,128)(2,1)}, u32[]{:S(2)}, u32[]{:S(2)}) %collective-permute-start.19) | collective-permute-done | bytes 524320 | tf_op jit(solution)/shard_map/ppermute | solution.py:185
  96.6 5.0 %concatenate.85 = bf16[640,1024]{1,0:T(8,128)(2,1)S(1)} concatenate(bf16[148,1024]{1,0:T(8,128)(2,1)S(1)} %bitcast.378, bf16[1,1024]{1,0:T(2,128)(2,1)S(1)} %pad.15, bf16[11,1024]{1,0:T(8,128)(2,1)S(1)} %copy-done.53, bf16[160,1024]{1,0:T(8,128)(2,1)} %collective-permute-done.23, bf16[320,1024]{1,0:T(8,128)(2,1)} %collective-permute-done.24), dimensions={0} | concatenate | bytes 2621440 | tf_op jit(solution)/shard_map/concatenate | solution.py:228
  102.6 5.0 %concatenate.78 = bf16[640,1024]{1,0:T(8,128)(2,1)S(1)} concatenate(bf16[148,1024]{1,0:T(8,128)(2,1)S(1)} %bitcast.375, bf16[1,1024]{1,0:T(2,128)(2,1)S(1)} %pad.14, bf16[11,1024]{1,0:T(8,128)(2,1)S(1)} %copy-done.54, bf16[160,1024]{1,0:T(8,128)(2,1)} %copy-done.44, bf16[320,1024]{1,0:T(8,128)(2,1)} %collective-permute-done.1), dimensions={0} | concatenate | bytes 2621440 | tf_op jit(solution)/shard_map/concatenate | solution.py:228
  109.0 6.8 %collective-permute-done.7 = bf16[4,128,768]{2,1,0:T(8,128)(2,1)} collective-permute-done((bf16[4,128,768]{2,1,0:T(8,128)(2,1)}, bf16[4,128,768]{2,1,0:T(8,128)(2,1)}, u32[]{:S(2)}, u32[]{:S(2)}) %collective-permute-start.7) | collective-permute-done | bytes 786464 | tf_op jit(solution)/shard_map/ppermute | solution.py:185
  120.2 8.6 %attn_fwd.3 = bf16[640,256]{1,0:T(8,128)(2,1)S(1)} custom-call(bf16[640,768]{1,0:T(8,128)(2,1)S(1)} %add_convert_fusion.4.q_ref.k_ref.v_ref, bf16[640,768]{1,0:T(8,128)(2,1)S(1)} %add_convert_fusion.4.q_ref.k_ref.v_ref, bf16[640,768]{1,0:T(8,128)(2,1)S(1)} %add_convert_fusion.4.q_ref.k_ref.v_ref, f32[1,640]{1,0:T(1,128)S(1)} %mul.269.bias_ref), custom_call_target="tpu_custom_call" | custom-call | flops 1677721600 | bytes 1310720 | tf_op jit(solution)/shard_map/attn_fwd/pallas_call | solution.py:113
  131.4 8.6 %attn_fwd.2 = bf16[640,256]{1,0:T(8,128)(2,1)S(1)} custom-call(bf16[640,768]{1,0:T(8,128)(2,1)S(1)} %add_convert_fusion.5.q_ref.k_ref.v_ref, bf16[640,768]{1,0:T(8,128)(2,1)S(1)} %add_convert_fusion.5.q_ref.k_ref.v_ref, bf16[640,768]{1,0:T(8,128)(2,1)S(1)} %add_convert_fusion.5.q_ref.k_ref.v_ref, f32[1,640]{1,0:T(1,128)S(1)} %mul.253.bias_ref), custom_call_target="tpu_custom_call" | custom-call | flops 1677721600 | bytes 1310720 | tf_op jit(solution)/shard_map/attn_fwd/pallas_call | solution.py:113
  140.0 2.0 fusion.97
  142.0 2.3 slice.538
  148.7 2.3 copy.111
  157.1 7.3 %collective-permute-done.26 = bf16[320,1024]{1,0:T(8,128)(2,1)} collective-permute-done((bf16[320,1024]{1,0:T(8,128)(2,1)}, bf16[320,1024]{1,0:T(8,128)(2,1)}, u32[]{:S(2)}, u32[]{:S(2)}) %collective-permute-start.26) | collective-permute-done | bytes 655392 | tf_op jit(solution)/shard_map/ppermute | solution.py:185
  166.1 11.9 %collective-permute-done.13 = bf16[320,1024]{1,0:T(8,128)(2,1)S(1)} collective-permute-done((bf16[320,1024]{1,0:T(8,128)(2,1)S(1)}, bf16[320,1024]{1,0:T(8,128)(2,1)S(1)}, u32[]{:S(2)}, u32[]{:S(2)}) %collective-permute-start.13) | collective-permute-done | bytes 655392 | tf_op jit(solution)/shard_map/ppermute | solution.py:185
  178.1 1.9 fusion.82
  183.8 3.7 fusion.83
  198.2 3.4 fusion.96
  203.2 1.8 fusion.24
  205.0 3.6 fusion.95
  212.6 1.8 convolution_add_fusion.1
  216.2 5.0 %fusion.71 = f32[1024,1024]{1,0:T(8,128)} fusion(bf16[320,1024]{1,0:T(8,128)(2,1)} %collective-permute-done.38, bf16[160,1024]{1,0:T(8,128)(2,1)S(1)} %copy-done.48, bf16[160,1024]{1,0:T(8,128)(2,1)S(1)} %copy-done.24, f32[640,1024]{1,0:T(8,128)S(1)} %copy-done.97, f32[1024]{0:T(1024)S(1)} %bitcast.432), kind=kOutput, calls=%fused_computation.327 | convolution fusion | flops 1350696960 | bytes 8130560 | tf_op jit(solution)/shard_map/dot_general | solution.py:30
  221.2 4.3 convolution_add_fusion
  233.5 5.8 %collective-permute-done.22 = bf16[160,1024]{1,0:T(8,128)(2,1)S(1)} collective-permute-done((bf16[160,1024]{1,0:T(8,128)(2,1)S(1)}, bf16[160,1024]{1,0:T(8,128)(2,1)S(1)}, u32[]{:S(2)}, u32[]{:S(2)}) %collective-permute-start.22) | collective-permute-done | bytes 327712 | tf_op jit(solution)/shard_map/ppermute | solution.py:185
  240.1 6.2 %collective-permute-done.29 = bf16[160,1024]{1,0:T(8,128)(2,1)S(1)} collective-permute-done((bf16[160,1024]{1,0:T(8,128)(2,1)S(1)}, bf16[160,1024]{1,0:T(8,128)(2,1)S(1)}, u32[]{:S(2)}, u32[]{:S(2)}) %collective-permute-start.29) | collective-permute-done | bytes 327712 | tf_op jit(solution)/shard_map/ppermute | solution.py:185
  251.1 11.3 %collective-permute-done.65 = bf16[4,128,1024]{2,1,0:T(8,128)(2,1)S(1)} collective-permute-done((bf16[4,128,1024]{2,1,0:T(8,128)(2,1)S(1)}, bf16[4,128,1024]{2,1,0:T(8,128)(2,1)S(1)}, u32[]{:S(2)}, u32[]{:S(2)}) %collective-permute-start.65) | collective-permute-done | bytes 1048608 | tf_op jit(solution)/shard_map/ppermute | solution.py:185
  265.3 8.1 %collective-permute-done.40 = bf16[320,1024]{1,0:T(8,128)(2,1)S(1)} collective-permute-done((bf16[320,1024]{1,0:T(8,128)(2,1)S(1)}, bf16[320,1024]{1,0:T(8,128)(2,1)S(1)}, u32[]{:S(2)}, u32[]{:S(2)}) %collective-permute-start.40) | collective-permute-done | bytes 655392 | tf_op jit(solution)/shard_map/ppermute | solution.py:185
  274.9 1.9 collective-permute-start.62
  277.1 2.1 collective-permute-start.67
  279.8 16.3 %collective-permute-done.62 = bf16[1,128,1024]{2,1,0:T(8,128)(2,1)S(1)} collective-permute-done((bf16[1,128,1024]{2,1,0:T(8,128)(2,1)S(1)}, bf16[1,128,1024]{2,1,0:T(8,128)(2,1)S(1)}, u32[]{:S(2)}, u32[]{:S(2)}) %collective-permute-start.62) | collective-permute-done | bytes 262176 | tf_op jit(solution)/shard_map/ppermute | solution.py:185
  297.4 4.0 collective-permute-done.67
  303.0 1.9 fusion.9
  304.9 4.1 multiply_add_fusion.1
  309.8 12.9 %attn_bwd.3 = (bf16[640,256]{1,0:T(8,128)(2,1)S(1)}, bf16[640,256]{1,0:T(8,128)(2,1)S(1)}, bf16[640,256]{1,0:T(8,128)(2,1)S(1)}, f32[8,256]{1,0:T(8,128)S(1)}) custom-call(bf16[640,768]{1,0:T(8,128)(2,1)S(1)} %add_convert_fusion.4.q_ref.k_ref.v_ref, bf16[640,768]{1,0:T(8,128)(2,1)S(1)} %add_convert_fusion.4.q_ref.k_ref.v_ref, ...), custom_call_target="tpu_custom_call" | custom-call | flops 4194304000 | bytes 2621440 | tf_op jit(solution)/shard_map/attn_bwd/pallas_call | solution.py:134
  322.9 2.8 fusion.100
  325.7 3.4 fusion.47
  331.4 12.7 %attn_bwd.2 = (bf16[640,256]{1,0:T(8,128)(2,1)S(1)}, bf16[640,256]{1,0:T(8,128)(2,1)S(1)}, bf16[640,256]{1,0:T(8,128)(2,1)S(1)}, f32[8,256]{1,0:T(8,128)S(1)}) custom-call(bf16[640,768]{1,0:T(8,128)(2,1)S(1)} %add_convert_fusion.5.q_ref.k_ref.v_ref, bf16[640,768]{1,0:T(8,128)(2,1)S(1)} %add_convert_fusion.5.q_ref.k_ref.v_ref, ...), custom_call_target="tpu_custom_call" | custom-call | flops 4194304000 | bytes 2621440 | tf_op jit(solution)/shard_map/attn_bwd/pallas_call | solution.py:134
  345.6 3.3 slice.531
  349.0 4.1 convolution_add_fusion.2
  356.2 2.2 slice_reduce_fusion.2
  358.4 5.4 %collective-permute-done.54 = bf16[4,32,1024]{2,1,0:T(8,128)(2,1)S(1)} collective-permute-done((bf16[4,32,1024]{2,1,0:T(8,128)(2,1)S(1)}, bf16[4,32,1024]{2,1,0:T(8,128)(2,1)S(1)}, u32[]{:S(2)}, u32[]{:S(2)}) %collective-permute-start.54) | collective-permute-done | bytes 262176 | tf_op jit(solution)/shard_map/ppermute | solution.py:185
  366.2 3.9 collective-permute-done.55
  371.6 4.2 collective-permute-done.56
  377.6 6.9 %collective-permute-start.58 = (bf16[32,1024]{1,0:T(8,128)(2,1)S(1)}, bf16[32,1024]{1,0:T(8,128)(2,1)S(1)}, u32[]{:S(2)}, u32[]{:S(2)}) collective-permute-start(bf16[32,1024]{1,0:T(8,128)(2,1)S(1)} %collective-permute-done.57), channel_id=1, source_target_pairs={{0,2},{1,3},{2,0},{3,1},{4,6},{5,7},{6,4},{7,5},{8,10},{9,11},{10,... | collective-permute-start | bytes 196616 | tf_op jit(solution)/shard_map/ppermute | solution.py:185
  384.6 2.2 collective-permute-done.58
  390.9 2.3 collective-permute-start.36
  408.9 2.3 multiply_reduce_fusion.5
  411.5 3.0 collective-permute-start.44
  416.4 2.1 collective-permute-start.45
  420.2 3.9 collective-permute-start.46
  427.0 2.8 collective-permute-start.51
  431.3 4.4 collective-permute-done.51
  437.4 4.2 collective-permute-done.52
  445.3 3.0 copy.133
  (546 shorter events, 141.8 us)
Async XLA Ops:
  2.8 56.8 %collective-permute-start.18 = (bf16[1,128,1024]{1,2,0:T(8,128)(2,1)}, bf16[1,128,1024]{1,2,0:T(8,128)(2,1)}, u32[]{:S(2)}, u32[]{:S(2)}) collective-permute-start(bf16[1,128,1024]{1,2,0:T(8,128)(2,1)} %bitcast.56), channel_id=1, source_target_pairs={{0,16},{1,17},{2,18},{3,19},{4,20},{5,21},{6,22},{7,23},{8,24},{9,... | collective-permute-start | bytes 786440 | tf_op jit(solution)/shard_map/ppermute | solution.py:185
  8.5 54.3 %collective-permute-start.15 = (bf16[1,128,1024]{1,2,0:T(8,128)(2,1)S(1)}, bf16[1,128,1024]{1,2,0:T(8,128)(2,1)}, u32[]{:S(2)}, u32[]{:S(2)}) collective-permute-start(bf16[1,128,1024]{1,2,0:T(8,128)(2,1)S(1)} %bitcast.405), channel_id=1, source_target_pairs={{0,16},{1,17},{2,18},{3,19},{4,20},{5,21},{6,22},{7,23},{8,24},{9,... | collective-permute-start | bytes 786440 | tf_op jit(solution)/shard_map/ppermute | solution.py:185
  8.7 26.7 %collective-permute-start.2 = (bf16[1,12,128]{2,1,0:T(8,128)(2,1)S(1)}, bf16[1,12,128]{2,1,0:T(8,128)(2,1)S(1)}, u32[]{:S(2)}, u32[]{:S(2)}) collective-permute-start(bf16[1,12,128]{2,1,0:T(8,128)(2,1)S(1)} %bitcast.421), channel_id=1, source_target_pairs={{0,16},{1,17},{2,18},{3,19},{4,20},{5,21},{6,22},{7,23},{8,24},{9,... | collective-permute-start | bytes 9224 | tf_op jit(solution)/shard_map/ppermute | solution.py:185
  12.7 45.7 %collective-permute-start.5 = (bf16[1,128,768]{1,2,0:T(8,128)(2,1)}, bf16[1,128,768]{1,2,0:T(8,128)(2,1)}, u32[]{:S(2)}, u32[]{:S(2)}) collective-permute-start(bf16[1,128,768]{1,2,0:T(8,128)(2,1)} %bitcast.19), channel_id=1, source_target_pairs={{0,16},{1,17},{2,18},{3,19},{4,20},{5,21},{6,22},{7,23},{8,24},{9,... | collective-permute-start | bytes 589832 | tf_op jit(solution)/shard_map/ppermute | solution.py:185
  14.8 57.9 %collective-permute-start.23 = (bf16[160,1024]{1,0:T(8,128)(2,1)}, bf16[160,1024]{1,0:T(8,128)(2,1)}, u32[]{:S(2)}, u32[]{:S(2)}) collective-permute-start(bf16[160,1024]{1,0:T(8,128)(2,1)} %get-tuple-element.181), channel_id=1, source_target_pairs={{0,2},{1,3},{2,0},{3,1},{4,6},{5,7},{6,4},{7,5},{8,10},{9,11},{10,... | collective-permute-start | bytes 983048 | tf_op jit(solution)/shard_map/ppermute | solution.py:185
  39.2 3.8 collective-permute-start.4
  45.0 10.4 %collective-permute-start.9 = (bf16[1,32,1024]{2,1,0:T(8,128)(2,1)S(1)}, bf16[1,32,1024]{2,1,0:T(8,128)(2,1)S(1)}, u32[]{:S(2)}, u32[]{:S(2)}) collective-permute-start(bf16[1,32,1024]{2,1,0:T(8,128)(2,1)S(1)} %bitcast.415), channel_id=1, source_target_pairs={{0,16},{1,17},{2,18},{3,19},{4,20},{5,21},{6,22},{7,23},{8,24},{9,... | collective-permute-start | bytes 196616 | tf_op jit(solution)/shard_map/ppermute | solution.py:185
  55.4 17.4 %collective-permute-start = (bf16[160,1024]{1,0:T(8,128)(2,1)}, bf16[160,1024]{1,0:T(8,128)(2,1)S(1)}, u32[]{:S(2)}, u32[]{:S(2)}) collective-permute-start(bf16[160,1024]{1,0:T(8,128)(2,1)} %get-tuple-element.180), channel_id=1, source_target_pairs={{0,2},{1,3},{2,0},{3,1},{4,6},{5,7},{6,4},{7,5},{8,10},{9,11},{10,... | collective-permute-start | bytes 983048 | tf_op jit(solution)/shard_map/ppermute | solution.py:185
  58.4 19.1 %collective-permute-start.30 = (bf16[160,1024]{1,0:T(8,128)(2,1)S(1)}, bf16[160,1024]{1,0:T(8,128)(2,1)S(1)}, u32[]{:S(2)}, u32[]{:S(2)}) collective-permute-start(bf16[160,1024]{1,0:T(8,128)(2,1)S(1)} %pad.16), channel_id=1, source_target_pairs={{0,2},{1,3},{2,0},{3,1},{4,6},{5,7},{6,4},{7,5},{8,10},{9,11},{10,... | collective-permute-start | bytes 983048 | tf_op jit(solution)/shard_map/ppermute | solution.py:185
  59.6 18.9 %collective-permute-start.37 = (bf16[160,1024]{1,0:T(8,128)(2,1)S(1)}, bf16[160,1024]{1,0:T(8,128)(2,1)S(1)}, u32[]{:S(2)}, u32[]{:S(2)}) collective-permute-start(bf16[160,1024]{1,0:T(8,128)(2,1)S(1)} %pad.17), channel_id=1, source_target_pairs={{0,2},{1,3},{2,0},{3,1},{4,6},{5,7},{6,4},{7,5},{8,10},{9,11},{10,... | collective-permute-start | bytes 983048 | tf_op jit(solution)/shard_map/ppermute | solution.py:185
  62.8 6.2 %collective-permute-start.10 = (bf16[2,32,1024]{2,1,0:T(8,128)(2,1)S(1)}, bf16[2,32,1024]{2,1,0:T(8,128)(2,1)S(1)}, u32[]{:S(2)}, u32[]{:S(2)}) collective-permute-start(bf16[2,32,1024]{2,1,0:T(8,128)(2,1)S(1)} %maximum_bitcast_fusion.3), channel_id=1, source_target_pairs={{0,8},{1,9},{2,10},{3,11},{4,12},{5,13},{6,14},{7,15},{8,0},{9,1},... | collective-permute-start | bytes 393224 | tf_op jit(solution)/shard_map/ppermute | solution.py:185
  68.9 12.1 %collective-permute-start.6 = (bf16[2,128,768]{1,2,0:T(8,128)(2,1)S(1)}, bf16[2,128,768]{1,2,0:T(8,128)(2,1)S(1)}, u32[]{:S(2)}, u32[]{:S(2)}) collective-permute-start(bf16[2,128,768]{1,2,0:T(8,128)(2,1)S(1)} %maximum_bitcast_fusion.2), channel_id=1, source_target_pairs={{0,8},{1,9},{2,10},{3,11},{4,12},{5,13},{6,14},{7,15},{8,0},{9,1},... | collective-permute-start | bytes 1179656 | tf_op jit(solution)/shard_map/ppermute | solution.py:185
  72.7 19.6 %collective-permute-start.19 = (bf16[2,128,1024]{1,2,0:T(8,128)(2,1)}, bf16[2,128,1024]{1,2,0:T(8,128)(2,1)}, u32[]{:S(2)}, u32[]{:S(2)}) collective-permute-start(bf16[2,128,1024]{1,2,0:T(8,128)(2,1)} %maximum_bitcast_fusion.1), channel_id=1, source_target_pairs={{0,8},{1,9},{2,10},{3,11},{4,12},{5,13},{6,14},{7,15},{8,0},{9,1},... | collective-permute-start | bytes 1572872 | tf_op jit(solution)/shard_map/ppermute | solution.py:185
  72.8 6.8 %collective-permute-start.11 = (bf16[4,32,1024]{2,1,0:T(8,128)(2,1)S(1)}, bf16[4,32,1024]{2,1,0:T(8,128)(2,1)S(1)}, u32[]{:S(2)}, u32[]{:S(2)}) collective-permute-start(bf16[4,32,1024]{2,1,0:T(8,128)(2,1)S(1)} %bitcast.407), channel_id=1, source_target_pairs={{0,4},{1,5},{2,6},{3,7},{4,0},{5,1},{6,2},{7,3},{8,12},{9,13},{10,... | collective-permute-start | bytes 786440 | tf_op jit(solution)/shard_map/ppermute | solution.py:185
  77.5 66.8 %collective-permute-start.16 = (bf16[2,128,1024]{1,2,0:T(8,128)(2,1)}, bf16[2,128,1024]{1,2,0:T(8,128)(2,1)}, u32[]{:S(2)}, u32[]{:S(2)}) collective-permute-start(bf16[2,128,1024]{1,2,0:T(8,128)(2,1)} %maximum_bitcast_fusion), channel_id=1, source_target_pairs={{0,8},{1,9},{2,10},{3,11},{4,12},{5,13},{6,14},{7,15},{8,0},{9,1},... | collective-permute-start | bytes 1572872 | tf_op jit(solution)/shard_map/ppermute | solution.py:185
  78.5 16.6 %collective-permute-start.24 = (bf16[320,1024]{1,0:T(8,128)(2,1)}, bf16[320,1024]{1,0:T(8,128)(2,1)}, u32[]{:S(2)}, u32[]{:S(2)}) collective-permute-start(bf16[320,1024]{1,0:T(8,128)(2,1)} %get-tuple-element.179), channel_id=1, source_target_pairs={{0,1},{1,0},{2,3},{3,2},{4,5},{5,4},{6,7},{7,6},{8,9},{9,8},{10,11... | collective-permute-start | bytes 1966088 | tf_op jit(solution)/shard_map/ppermute | solution.py:185
  79.6 22.3 %collective-permute-start.1 = (bf16[320,1024]{1,0:T(8,128)(2,1)}, bf16[320,1024]{1,0:T(8,128)(2,1)}, u32[]{:S(2)}, u32[]{:S(2)}) collective-permute-start(bf16[320,1024]{1,0:T(8,128)(2,1)} %get-tuple-element.178), channel_id=1, source_target_pairs={{0,1},{1,0},{2,3},{3,2},{4,5},{5,4},{6,7},{7,6},{8,9},{9,8},{10,11... | collective-permute-start | bytes 1966088 | tf_op jit(solution)/shard_map/ppermute | solution.py:185
  81.0 124.0 %collective-permute-start.31 = (bf16[320,1024]{1,0:T(8,128)(2,1)}, bf16[320,1024]{1,0:T(8,128)(2,1)}, u32[]{:S(2)}, u32[]{:S(2)}) collective-permute-start(bf16[320,1024]{1,0:T(8,128)(2,1)} %pad_maximum_fusion.10), channel_id=1, source_target_pairs={{0,1},{1,0},{2,3},{3,2},{4,5},{5,4},{6,7},{7,6},{8,9},{9,8},{10,11... | collective-permute-start | bytes 1966088 | tf_op jit(solution)/shard_map/ppermute | solution.py:185
  92.4 105.8 %collective-permute-start.38 = (bf16[320,1024]{1,0:T(8,128)(2,1)}, bf16[320,1024]{1,0:T(8,128)(2,1)}, u32[]{:S(2)}, u32[]{:S(2)}) collective-permute-start(bf16[320,1024]{1,0:T(8,128)(2,1)} %pad_maximum_fusion.11), channel_id=1, source_target_pairs={{0,1},{1,0},{2,3},{3,2},{4,5},{5,4},{6,7},{7,6},{8,9},{9,8},{10,11... | collective-permute-start | bytes 1966088 | tf_op jit(solution)/shard_map/ppermute | solution.py:185
  95.1 20.7 %collective-permute-start.7 = (bf16[4,128,768]{2,1,0:T(8,128)(2,1)}, bf16[4,128,768]{2,1,0:T(8,128)(2,1)}, u32[]{:S(2)}, u32[]{:S(2)}) collective-permute-start(bf16[4,128,768]{2,1,0:T(8,128)(2,1)} %bitcast.25), channel_id=1, source_target_pairs={{0,4},{1,5},{2,6},{3,7},{4,0},{5,1},{6,2},{7,3},{8,12},{9,13},{10,... | collective-permute-start | bytes 2359304 | tf_op jit(solution)/shard_map/ppermute | solution.py:185
  102.0 51.7 %collective-permute-start.20 = (bf16[4,128,1024]{2,1,0:T(8,128)(2,1)}, bf16[4,128,1024]{2,1,0:T(8,128)(2,1)}, u32[]{:S(2)}, u32[]{:S(2)}) collective-permute-start(bf16[4,128,1024]{2,1,0:T(8,128)(2,1)} %bitcast.62), channel_id=1, source_target_pairs={{0,4},{1,5},{2,6},{3,7},{4,0},{5,1},{6,2},{7,3},{8,12},{9,13},{10,... | collective-permute-start | bytes 3145736 | tf_op jit(solution)/shard_map/ppermute | solution.py:185
  129.4 16.1 %collective-permute-start.25 = (bf16[320,1024]{1,0:T(8,128)(2,1)S(1)}, bf16[320,1024]{1,0:T(8,128)(2,1)S(1)}, u32[]{:S(2)}, u32[]{:S(2)}) collective-permute-start(bf16[320,1024]{1,0:T(8,128)(2,1)S(1)} %slice.536), channel_id=1, source_target_pairs={{0,1},{1,0},{2,3},{3,2},{4,5},{5,4},{6,7},{7,6},{8,9},{9,8},{10,11... | collective-permute-start | bytes 1966088 | tf_op jit(solution)/shard_map/ppermute | solution.py:185
  144.3 6.8 %collective-permute-start.12 = (bf16[320,1024]{1,0:T(8,128)(2,1)}, bf16[320,1024]{1,0:T(8,128)(2,1)}, u32[]{:S(2)}, u32[]{:S(2)}) collective-permute-start(bf16[320,1024]{1,0:T(8,128)(2,1)} %slice.538), channel_id=1, source_target_pairs={{0,1},{1,0},{2,3},{3,2},{4,5},{5,4},{6,7},{7,6},{8,9},{9,8},{10,11... | collective-permute-start | bytes 1966088 | tf_op jit(solution)/shard_map/ppermute | solution.py:185
  146.6 17.8 %collective-permute-start.26 = (bf16[320,1024]{1,0:T(8,128)(2,1)}, bf16[320,1024]{1,0:T(8,128)(2,1)}, u32[]{:S(2)}, u32[]{:S(2)}) collective-permute-start(bf16[320,1024]{1,0:T(8,128)(2,1)} %fusion.13), channel_id=1, source_target_pairs={{0,2},{1,3},{2,0},{3,1},{4,6},{5,7},{6,4},{7,5},{8,10},{9,11},{10,... | collective-permute-start | bytes 1966088 | tf_op jit(solution)/shard_map/ppermute | solution.py:185
  151.1 29.3 %collective-permute-start.17 = (bf16[4,128,1024]{2,1,0:T(8,128)(2,1)}, bf16[4,128,1024]{2,1,0:T(8,128)(2,1)S(1)}, u32[]{:S(2)}, u32[]{:S(2)}) collective-permute-start(bf16[4,128,1024]{2,1,0:T(8,128)(2,1)} %bitcast.381), channel_id=1, source_target_pairs={{0,4},{1,5},{2,6},{3,7},{4,0},{5,1},{6,2},{7,3},{8,12},{9,13},{10,... | collective-permute-start | bytes 3145736 | tf_op jit(solution)/shard_map/ppermute | solution.py:185
  153.6 24.3 %collective-permute-start.13 = (bf16[320,1024]{1,0:T(8,128)(2,1)S(1)}, bf16[320,1024]{1,0:T(8,128)(2,1)S(1)}, u32[]{:S(2)}, u32[]{:S(2)}) collective-permute-start(bf16[320,1024]{1,0:T(8,128)(2,1)S(1)} %fusion.12), channel_id=1, source_target_pairs={{0,2},{1,3},{2,0},{3,1},{4,6},{5,7},{6,4},{7,5},{8,10},{9,11},{10,... | collective-permute-start | bytes 1966088 | tf_op jit(solution)/shard_map/ppermute | solution.py:185
  166.0 16.2 %collective-permute-start.27 = (bf16[320,1024]{1,0:T(8,128)(2,1)S(1)}, bf16[320,1024]{1,0:T(8,128)(2,1)S(1)}, u32[]{:S(2)}, u32[]{:S(2)}) collective-permute-start(bf16[320,1024]{1,0:T(8,128)(2,1)S(1)} %get-tuple-element.106), channel_id=1, source_target_pairs={{0,1},{1,0},{2,3},{3,2},{4,5},{5,4},{6,7},{7,6},{8,9},{9,8},{10,11... | collective-permute-start | bytes 1966088 | tf_op jit(solution)/shard_map/ppermute | solution.py:185
  192.5 33.9 %collective-permute-start.21 = (bf16[320,1024]{1,0:T(8,128)(2,1)}, bf16[320,1024]{1,0:T(8,128)(2,1)}, u32[]{:S(2)}, u32[]{:S(2)}) collective-permute-start(bf16[320,1024]{1,0:T(8,128)(2,1)} %slice.537), channel_id=1, source_target_pairs={{0,1},{1,0},{2,3},{3,2},{4,5},{5,4},{6,7},{7,6},{8,9},{9,8},{10,11... | collective-permute-start | bytes 1966088 | tf_op jit(solution)/shard_map/ppermute | solution.py:185
  197.9 30.8 %collective-permute-start.28 = (bf16[320,1024]{1,0:T(8,128)(2,1)}, bf16[320,1024]{1,0:T(8,128)(2,1)}, u32[]{:S(2)}, u32[]{:S(2)}) collective-permute-start(bf16[320,1024]{1,0:T(8,128)(2,1)} %slice.535), channel_id=1, source_target_pairs={{0,1},{1,0},{2,3},{3,2},{4,5},{5,4},{6,7},{7,6},{8,9},{9,8},{10,11... | collective-permute-start | bytes 1966088 | tf_op jit(solution)/shard_map/ppermute | solution.py:185
  211.1 19.7 %collective-permute-start.32 = (bf16[320,1024]{1,0:T(8,128)(2,1)}, bf16[320,1024]{1,0:T(8,128)(2,1)S(1)}, u32[]{:S(2)}, u32[]{:S(2)}) collective-permute-start(bf16[320,1024]{1,0:T(8,128)(2,1)} %slice.534), channel_id=1, source_target_pairs={{0,1},{1,0},{2,3},{3,2},{4,5},{5,4},{6,7},{7,6},{8,9},{9,8},{10,11... | collective-permute-start | bytes 1966088 | tf_op jit(solution)/shard_map/ppermute | solution.py:185
  212.3 20.1 %collective-permute-start.39 = (bf16[320,1024]{1,0:T(8,128)(2,1)}, bf16[320,1024]{1,0:T(8,128)(2,1)S(1)}, u32[]{:S(2)}, u32[]{:S(2)}) collective-permute-start(bf16[320,1024]{1,0:T(8,128)(2,1)} %slice.532), channel_id=1, source_target_pairs={{0,1},{1,0},{2,3},{3,2},{4,5},{5,4},{6,7},{7,6},{8,9},{9,8},{10,11... | collective-permute-start | bytes 1966088 | tf_op jit(solution)/shard_map/ppermute | solution.py:185
  214.7 33.6 %collective-permute-start.60 = (bf16[4,128,1024]{2,1,0:T(8,128)(2,1)S(1)}, bf16[4,128,1024]{2,1,0:T(8,128)(2,1)}, u32[]{:S(2)}, u32[]{:S(2)}) collective-permute-start(bf16[4,128,1024]{2,1,0:T(8,128)(2,1)S(1)} %fusion.11), channel_id=1, source_target_pairs={{0,4},{1,5},{2,6},{3,7},{4,0},{5,1},{6,2},{7,3},{8,12},{9,13},{10,... | collective-permute-start | bytes 3145736 | tf_op jit(solution)/shard_map/ppermute | solution.py:185
  226.4 36.1 %collective-permute-start.65 = (bf16[4,128,1024]{2,1,0:T(8,128)(2,1)S(1)}, bf16[4,128,1024]{2,1,0:T(8,128)(2,1)S(1)}, u32[]{:S(2)}, u32[]{:S(2)}) collective-permute-start(bf16[4,128,1024]{2,1,0:T(8,128)(2,1)S(1)} %fusion.10), channel_id=1, source_target_pairs={{0,4},{1,5},{2,6},{3,7},{4,0},{5,1},{6,2},{7,3},{8,12},{9,13},{10,... | collective-permute-start | bytes 3145736 | tf_op jit(solution)/shard_map/ppermute | solution.py:185
  228.7 10.7 %collective-permute-start.22 = (bf16[160,1024]{1,0:T(8,128)(2,1)S(1)}, bf16[160,1024]{1,0:T(8,128)(2,1)S(1)}, u32[]{:S(2)}, u32[]{:S(2)}) collective-permute-start(bf16[160,1024]{1,0:T(8,128)(2,1)S(1)} %slice.542), channel_id=1, source_target_pairs={{0,2},{1,3},{2,0},{3,1},{4,6},{5,7},{6,4},{7,5},{8,10},{9,11},{10,... | collective-permute-start | bytes 983048 | tf_op jit(solution)/shard_map/ppermute | solution.py:185
  230.9 15.5 %collective-permute-start.29 = (bf16[160,1024]{1,0:T(8,128)(2,1)S(1)}, bf16[160,1024]{1,0:T(8,128)(2,1)S(1)}, u32[]{:S(2)}, u32[]{:S(2)}) collective-permute-start(bf16[160,1024]{1,0:T(8,128)(2,1)S(1)} %slice.541), channel_id=1, source_target_pairs={{0,2},{1,3},{2,0},{3,1},{4,6},{5,7},{6,4},{7,5},{8,10},{9,11},{10,... | collective-permute-start | bytes 983048 | tf_op jit(solution)/shard_map/ppermute | solution.py:185
  232.4 32.2 %collective-permute-start.33 = (bf16[320,1024]{1,0:T(8,128)(2,1)S(1)}, bf16[320,1024]{1,0:T(8,128)(2,1)S(1)}, u32[]{:S(2)}, u32[]{:S(2)}) collective-permute-start(bf16[320,1024]{1,0:T(8,128)(2,1)S(1)} %fusion.14), channel_id=1, source_target_pairs={{0,2},{1,3},{2,0},{3,1},{4,6},{5,7},{6,4},{7,5},{8,10},{9,11},{10,... | collective-permute-start | bytes 1966088 | tf_op jit(solution)/shard_map/ppermute | solution.py:185
  239.3 34.1 %collective-permute-start.40 = (bf16[320,1024]{1,0:T(8,128)(2,1)S(1)}, bf16[320,1024]{1,0:T(8,128)(2,1)S(1)}, u32[]{:S(2)}, u32[]{:S(2)}) collective-permute-start(bf16[320,1024]{1,0:T(8,128)(2,1)S(1)} %fusion.15), channel_id=1, source_target_pairs={{0,2},{1,3},{2,0},{3,1},{4,6},{5,7},{6,4},{7,5},{8,10},{9,11},{10,... | collective-permute-start | bytes 1966088 | tf_op jit(solution)/shard_map/ppermute | solution.py:185
  249.8 24.8 %collective-permute-start.61 = (bf16[2,128,1024]{2,1,0:T(8,128)(2,1)S(1)}, bf16[2,128,1024]{2,1,0:T(8,128)(2,1)S(1)}, u32[]{:S(2)}, u32[]{:S(2)}) collective-permute-start(bf16[2,128,1024]{2,1,0:T(8,128)(2,1)S(1)} %fusion.43), channel_id=1, source_target_pairs={{0,8},{1,9},{2,10},{3,11},{4,12},{5,13},{6,14},{7,15},{8,0},{9,1},... | collective-permute-start | bytes 1572872 | tf_op jit(solution)/shard_map/ppermute | solution.py:185
  263.1 13.7 %collective-permute-start.66 = (bf16[2,128,1024]{2,1,0:T(8,128)(2,1)S(1)}, bf16[2,128,1024]{2,1,0:T(8,128)(2,1)S(1)}, u32[]{:S(2)}, u32[]{:S(2)}) collective-permute-start(bf16[2,128,1024]{2,1,0:T(8,128)(2,1)S(1)} %fusion.44), channel_id=1, source_target_pairs={{0,8},{1,9},{2,10},{3,11},{4,12},{5,13},{6,14},{7,15},{8,0},{9,1},... | collective-permute-start | bytes 1572872 | tf_op jit(solution)/shard_map/ppermute | solution.py:185
  265.3 37.5 %collective-permute-start.34 = (bf16[320,1024]{1,0:T(8,128)(2,1)S(1)}, bf16[320,1024]{1,0:T(8,128)(2,1)S(1)}, u32[]{:S(2)}, u32[]{:S(2)}) collective-permute-start(bf16[320,1024]{1,0:T(8,128)(2,1)S(1)} %get-tuple-element.96), channel_id=1, source_target_pairs={{0,1},{1,0},{2,3},{3,2},{4,5},{5,4},{6,7},{7,6},{8,9},{9,8},{10,11... | collective-permute-start | bytes 1966088 | tf_op jit(solution)/shard_map/ppermute | solution.py:185
  273.9 29.0 %collective-permute-start.41 = (bf16[320,1024]{1,0:T(8,128)(2,1)S(1)}, bf16[320,1024]{1,0:T(8,128)(2,1)S(1)}, u32[]{:S(2)}, u32[]{:S(2)}) collective-permute-start(bf16[320,1024]{1,0:T(8,128)(2,1)S(1)} %get-tuple-element.98), channel_id=1, source_target_pairs={{0,1},{1,0},{2,3},{3,2},{4,5},{5,4},{6,7},{7,6},{8,9},{9,8},{10,11... | collective-permute-start | bytes 1966088 | tf_op jit(solution)/shard_map/ppermute | solution.py:185
  274.9 21.3 %collective-permute-start.62 = (bf16[1,128,1024]{2,1,0:T(8,128)(2,1)S(1)}, bf16[1,128,1024]{2,1,0:T(8,128)(2,1)S(1)}, u32[]{:S(2)}, u32[]{:S(2)}) collective-permute-start(bf16[1,128,1024]{2,1,0:T(8,128)(2,1)S(1)} %dynamic-slice_convert_fusion.3), channel_id=1, source_target_pairs={{0,16},{1,17},{2,18},{3,19},{4,20},{5,21},{6,22},{7,23},{8,24},{9,... | collective-permute-start | bytes 786440 | tf_op jit(solution)/shard_map/ppermute | solution.py:185
  277.1 24.4 %collective-permute-start.67 = (bf16[1,128,1024]{2,1,0:T(8,128)(2,1)S(1)}, bf16[1,128,1024]{2,1,0:T(8,128)(2,1)S(1)}, u32[]{:S(2)}, u32[]{:S(2)}) collective-permute-start(bf16[1,128,1024]{2,1,0:T(8,128)(2,1)S(1)} %dynamic-slice_convert_fusion.2), channel_id=1, source_target_pairs={{0,16},{1,17},{2,18},{3,19},{4,20},{5,21},{6,22},{7,23},{8,24},{9,... | collective-permute-start | bytes 786440 | tf_op jit(solution)/shard_map/ppermute | solution.py:185
  296.9 68.1 %collective-permute-start.63 = (bf16[128,1024]{1,0:T(8,128)(2,1)}, bf16[128,1024]{1,0:T(8,128)(2,1)}, u32[]{:S(2)}, u32[]{:S(2)}) collective-permute-start(bf16[128,1024]{1,0:T(8,128)(2,1)} %fusion.56), channel_id=1, source_target_pairs={{0,2},{1,3},{2,0},{3,1},{4,6},{5,7},{6,4},{7,5},{8,10},{9,11},{10,... | collective-permute-start | bytes 786440 | tf_op jit(solution)/shard_map/ppermute | solution.py:185
  302.2 73.7 %collective-permute-start.68 = (bf16[128,1024]{1,0:T(8,128)(2,1)}, bf16[128,1024]{1,0:T(8,128)(2,1)}, u32[]{:S(2)}, u32[]{:S(2)}) collective-permute-start(bf16[128,1024]{1,0:T(8,128)(2,1)} %fusion.57), channel_id=1, source_target_pairs={{0,2},{1,3},{2,0},{3,1},{4,6},{5,7},{6,4},{7,5},{8,10},{9,11},{10,... | collective-permute-start | bytes 786440 | tf_op jit(solution)/shard_map/ppermute | solution.py:185
  345.5 42.4 %collective-permute-start.35 = (bf16[320,1024]{1,0:T(8,128)(2,1)S(1)}, bf16[320,1024]{1,0:T(8,128)(2,1)S(1)}, u32[]{:S(2)}, u32[]{:S(2)}) collective-permute-start(bf16[320,1024]{1,0:T(8,128)(2,1)S(1)} %slice.533), channel_id=1, source_target_pairs={{0,1},{1,0},{2,3},{3,2},{4,5},{5,4},{6,7},{7,6},{8,9},{9,8},{10,11... | collective-permute-start | bytes 1966088 | tf_op jit(solution)/shard_map/ppermute | solution.py:185
  348.9 41.9 %collective-permute-start.42 = (bf16[320,1024]{1,0:T(8,128)(2,1)}, bf16[320,1024]{1,0:T(8,128)(2,1)}, u32[]{:S(2)}, u32[]{:S(2)}) collective-permute-start(bf16[320,1024]{1,0:T(8,128)(2,1)} %slice.531), channel_id=1, source_target_pairs={{0,1},{1,0},{2,3},{3,2},{4,5},{5,4},{6,7},{7,6},{8,9},{9,8},{10,11... | collective-permute-start | bytes 1966088 | tf_op jit(solution)/shard_map/ppermute | solution.py:185
  355.1 8.8 %collective-permute-start.54 = (bf16[4,32,1024]{2,1,0:T(8,128)(2,1)S(1)}, bf16[4,32,1024]{2,1,0:T(8,128)(2,1)S(1)}, u32[]{:S(2)}, u32[]{:S(2)}) collective-permute-start(bf16[4,32,1024]{2,1,0:T(8,128)(2,1)S(1)} %fusion.55), channel_id=1, source_target_pairs={{0,4},{1,5},{2,6},{3,7},{4,0},{5,1},{6,2},{7,3},{8,12},{9,13},{10,... | collective-permute-start | bytes 786440 | tf_op jit(solution)/shard_map/ppermute | solution.py:185
  363.9 43.1 %collective-permute-start.49 = (bf16[4,128,768]{2,1,0:T(8,128)(2,1)}, bf16[4,128,768]{2,1,0:T(8,128)(2,1)}, u32[]{:S(2)}, u32[]{:S(2)}) collective-permute-start(bf16[4,128,768]{2,1,0:T(8,128)(2,1)} %fusion.16), channel_id=1, source_target_pairs={{0,4},{1,5},{2,6},{3,7},{4,0},{5,1},{6,2},{7,3},{8,12},{9,13},{10,... | collective-permute-start | bytes 2359304 | tf_op jit(solution)/shard_map/ppermute | solution.py:185
  365.0 5.0 %collective-permute-start.55 = (bf16[2,32,1024]{2,1,0:T(8,128)(2,1)S(1)}, bf16[2,32,1024]{2,1,0:T(8,128)(2,1)S(1)}, u32[]{:S(2)}, u32[]{:S(2)}) collective-permute-start(bf16[2,32,1024]{2,1,0:T(8,128)(2,1)S(1)} %fusion.61), channel_id=1, source_target_pairs={{0,8},{1,9},{2,10},{3,11},{4,12},{5,13},{6,14},{7,15},{8,0},{9,1},... | collective-permute-start | bytes 393224 | tf_op jit(solution)/shard_map/ppermute | solution.py:185
  370.1 5.8 %collective-permute-start.56 = (bf16[1,32,1024]{2,1,0:T(8,128)(2,1)S(1)}, bf16[1,32,1024]{2,1,0:T(8,128)(2,1)S(1)}, u32[]{:S(2)}, u32[]{:S(2)}) collective-permute-start(bf16[1,32,1024]{2,1,0:T(8,128)(2,1)S(1)} %dynamic-slice_convert_fusion.6), channel_id=1, source_target_pairs={{0,16},{1,17},{2,18},{3,19},{4,20},{5,21},{6,22},{7,23},{8,24},{9,... | collective-permute-start | bytes 196616 | tf_op jit(solution)/shard_map/ppermute | solution.py:185
  375.8 19.6 %collective-permute-start.64 = (bf16[2,128,1024]{2,1,0:T(8,128)(2,1)S(1)}, bf16[2,128,1024]{2,1,0:T(8,128)(2,1)S(1)}, u32[]{:S(2)}, u32[]{:S(2)}) collective-permute-start(bf16[2,128,1024]{2,1,0:T(8,128)(2,1)S(1)} %pad_maximum_fusion.15), channel_id=1, source_target_pairs={{0,1},{1,0},{2,3},{3,2},{4,5},{5,4},{6,7},{7,6},{8,9},{9,8},{10,11... | collective-permute-start | bytes 1572872 | tf_op jit(solution)/shard_map/ppermute | solution.py:185
  377.6 9.1 %collective-permute-start.58 = (bf16[32,1024]{1,0:T(8,128)(2,1)S(1)}, bf16[32,1024]{1,0:T(8,128)(2,1)S(1)}, u32[]{:S(2)}, u32[]{:S(2)}) collective-permute-start(bf16[32,1024]{1,0:T(8,128)(2,1)S(1)} %collective-permute-done.57), channel_id=1, source_target_pairs={{0,2},{1,3},{2,0},{3,1},{4,6},{5,7},{6,4},{7,5},{8,10},{9,11},{10,... | collective-permute-start | bytes 196616 | tf_op jit(solution)/shard_map/ppermute | solution.py:185
  386.8 8.7 %collective-permute-start.69 = (bf16[2,128,1024]{2,1,0:T(8,128)(2,1)S(1)}, bf16[2,128,1024]{2,1,0:T(8,128)(2,1)S(1)}, u32[]{:S(2)}, u32[]{:S(2)}) collective-permute-start(bf16[2,128,1024]{2,1,0:T(8,128)(2,1)S(1)} %pad_maximum_fusion.16), channel_id=1, source_target_pairs={{0,1},{1,0},{2,3},{3,2},{4,5},{5,4},{6,7},{7,6},{8,9},{9,8},{10,11... | collective-permute-start | bytes 1572872 | tf_op jit(solution)/shard_map/ppermute | solution.py:185
  388.8 16.0 %collective-permute-start.59 = (bf16[2,32,1024]{2,1,0:T(8,128)(2,1)}, bf16[2,32,1024]{2,1,0:T(8,128)(2,1)}, u32[]{:S(2)}, u32[]{:S(2)}) collective-permute-start(bf16[2,32,1024]{2,1,0:T(8,128)(2,1)} %pad_maximum_fusion.22), channel_id=1, source_target_pairs={{0,1},{1,0},{2,3},{3,2},{4,5},{5,4},{6,7},{7,6},{8,9},{9,8},{10,11... | collective-permute-start | bytes 393224 | tf_op jit(solution)/shard_map/ppermute | solution.py:185
  390.9 17.9 %collective-permute-start.36 = (bf16[160,1024]{1,0:T(8,128)(2,1)}, bf16[160,1024]{1,0:T(8,128)(2,1)}, u32[]{:S(2)}, u32[]{:S(2)}) collective-permute-start(bf16[160,1024]{1,0:T(8,128)(2,1)} %slice.540), channel_id=1, source_target_pairs={{0,2},{1,3},{2,0},{3,1},{4,6},{5,7},{6,4},{7,5},{8,10},{9,11},{10,... | collective-permute-start | bytes 983048 | tf_op jit(solution)/shard_map/ppermute | solution.py:185
  395.4 13.4 %collective-permute-start.43 = (bf16[160,1024]{1,0:T(8,128)(2,1)}, bf16[160,1024]{1,0:T(8,128)(2,1)}, u32[]{:S(2)}, u32[]{:S(2)}) collective-permute-start(bf16[160,1024]{1,0:T(8,128)(2,1)} %slice.539), channel_id=1, source_target_pairs={{0,2},{1,3},{2,0},{3,1},{4,6},{5,7},{6,4},{7,5},{8,10},{9,11},{10,... | collective-permute-start | bytes 983048 | tf_op jit(solution)/shard_map/ppermute | solution.py:185
  408.4 18.5 %collective-permute-start.50 = (bf16[2,128,768]{2,1,0:T(8,128)(2,1)S(1)}, bf16[2,128,768]{2,1,0:T(8,128)(2,1)S(1)}, u32[]{:S(2)}, u32[]{:S(2)}) collective-permute-start(bf16[2,128,768]{2,1,0:T(8,128)(2,1)S(1)} %fusion.45), channel_id=1, source_target_pairs={{0,8},{1,9},{2,10},{3,11},{4,12},{5,13},{6,14},{7,15},{8,0},{9,1},... | collective-permute-start | bytes 1179656 | tf_op jit(solution)/shard_map/ppermute | solution.py:185
  411.5 4.8 %collective-permute-start.44 = (f32[4,12,128]{2,0,1:T(4,128)S(1)}, f32[4,12,128]{2,0,1:T(4,128)S(1)}, u32[]{:S(2)}, u32[]{:S(2)}) collective-permute-start(f32[4,12,128]{2,0,1:T(4,128)S(1)} %bitcast.420), channel_id=1, source_target_pairs={{0,4},{1,5},{2,6},{3,7},{4,0},{5,1},{6,2},{7,3},{8,12},{9,13},{10,... | collective-permute-start | bytes 73736 | tf_op jit(solution)/shard_map/ppermute | solution.py:185
  416.4 3.8 collective-permute-start.45
  420.2 5.5 %collective-permute-start.46 = (f32[1,12,128]{2,0,1:T(1,128)S(1)}, f32[1,12,128]{2,0,1:T(1,128)S(1)}, u32[]{:S(2)}, u32[]{:S(2)}) collective-permute-start(f32[1,12,128]{2,0,1:T(1,128)S(1)} %constant_dynamic-slice_fusion), channel_id=1, source_target_pairs={{0,16},{1,17},{2,18},{3,19},{4,20},{5,21},{6,22},{7,23},{8,24},{9,... | collective-permute-start | bytes 18440 | tf_op jit(solution)/shard_map/ppermute | solution.py:185
  425.7 4.1 collective-permute-start.47
  427.0 8.8 %collective-permute-start.51 = (bf16[1,128,768]{2,1,0:T(8,128)(2,1)S(1)}, bf16[1,128,768]{2,1,0:T(8,128)(2,1)S(1)}, u32[]{:S(2)}, u32[]{:S(2)}) collective-permute-start(bf16[1,128,768]{2,1,0:T(8,128)(2,1)S(1)} %dynamic-slice_convert_fusion.5), channel_id=1, source_target_pairs={{0,16},{1,17},{2,18},{3,19},{4,20},{5,21},{6,22},{7,23},{8,24},{9,... | collective-permute-start | bytes 589832 | tf_op jit(solution)/shard_map/ppermute | solution.py:185
  435.8 5.7 %collective-permute-start.52 = (bf16[128,768]{1,0:T(8,128)(2,1)S(1)}, bf16[128,768]{1,0:T(8,128)(2,1)S(1)}, u32[]{:S(2)}, u32[]{:S(2)}) collective-permute-start(bf16[128,768]{1,0:T(8,128)(2,1)S(1)} %fusion.58), channel_id=1, source_target_pairs={{0,2},{1,3},{2,0},{3,1},{4,6},{5,7},{6,4},{7,5},{8,10},{9,11},{10,... | collective-permute-start | bytes 589832 | tf_op jit(solution)/shard_map/ppermute | solution.py:185
  (108 other events, 831.2 us)

commit v2 on v1

v2 whole, which is shorter than its diff:
```python
import functools

import jax
import jax.numpy as jnp
from jax import lax
from jax.experimental import pallas as pl
from jax.experimental.pallas import tpu as pltpu
from jax.sharding import PartitionSpec as P

D = 1024
HEADS = 16
HEAD_DIM = 64
LIVE = 577
PAD = 160
MASK_ROW = 148
NEG = -1e30
F32 = jnp.float32
BF16 = jnp.bfloat16


def dot(a, b):
    return lax.dot_general(a, b, (((1,), (0,)), ((), ())), preferred_element_type=F32)


def dot_nt(a, b):
    return lax.dot_general(a, b, (((1,), (1,)), ((), ())), preferred_element_type=F32)


def dot_tn(a, b):
    return lax.dot_general(a, b, (((0,), (0,)), ((), ())), preferred_element_type=F32)


def layer_norm(values):
    centred = values - jnp.mean(values, axis=-1, keepdims=True)
    inverse = lax.rsqrt(jnp.mean(centred * centred, axis=-1, keepdims=True) + 1e-05)
    return centred * inverse, inverse


def norm_reverse(grad, normed, inverse):
    first = jnp.mean(grad, axis=-1, keepdims=True)
    second = jnp.mean(grad * normed, axis=-1, keepdims=True)
    return inverse * (grad - first - normed * second)


def attn_fwd_kernel(qkv_ref, bias_ref, o_ref):
    rows = qkv_ref.shape[0]
    lane = lax.broadcasted_iota(jnp.int32, (1, 128), 1)
    k = qkv_ref[:, 128:256]
    v = qkv_ref[:, 256:384]
    bias = bias_ref[...]
    for start in range(0, rows, 128):
        q = qkv_ref[start : start + 128, 0:128] * 0.125
        outs = []
        for h in range(2):
            qh = jnp.where((lane // 64) == h, q, jnp.zeros_like(q))
            s = dot_nt(qh, k) + bias
            top = jnp.max(s, axis=-1, keepdims=True)
            e = jnp.exp(s - top)
            total = jnp.sum(e, axis=-1, keepdims=True)
            p = (e * (1.0 / total)).astype(BF16)
            outs.append(dot(p, v))
        o_ref[start : start + 128, :] = jnp.where(lane < 64, outs[0], outs[1]).astype(BF16)


def attn_bwd_kernel(qkv_ref, g_ref, bias_ref, d_ref, sum_ref, dk_acc, dv_acc):
    rows = qkv_ref.shape[0]
    lane = lax.broadcasted_iota(jnp.int32, (1, 128), 1)
    k = qkv_ref[:, 128:256]
    v = qkv_ref[:, 256:384]
    bias = bias_ref[:, 0:1]
    qsum = jnp.zeros((1, 128), F32)
    for start in range(0, rows, 128):
        q = qkv_ref[start : start + 128, 0:128] * 0.125
        g = g_ref[start : start + 128, :]
        dqs, dks, dvs = [], [], []
        for h in range(2):
            mine = (lane // 64) == h
            qh = jnp.where(mine, q, jnp.zeros_like(q))
            gh = jnp.where(mine, g, jnp.zeros_like(g))
            s = dot_nt(k, qh) + bias
            top = jnp.max(s, axis=0, keepdims=True)
            e = jnp.exp(s - top)
            total = jnp.sum(e, axis=0, keepdims=True)
            p = e * (1.0 / total)
            dp = dot_nt(v, gh)
            delta = jnp.sum(p * dp, axis=0, keepdims=True)
            ds = (p * (dp - delta)).astype(BF16)
            dvs.append(dot(p.astype(BF16), gh))
            dks.append(dot(ds, qh))
            dqs.append(dot_tn(ds, k))
        dq = jnp.where(lane < 64, dqs[0], dqs[1]) * 0.125
        qsum = qsum + jnp.sum(dq, axis=0, keepdims=True)
        d_ref[start : start + 128, 0:128] = dq.astype(BF16)
        dk = dks[0] + dks[1]
        dv = dvs[0] + dvs[1]
        if start == 0:
            dk_acc[...] = dk
            dv_acc[...] = dv
        else:
            dk_acc[...] += dk
            dv_acc[...] += dv
    d_ref[:, 128:256] = dk_acc[...].astype(BF16)
    dv = dv_acc[...]
    d_ref[:, 256:384] = dv.astype(BF16)
    vsum = jnp.sum(dv, axis=0, keepdims=True)
    sum_ref[...] = jnp.concatenate([qsum, vsum, jnp.zeros((6, 128), F32)], axis=0)


def params(mib):
    return pltpu.CompilerParams(vmem_limit_bytes=mib << 20)


def cost(us):
    return pl.CostEstimate(flops=int(us * 1.1535e9), bytes_accessed=1024, transcendentals=0)


def attention(qkv, bias_row):
    rows = qkv.shape[0]
    return pl.pallas_call(
        attn_fwd_kernel,
        out_shape=jax.ShapeDtypeStruct((rows, 128), BF16),
        compiler_params=params(40),
        cost_estimate=cost(4.2),
        name="attn_fwd",
    )(qkv, bias_row)


def attention_back(pair, qkv, grad, bias_col):
    rows = grad.shape[0]
    full = lambda shape: pl.BlockSpec(shape, lambda i: (0, 0))
    return pl.pallas_call(
        attn_bwd_kernel,
        grid=(1,),
        in_specs=[
            full((rows, 384)),
            pl.BlockSpec((rows, 128), lambda i: (0, pair)),
            full((rows, 128)),
        ],
        out_specs=[full((rows, 384)), full((8, 128))],
        out_shape=[
            jax.ShapeDtypeStruct((rows, 384), BF16),
            jax.ShapeDtypeStruct((8, 128), F32),
        ],
        scratch_shapes=[pltpu.VMEM((rows, 128), F32)] * 2,
        compiler_params=params(48),
        cost_estimate=cost(6.0),
        name="attn_bwd",
    )(qkv, grad, bias_col)


CHUNK = 32
SC_SCATTER = True
SLOTS = (0, 2, 1, 3)


def prepare_kernel(n_img, *refs):
    slots, vec_ref, outs = refs[:4], refs[4], refs[5:]
    gain, add = vec_ref[0:1, :], vec_ref[2:3, :]
    for i in range(n_img):
        out_ref, bias_ref = outs[i], outs[n_img + i]
        for j, src in enumerate(slots):

            def step(k, carry):
                lo = pl.multiple_of(k * CHUNK, CHUNK)
                normed, _ = layer_norm(src[i, pl.ds(lo, CHUNK), :].astype(F32))
                out_ref[pl.ds(j * PAD + lo, CHUNK), :] = (normed * gain + add).astype(BF16)
                return carry

            lax.fori_loop(0, PAD // CHUNK, step, 0)
        masks = [src[i, MASK_ROW : MASK_ROW + 1, 0:PAD].astype(F32) for src in slots]
        bias_ref[...] = (1.0 - jnp.concatenate(masks, axis=1)) * NEG


def prepare(slots, small):
    n_img = slots[0].shape[0]
    out = pl.pallas_call(
        functools.partial(prepare_kernel, n_img),
        out_shape=[jax.ShapeDtypeStruct((4 * PAD, D), BF16)] * n_img
        + [jax.ShapeDtypeStruct((1, 4 * PAD), F32)] * n_img,
        compiler_params=params(40),
        cost_estimate=cost(6.0),
        name="prepare",
    )(*slots, small)
    return out[:n_img], out[n_img:]


def stack_kernel(n_img, *refs):
    slots, outs = refs[:4], refs[4:]
    for i in range(n_img):
        for j, src in enumerate(slots):
            outs[i][j * PAD : j * PAD + PAD, :] = src[i]


def stack_rows(slots):
    n_img = slots[0].shape[0]
    return pl.pallas_call(
        functools.partial(stack_kernel, n_img),
        out_shape=[jax.ShapeDtypeStruct((4 * PAD, D), BF16)] * n_img,
        compiler_params=params(32),
        cost_estimate=cost(2.0),
        name="stack_rows",
    )(*slots)


def middle_kernel(*refs):
    slots, (a_ref, b_ref, vec_ref, mid_ref, out_ref) = refs[:4], refs[4:]
    shift, gain, add = vec_ref[6:7, :], vec_ref[1:2, :], vec_ref[3:4, :]

    for j, src in enumerate(slots):
        part_ref = a_ref if j < 2 else b_ref

        def step(i, carry):
            lo = pl.multiple_of(i * CHUNK, CHUNK)
            at = pl.ds(j * PAD + lo, CHUNK)
            m = src[0, pl.ds(lo, CHUNK), :].astype(F32) + shift
            m = m + part_ref[pl.ds((j % 2) * PAD + lo, CHUNK), :].astype(F32)
            mid_ref[at, :] = m
            normed, _ = layer_norm(m)
            out_ref[at, :] = (normed * gain + add).astype(BF16)
            return carry

        lax.fori_loop(0, PAD // CHUNK, step, 0)


def middle_rows(image, slots, a, b, small):
    rows = 4 * PAD
    piece = pl.BlockSpec((1, PAD, D), lambda i: (image, 0, 0))
    full = lambda shape: pl.BlockSpec(shape, lambda i: (0, 0))
    return pl.pallas_call(
        middle_kernel,
        grid=(1,),
        in_specs=[piece] * 4 + [full(a.shape), full(b.shape), full(small.shape)],
        out_specs=[full((rows, D)), full((rows, D))],
        out_shape=[
            jax.ShapeDtypeStruct((rows, D), F32),
            jax.ShapeDtypeStruct((rows, D), BF16),
        ],
        compiler_params=params(32),
        cost_estimate=cost(2.4),
        name="middle",
    )(*slots, a, b, small)


def middle_back_kernel(mid_ref, a_ref, b_ref, g_ref, vec_ref, low_ref, own_ref, sum_ref):
    gain = vec_ref[1:2, :]
    half = a_ref.shape[0]

    def rows(src, base, lo):
        at = pl.ds(base + lo, CHUNK)
        normed, inverse = layer_norm(mid_ref[at, :])
        t = src[pl.ds(lo, CHUNK), :].astype(F32)
        g = g_ref[at, :].astype(F32)
        d = g + norm_reverse(t * gain, normed, inverse)
        low_ref[at, :] = d.astype(BF16)
        return normed, t, g, d

    def own(i, carry):
        lo = pl.multiple_of(i * CHUNK, CHUNK)
        normed, t, g, d = rows(a_ref, 0, lo)
        own_ref[pl.ds(lo, CHUNK), :] = d
        new = [jnp.sum(v, axis=0, keepdims=True) for v in (t * normed, t, d, g)]
        return tuple(c + n for c, n in zip(carry, new))

    zero = jnp.zeros((1, D), F32)
    sums = lax.fori_loop(0, PAD // CHUNK, own, (zero,) * 4)

    def other(src, base, first):
        def step(i, carry):
            rows(src, base, pl.multiple_of(i * CHUNK, CHUNK))
            return carry

        lax.fori_loop(first, half // CHUNK, step, 0, unroll=2 if first == 0 else 1)

    other(a_ref, 0, PAD // CHUNK)
    other(b_ref, half, 0)
    sum_ref[...] = jnp.concatenate(list(sums) + [jnp.zeros((4, D), F32)], axis=0)


def middle_back(mid, a, b, g, small):
    rows = mid.shape[0]
    return pl.pallas_call(
        middle_back_kernel,
        out_shape=[
            jax.ShapeDtypeStruct((rows, D), BF16),
            jax.ShapeDtypeStruct((PAD, D), F32),
            jax.ShapeDtypeStruct((8, D), F32),
        ],
        compiler_params=params(32),
        cost_estimate=cost(4.0),
        name="middle_back",
    )(mid, a, b, g, small)


def pieces_of(length):
    return [(lo, min(CHUNK, length - lo)) for lo in range(0, length, CHUNK)]


def result_kernel(n_img, *refs):
    mids, mine, got = refs[:n_img], refs[n_img : 2 * n_img], refs[2 * n_img : 3 * n_img]
    vec_ref, out_ref = refs[3 * n_img :]
    shift = vec_ref[7:8, :]
    for i in range(n_img):
        for lo, n in pieces_of(out_ref.shape[1]):
            at = slice(lo, lo + n)
            total = mids[i][at, :] + mine[i][at, :].astype(F32) + got[i][at, :].astype(F32)
            out_ref[i, at, :] = (total + shift).astype(BF16)


def result_rows(length, mids, mine, got, small):
    n_img = len(mids)
    spec = pl.BlockSpec((PAD, D), lambda i: (0, 0))
    return pl.pallas_call(
        functools.partial(result_kernel, n_img),
        grid=(1,),
        in_specs=[spec] * (3 * n_img) + [pl.BlockSpec(small.shape, lambda i: (0, 0))],
        out_specs=pl.BlockSpec((n_img, length, D), lambda i: (0, 0, 0)),
        out_shape=jax.ShapeDtypeStruct((n_img, length, D), BF16),
        compiler_params=params(32),
        cost_estimate=cost(1.5),
        name="result",
    )(*mids, *mine, *got, small)


def tokens_back_kernel(n_img, x_ref, *refs):
    dmid, mine, got = refs[:n_img], refs[n_img : 2 * n_img], refs[2 * n_img : 3 * n_img]
    vec_ref, out_ref, sum_ref = refs[3 * n_img :]
    gain = vec_ref[0:1, :]
    first = jnp.zeros((1, D), F32)
    second = jnp.zeros((1, D), F32)
    for i in range(n_img):
        for lo, n in pieces_of(out_ref.shape[1]):
            at = slice(lo, lo + n)
            normed, inverse = layer_norm(x_ref[i, at, :].astype(F32))
            u = mine[i][at, :].astype(F32) + got[i][at, :].astype(F32)
            first = first + jnp.sum(u * normed, axis=0, keepdims=True)
            second = second + jnp.sum(u, axis=0, keepdims=True)
            d = dmid[i][at, :] + norm_reverse(u * gain, normed, inverse)
            out_ref[i, at, :] = d.astype(BF16)
    sum_ref[...] = jnp.concatenate([first, second, jnp.zeros((6, D), F32)], axis=0)


def tokens_back(length, x, dmid, mine, got, small):
    n_img = len(dmid)
    spec = pl.BlockSpec((PAD, D), lambda i: (0, 0))
    return pl.pallas_call(
        functools.partial(tokens_back_kernel, n_img),
        grid=(1,),
        in_specs=[pl.BlockSpec(x.shape, lambda i: (0, 0, 0))]
        + [spec] * (3 * n_img)
        + [pl.BlockSpec(small.shape, lambda i: (0, 0))],
        out_specs=[
            pl.BlockSpec((n_img, length, D), lambda i: (0, 0, 0)),
            pl.BlockSpec((8, D), lambda i: (0, 0)),
        ],
        out_shape=[
            jax.ShapeDtypeStruct((n_img, length, D), BF16),
            jax.ShapeDtypeStruct((8, D), F32),
        ],
        compiler_params=params(32),
        cost_estimate=cost(2.0),
        name="tokens_back",
    )(x, *dmid, *mine, *got, small)


def weave_kernel(bit_ref, a_ref, b_ref, o_ref):
    up = bit_ref[0]
    for i in range(a_ref.shape[0]):
        o_ref[i, up] = a_ref[i]
        o_ref[i, 1 - up] = b_ref[i]


def weave(bit, a, b):
    m, r, w = a.shape
    if r % 8 or w % 128:
        up = bit == 1
        low, high = jnp.where(up, b, a), jnp.where(up, a, b)
        return jnp.stack([low, high], axis=1).reshape(2 * m, r, w)
    vmem = pl.BlockSpec(memory_space=pltpu.VMEM)
    out = pl.pallas_call(
        weave_kernel,
        in_specs=[pl.BlockSpec(memory_space=pltpu.SMEM), vmem, vmem],
        out_specs=vmem,
        out_shape=jax.ShapeDtypeStruct((m, 2, r, w), a.dtype),
        compiler_params=params(24),
        cost_estimate=cost(0.5 + m * r * w * 2e-6),
        name="weave",
    )(bit.astype(jnp.int32).reshape(1), a, b)
    return out.reshape(2 * m, r, w)


def place_qkv_kernel(c_ref, *refs):
    out_ref = refs[-1]
    c = c_ref[0]
    for j, ref in enumerate(refs[:-1]):
        pair, slot = j // 4, j % 4
        for k in range(3):
            at = pl.multiple_of(k * D + (c ^ SLOTS[slot]) * 256 + pair * 128, 128)
            out_ref[:, pl.ds(at, 128)] = ref[:, k * 128 : k * 128 + 128].astype(F32)


def place_rest_kernel(r, wide, piece, c_ref, *refs):
    slots, (fc2_ref, fc1_ref, out_ref) = refs[:4], refs[4:]
    c = c_ref[0]
    for slot, ref in enumerate(slots):
        q = c ^ SLOTS[slot]
        fc2_ref[pl.ds(pl.multiple_of(q * wide, 8), wide), :] = ref[0:wide, :].astype(F32)
        for f in range(D // wide):
            at = pl.multiple_of(f * 4 * wide + q * wide, 128)
            fc1_ref[:, pl.ds(at, wide)] = ref[wide : wide + r, f * wide : (f + 1) * wide].astype(F32)
        out_ref[pl.ds(pl.multiple_of(q * piece, 8), piece), :] = ref[wide + r :, :].astype(F32)


def in_order(c, slots):
    own, y, core, both = slots
    odd = c % 2 == 1
    low = [jnp.where(odd, core, own), jnp.where(odd, own, core)]
    high = [jnp.where(odd, both, y), jnp.where(odd, y, both)]
    up = c // 2 == 1
    return jnp.stack(
        [jnp.where(up, b, a) for a, b in zip(low, high)]
        + [jnp.where(up, a, b) for a, b in zip(low, high)]
    )


def place_qkv(c, pairs):
    r = pairs[0][0].shape[0]
    smem = pl.BlockSpec(memory_space=pltpu.SMEM)
    vmem = pl.BlockSpec(memory_space=pltpu.VMEM)
    flat = [v for slots in pairs for v in slots]
    return pl.pallas_call(
        place_qkv_kernel,
        in_specs=[smem] + [vmem] * len(flat),
        out_specs=vmem,
        out_shape=jax.ShapeDtypeStruct((r, 3 * D), F32),
        compiler_params=params(24),
        cost_estimate=cost(1.5),
        name="place_qkv",
    )(c.astype(jnp.int32).reshape(1), *flat)


def place_rest(c, r, wide, piece, slots):
    if wide % 128 or piece % 8:
        full = in_order(c, slots).astype(F32)
        fc2 = full[:, :wide].reshape(-1, D)
        fc1 = full[:, wide : wide + r].reshape(4, r, D // wide, wide)
        fc1 = fc1.transpose(1, 2, 0, 3).reshape(r, 4 * D)
        return fc2, fc1, full[:, wide + r :].reshape(-1, D)
    smem = pl.BlockSpec(memory_space=pltpu.SMEM)
    vmem = pl.BlockSpec(memory_space=pltpu.VMEM)
    return pl.pallas_call(
        functools.partial(place_rest_kernel, r, wide, piece),
        in_specs=[smem] + [vmem] * 4,
        out_specs=[vmem] * 3,
        out_shape=[
            jax.ShapeDtypeStruct((4 * wide, D), F32),
            jax.ShapeDtypeStruct((r, 4 * D), F32),
            jax.ShapeDtypeStruct((4 * piece, D), F32),
        ],
        compiler_params=params(32),
        cost_estimate=cost(4.0),
        name="place_rest",
    )(c.astype(jnp.int32).reshape(1), *slots)


def gate(value, *after):
    return lax.optimization_barrier((value,) + after)[0]


def body(
    nf,
    nc,
    tokens,
    out_grad,
    key_mask,
    slot_valid,
    norm_gains,
    norm_shifts,
    qkv_weight,
    qv_bias,
    out_weight,
    out_bias,
    fc1_weight,
    fc1_bias,
    fc2_weight,
    fc2_bias,
):
    f = lax.axis_index("fsdp")
    c = lax.axis_index("ctx")
    axes = ("fsdp", "ctx")
    bits = []
    while (1 << len(bits)) < nf:
        bits.append(1 << len(bits))

    def swap(v, df, dc):
        pairs = [(i * nc + j, (i ^ df) * nc + (j ^ dc)) for i in range(nf) for j in range(nc)]
        return lax.ppermute(v, axes, pairs)

    def core(v):
        return swap(v, 0, 1)

    def across(v):
        return swap(v, 0, 2)

    def gather_steps(shard):
        held = [shard[None]]
        for b in reversed(bits):
            buf = held[-1]
            held.append(weave((f // b) % 2, buf, swap(buf, b, 0)))
        return held

    def flat(buf):
        return buf.reshape((-1,) + buf.shape[2:])

    def scatter(full, low):
        for b in bits:
            v = full.reshape((full.shape[0] // 2, 2) + full.shape[1:])
            up = (f // b) % 2
            send = lax.dynamic_index_in_dim(v, 1 - up, 1, keepdims=False).astype(low)
            keep = lax.dynamic_index_in_dim(v, up, 1, keepdims=False)
            full = keep + swap(send, b, 0).astype(F32)
        return full[0]

    def slots_of(v):
        y = across(v)
        return [v, y, core(v), core(y)]

    n_img, length = tokens.shape[0], tokens.shape[1]
    quarter = D // nc
    rows_w = D // nf
    wide = 4 * D // nf // nc
    piece = rows_w // nc
    half = 2 * PAD

    by_pair = lax.dynamic_index_in_dim(
        qkv_weight.reshape(rows_w, 3, nc, 2, 128), c, 2, keepdims=False
    )
    qkv_held = [gather_steps(by_pair[:, :, p, :].reshape(rows_w, 384)) for p in range(2)]
    w_qkv = [flat(held[-1]) for held in qkv_held]

    small = jnp.concatenate(
        [
            norm_gains,
            norm_shifts,
            qv_bias,
            out_bias[None],
            fc2_bias[None],
            fc1_bias.reshape(4, D // nf),
        ],
        axis=0,
    )
    buf = small[None]
    for b in reversed(bits):
        other = swap(buf, b, 0)
        up = (f // b) % 2 == 1
        low, high = jnp.where(up, other, buf), jnp.where(up, buf, other)
        buf = jnp.stack([low, high], axis=1).reshape((2 * buf.shape[0],) + small.shape)
    small = buf.transpose(1, 0, 2).reshape(12, D).astype(F32)
    fc1_shift = lax.dynamic_slice_in_dim(small, 8 + c, 1, 0)
    qkv_shift = []
    for p in range(2):
        q_shift = lax.dynamic_slice(small, (4, c * quarter + p * 128), (1, 128))
        v_shift = lax.dynamic_slice(small, (5, c * quarter + p * 128), (1, 128))
        qkv_shift.append(jnp.concatenate([q_shift, jnp.zeros_like(q_shift), v_shift], axis=1))

    mask_rows = jnp.pad(key_mask.astype(BF16), ((0, 0), (0, D - length)))[:, None, :]
    x_own = jnp.concatenate(
        [tokens, mask_rows, jnp.zeros((n_img, PAD - length - 1, D), BF16)], axis=1
    )
    x_slots = slots_of(x_own)
    position = c * length + jnp.arange(length)
    keep = (position < LIVE)[None, :] & (slot_valid[:, None] > 0)
    g_own = jnp.where(keep[:, :, None], out_grad, jnp.zeros((), BF16))
    g_own = jnp.pad(g_own, ((0, 0), (0, PAD - length), (0, 0)))
    g_slots = slots_of(gate(g_own, x_slots[1]))
    g_all = stack_rows(g_slots)

    out_pairs = []
    for fs in range(nf):
        for j in range(nc):
            dst_f = (fs % (nf // 4)) * 4 + j
            out_pairs.append((fs * nc + j, dst_f * nc + fs // (nf // 4)))
    out_back = [(b, a) for a, b in out_pairs]
    out_part = lax.dynamic_slice_in_dim(out_weight, c * piece, piece, 0)
    out_part = lax.ppermute(gate(out_part, qkv_held[0][1]), axes, out_pairs)
    out_held = gather_steps(gate(out_part, qkv_held[1][1]))
    fc1_part = lax.dynamic_index_in_dim(
        fc1_weight.reshape(rows_w, nf, 4, wide), c, 2, keepdims=False
    ).reshape(rows_w, D)
    fc1_held = gather_steps(gate(fc1_part, out_held[1], qkv_held[1][2]))
    fc2_part = lax.dynamic_slice_in_dim(fc2_weight, c * wide, wide, 0)
    fc2_held = gather_steps(gate(fc2_part, fc1_held[1]))
    w_out, w_fc1, w_fc2 = flat(out_held[-1]), flat(fc1_held[-1]), flat(fc2_held[-1])

    images = range(n_img)
    normed, bias = prepare(x_slots, small)
    qkv = [[None] * n_img for _ in range(2)]
    contexts = [[None] * n_img for _ in range(2)]

    def reduce_send(left, weight, back=False):
        product = dot_nt if back else dot
        return product(left[half:], weight).astype(BF16)

    def reduce_mine(left, weight, got, back=False):
        product = dot_nt if back else dot
        return (product(left[:half], weight) + got.astype(F32)).astype(BF16)

    def finish(mine):
        got = across(mine)
        got = jnp.concatenate([got[PAD:], got[:PAD]], axis=0)
        mine = (mine.astype(F32) + got.astype(F32)).astype(BF16)
        return mine, core(mine)

    context, sums1 = [None] * n_img, [None] * n_img
    last = None
    for p in range(2):
        for i in images:
            qkv[p][i] = (dot(normed[i], w_qkv[p]) + qkv_shift[p]).astype(BF16)
            ready = qkv[p][i] if last is None else gate(qkv[p][i], last)
            contexts[p][i] = attention(ready, bias[i])
            last = None
            if p == 1:
                context[i] = jnp.concatenate([contexts[0][i], contexts[1][i]], axis=1)
                send = reduce_send(context[i], w_out)
                mine = reduce_mine(context[i], w_out, core(send))
                sums1[i] = finish(mine)
                last = mine

    middle, normed_mid, hidden, d_pre_low, fc1_sum, sums2 = [], [], [], [], [], []
    for i in images:
        mid, low = middle_rows(i, x_slots, sums1[i][0], sums1[i][1], small)
        middle.append(mid)
        normed_mid.append(low)
        pre = dot(low, w_fc1) + fc1_shift
        sig = jax.nn.sigmoid(1.702 * pre)
        hidden.append((pre * sig).astype(BF16))
        d_hidden = dot_nt(g_all[i], w_fc2)
        d_pre = d_hidden * (sig + 1.702 * pre * sig * (1.0 - sig))
        fc1_sum.append(jnp.sum(d_pre, axis=0, keepdims=True))
        d_pre_low.append(d_pre.astype(BF16))
        send = reduce_send(d_pre_low[i], w_fc1, True)
        mine = reduce_mine(d_pre_low[i], w_fc1, core(send), True)
        sums2.append(finish(mine))
        last = mine

    def over_images(lefts, rights):
        total = dot_tn(lefts[0], rights[0])
        for a, b in zip(lefts[1:], rights[1:]):
            total = total + dot_tn(a, b)
        return total

    p_fc2 = over_images([gate(h, last) for h in hidden], g_all)
    p_fc1 = over_images(normed_mid, d_pre_low)
    if SC_SCATTER:
        both = jnp.concatenate([p_fc2.astype(BF16), p_fc1.astype(BF16)], axis=1)
        both = lax.psum_scatter(both, "fsdp", scatter_dimension=0, tiled=True)
        fc2_g, fc1_g = both[:, :D], both[:, D:]
    else:
        fc2_g = scatter(p_fc2.reshape(nf, -1, D), BF16).astype(BF16)
        fc1_g = scatter(p_fc1.reshape(nf, -1, D), BF16).astype(BF16)

    mines, gots = [], []
    for i in images:
        send = reduce_send(gate(hidden[i], sums2[-1][0]), w_fc2)
        mine = reduce_mine(hidden[i], w_fc2, core(send))
        mines.append(mine)
        gots.append(across(mine[PAD:]))
    result = result_rows(length, middle, mines, gots, small)

    d_mid_low, d_mid_own, mid_sums, d_context = [], [], [], []
    for i in images:
        low, own, sums = middle_back(middle[i], sums2[i][0], sums2[i][1], g_all[i], small)
        d_mid_low.append(low)
        d_mid_own.append(own)
        mid_sums.append(sums)
        d_context.append(dot_nt(low, w_out).astype(BF16))
    p_out = over_images(context, d_mid_low)
    out_g = scatter(p_out.reshape(nf, -1, D), BF16).astype(BF16)
    out_g = lax.ppermute(out_g, axes, out_back)

    d_raw = [[None] * n_img for _ in range(2)]
    qv_sum = []
    qkv_slots = []
    for p in range(2):
        sums = []
        for i in images:
            bias_col = jnp.broadcast_to(bias[i].reshape(-1, 1), (4 * PAD, 128))
            d_raw[p][i], s = attention_back(p, qkv[p][i], d_context[i], bias_col)
            sums.append(s)
        qv_sum.append(sum(sums[1:], sums[0]))
        lefts = normed if p == 0 else [gate(normed[0], result)] + list(normed[1:])
        p_qkv = over_images(lefts, d_raw[p])
        qkv_g = scatter(p_qkv.reshape(nf, -1, 384), BF16).astype(BF16)
        qkv_slots.append(slots_of(qkv_g))

    mines, gots = [], []
    for i in images:
        parts = [d_raw[p][i] for p in range(2)]
        send = sum(dot_nt(parts[p][half:], w_qkv[p]) for p in range(2)).astype(BF16)
        mine = sum(dot_nt(parts[p][:half], w_qkv[p]) for p in range(2))
        mine = (mine + core(send).astype(F32)).astype(BF16)
        mines.append(mine)
        gots.append(across(mine[PAD:]))
    token_gradient, tok_sums = tokens_back(length, x_own, d_mid_own, mines, gots, small)

    rest = jnp.concatenate([fc2_g, fc1_g, out_g], axis=0)
    fc2_full, fc1_full, out_full = place_rest(c, rows_w, wide, piece, slots_of(rest))
    qkv_full = place_qkv(c, qkv_slots)

    mid_sum = sum(mid_sums[1:], mid_sums[0])
    fc1_rows = jnp.where((jnp.arange(4) == c)[:, None], sum(fc1_sum[1:], fc1_sum[0]), 0.0)
    here = (jnp.arange(D) // quarter == c)[None]
    qv_rows = jnp.concatenate([s[0:2] for s in qv_sum], axis=1)
    qv_rows = jnp.where(here, jnp.tile(qv_rows, (1, nc)), 0.0)
    packed = jnp.concatenate(
        [tok_sums[0:1], mid_sum[0:1], tok_sums[1:2], mid_sum[1:2], qv_rows, mid_sum[2:4], fc1_rows],
        axis=0,
    )
    packed = packed.reshape(12, nf, D // nf).transpose(1, 0, 2)
    packed = scatter(packed, F32)
    packed = packed + across(packed)
    packed = packed + core(packed)

    return (
        result,
        token_gradient,
        packed[0:2],
        packed[2:4],
        qkv_full,
        packed[4:6],
        out_full,
        packed[6],
        fc1_full,
        packed[8:12].reshape(-1),
        fc2_full,
        packed[7],
    )


def solution(mesh):
    in_specs = (
        P("fsdp", "ctx", None),
        P("fsdp", "ctx", None),
        P("fsdp", "ctx"),
        P("fsdp"),
        P(None, "fsdp"),
        P(None, "fsdp"),
        P("fsdp", None),
        P(None, "fsdp"),
        P("fsdp", None),
        P("fsdp"),
        P("fsdp", None),
        P("fsdp"),
        P("fsdp", None),
        P("fsdp"),
    )
    out_specs = (
        P("fsdp", "ctx", None),
        P("fsdp", "ctx", None),
        P(None, "fsdp"),
        P(None, "fsdp"),
        P("fsdp", None),
        P(None, "fsdp"),
        P("fsdp", None),
        P("fsdp"),
        P("fsdp", None),
        P("fsdp"),
        P("fsdp", None),
        P("fsdp"),
    )
    step = functools.partial(body, mesh.shape["fsdp"], mesh.shape["ctx"])
    return jax.shard_map(step, mesh=mesh, in_specs=in_specs, out_specs=out_specs, check_vma=False)
```

time: 455 us -> 368 us (0.81)
  other arithmetic: 65.3 us -> 9.02 us
  Pallas kernels: 42.7 us -> 85.4 us
  local copies, waits for them, and re-layouts: 63.4 us -> 23.4 us
  waiting for transfers between devices: 141 us -> 105 us
  between operations: 5.16 us -> 16.2 us
  starting transfers between devices: 81.3 us -> 72.8 us
    pallas_call x4 -> x33, Pallas kernels: 42.7 us -> 85.4 us  [the longest x4 24.2 us: attention_back(): pl.pallas_call(attn_bwd_kernel, grid=(1,), in_specs=[full((rows, 384)), p...]
    ppermute x68 -> x67, waiting for transfers between devices: 141 us -> 105 us  [swap(): return lax.ppermute(v, axes, pairs)]
    another operation x43 -> x4, other arithmetic: 17.1 us -> 0.04 us  [body(): jnp.stack([low, high], axis=1).reshape((2 * buf.shape[0],) + small.shape)]
    reduce_sum x13 -> x0, other arithmetic: 14.4 us -> none  [the longest x3 4.23 us: layer_norm(): centred = values - jnp.mean(values, axis=-1, keepdims=True)]
    slice x32 -> x14, local copies, waits for them, and re-layouts: 15.5 us -> 3.39 us  [the longest x4 1.46 us: finish(): got = jnp.concatenate([got[PAD:], got[:PAD]], axis=0)]
    add x7 -> x4, other arithmetic: 9.88 us -> 0.02 us  [the longest x1 0.01 us: body(): mid_sum = sum(mid_sums[1:], mid_sums[0])]
    concatenate x4 -> x2, local copies, waits for them, and re-layouts: 9.97 us -> 0.14 us  [the longest x1 0.08 us: body(): jnp.concatenate([tokens, mask_rows, jnp.zeros((n_img, PAD - length - 1, D...]
    dot_general x8 -> x10, matrix products: 22.6 us -> 13.1 us  [dot_tn(): lax.dot_general(a, b, (((0,), (0,)), ((), ())), preferred_element_type=F32)]
  transfers between devices with their start and end apart: 70 -> 70, of which waited for: 27 -> 24; matrix products, arithmetic and copies ran while one was open for 37% -> 21% of each run, Pallas kernels for 10% -> 23%
where the time goes in v2:
time: 368 us; the launch traced here: 361 us
  waiting for transfers between devices  105 us (29%)
  Pallas kernels  85.4 us (23%)
  starting transfers between devices  72.8 us (20%)
  matrix products  49.8 us (14%)
  local copies, waits for them, and re-layouts  23.4 us (6%)
  between operations  16.2 us (4%)
  other arithmetic  9.02 us (2%)
    ppermute x67, waiting for transfers between devices, swap(): return lax.ppermute(v, axes, pairs)  105 us
    ppermute x67, starting transfers between devices, swap(): return lax.ppermute(v, axes, pairs)  71.4 us
    pallas_call x4, Pallas kernels, attention_back(): pl.pallas_call(attn_bwd_kernel, grid=(1,), in_specs=[full((rows, 384)), p...  24.2 us
    dot_general x14, matrix products, dot(): lax.dot_general(a, b, (((1,), (0,)), ((), ())), preferred_element_type=F32)  19.1 us
    dot_general x16, matrix products, dot_nt(): lax.dot_general(a, b, (((1,), (1,)), ((), ())), preferred_element_type=F32)  17.7 us
    pallas_call x4, Pallas kernels, attention(): pl.pallas_call(attn_fwd_kernel, out_shape=jax.ShapeDtypeStruct((rows, 128...  16.7 us
    dot_general x10, matrix products, dot_tn(): lax.dot_general(a, b, (((0,), (0,)), ((), ())), preferred_element_type=F32)  13.1 us
    pallas_call x2, Pallas kernels, middle_rows(): pl.pallas_call(middle_kernel, grid=(1,), in_specs=[piece] * 4 + [full(a.s...  10.6 us
  transfers between devices with their start and end apart: 70, of which 24 were waited for; matrix products, arithmetic and copies ran while one was open for 21% of the time, Pallas kernels for 23%

profile of v2, /device:TPU:0, one launch (start us, length us, event | category | flops | bytes accessed | tf_op | source)
XLA Modules:
  0.0 361.4 jit_solution(10523995335755464660)
XLA Ops:
  9.6 3.0 collective-permute-start
  13.7 2.7 collective-permute-start.6
  17.0 2.6 collective-permute-start.3
  20.2 2.6 reshape.241
  22.8 2.8 dynamic-slice_reduce_fusion
  32.7 1.6 collective-permute-start.7
  34.9 4.7 %collective-permute-start.13 = (bf16[1,32,1024]{2,1,0:T(8,128)(2,1)S(1)}, bf16[1,32,1024]{2,1,0:T(8,128)(2,1)S(1)}, u32[]{:S(2)}, u32[]{:S(2)}) collective-permute-start(bf16[1,32,1024]{2,1,0:T(8,128)(2,1)S(1)} %bitcast.253), channel_id=1, source_target_pairs={{0,16},{1,17},{2,18},{3,19},{4,20},{5,21},{6,22},{7,23},{8,24},{9,... | collective-permute-start | bytes 196616 | tf_op jit(solution)/shard_map/ppermute | solution.py:496
  39.6 5.0 %collective-permute-done.13.b_ref = bf16[1,32,1024]{2,1,0:T(8,128)(2,1)S(1)} collective-permute-done((bf16[1,32,1024]{2,1,0:T(8,128)(2,1)S(1)}, bf16[1,32,1024]{2,1,0:T(8,128)(2,1)S(1)}, u32[]{:S(2)}, u32[]{:S(2)}) %collective-permute-start.13) | collective-permute-done | bytes 65568 | tf_op jit(solution)/shard_map/ppermute | solution.py:496
  46.2 2.8 collective-permute-start.14
  49.0 2.1 collective-permute-start.8
  52.7 1.8 collective-permute-start.22
  55.2 11.8 %collective-permute-done.22.b_ref = bf16[1,128,1024]{2,1,0:T(8,128)(2,1)S(1)} collective-permute-done((bf16[1,128,1024]{2,1,0:T(8,128)(2,1)S(1)}, bf16[1,128,1024]{2,1,0:T(8,128)(2,1)S(1)}, u32[]{:S(2)}, u32[]{:S(2)}) %collective-permute-start.22) | collective-permute-done | bytes 262176 | tf_op jit(solution)/shard_map/ppermute | solution.py:496
  68.9 1.7 collective-permute-start.25
  70.7 6.5 %collective-permute-done.11.b_ref = bf16[4,128,384]{2,1,0:T(8,128)(2,1)S(1)} collective-permute-done((bf16[4,128,384]{2,1,0:T(8,128)(2,1)S(1)}, bf16[4,128,384]{2,1,0:T(8,128)(2,1)S(1)}, u32[]{:S(2)}, u32[]{:S(2)}) %collective-permute-start.11) | collective-permute-done | bytes 393248 | tf_op jit(solution)/shard_map/ppermute | solution.py:496
  77.3 7.4 %collective-permute-done.25.b_ref = bf16[1,128,1024]{2,1,0:T(8,128)(2,1)S(1)} collective-permute-done((bf16[1,128,1024]{2,1,0:T(8,128)(2,1)S(1)}, bf16[1,128,1024]{2,1,0:T(8,128)(2,1)S(1)}, u32[]{:S(2)}, u32[]{:S(2)}) %collective-permute-start.25) | collective-permute-done | bytes 262176 | tf_op jit(solution)/shard_map/ppermute | solution.py:496
  86.9 1.7 collective-permute-start.26
  90.2 10.1 %prepare.1 = (bf16[640,1024]{1,0:T(8,128)(2,1)S(1)}, bf16[640,1024]{1,0:T(8,128)(2,1)S(1)}, f32[1,640]{1,0:T(1,128)S(1)}, f32[1,640]{1,0:T(1,128)S(1)}) custom-call(bf16[2,160,1024]{2,1,0:T(8,128)(2,1)S(1)} %copy-done.19, bf16[2,160,1024]{2,1,0:T(8,128)(2,1)} %collective-permute-done.refs_1_, bf16[2,160,1024]{2,1,0:T(8,128)(2,1)} %collective-permute-done.1.refs_2_, ...), custom_call_target="tpu_custom_call" | custom-call | flops 6920999936 | bytes 1024 | tf_op jit(solution)/shard_map/prepare/pallas_call | solution.py:176
  101.2 4.1 %attn_fwd.4 = bf16[640,128]{1,0:T(8,128)(2,1)S(1)} custom-call(bf16[640,384]{1,0:T(8,128)(2,1)S(1)} %fusion.12.qkv_ref, f32[1,640]{1,0:T(1,128)S(1)} %get-tuple-element.53.bias_ref), custom_call_target="tpu_custom_call" | custom-call | flops 4844700160 | bytes 1024 | tf_op jit(solution)/shard_map/attn_fwd/pallas_call | solution.py:119
  106.2 4.1 %attn_fwd.5 = bf16[640,128]{1,0:T(8,128)(2,1)S(1)} custom-call(bf16[640,384]{1,0:T(8,128)(2,1)S(1)} %fusion.13.qkv_ref, f32[1,640]{1,0:T(1,128)S(1)} %get-tuple-element.53.bias_ref), custom_call_target="tpu_custom_call" | custom-call | flops 4844700160 | bytes 1024 | tf_op jit(solution)/shard_map/attn_fwd/pallas_call | solution.py:119
  113.1 4.1 %attn_fwd.6 = bf16[640,128]{1,0:T(8,128)(2,1)S(1)} custom-call(bf16[640,384]{1,0:T(8,128)(2,1)S(1)} %fusion.14.qkv_ref, f32[1,640]{1,0:T(1,128)S(1)} %get-tuple-element.58.bias_ref), custom_call_target="tpu_custom_call" | custom-call | flops 4844700160 | bytes 1024 | tf_op jit(solution)/shard_map/attn_fwd/pallas_call | solution.py:119
  118.4 4.3 %attn_fwd.7 = bf16[640,128]{1,0:T(8,128)(2,1)S(1)} custom-call(bf16[640,384]{1,0:T(8,128)(2,1)S(1)} %fusion.15.qkv_ref, f32[1,640]{1,0:T(1,128)S(1)} %get-tuple-element.58.bias_ref), custom_call_target="tpu_custom_call" | custom-call | flops 4844700160 | bytes 1024 | tf_op jit(solution)/shard_map/attn_fwd/pallas_call | solution.py:119
  125.6 1.8 collective-permute-start.27
  127.4 1.8 stack_rows.1
  129.3 2.7 weave.26
  135.2 6.8 %collective-permute-done.17 = bf16[320,1024]{1,0:T(8,128)(2,1)S(1)} collective-permute-done((bf16[320,1024]{1,0:T(8,128)(2,1)}, bf16[320,1024]{1,0:T(8,128)(2,1)S(1)}, u32[]{:S(2)}, u32[]{:S(2)}) %collective-permute-start.17) | collective-permute-done | bytes 655392 | tf_op jit(solution)/shard_map/ppermute | solution.py:496
  142.3 8.8 %collective-permute-done.27.b_ref = bf16[4,128,1024]{2,1,0:T(8,128)(2,1)S(1)} collective-permute-done((bf16[4,128,1024]{2,1,0:T(8,128)(2,1)S(1)}, bf16[4,128,1024]{2,1,0:T(8,128)(2,1)S(1)}, u32[]{:S(2)}, u32[]{:S(2)}) %collective-permute-start.27) | collective-permute-done | bytes 1048608 | tf_op jit(solution)/shard_map/ppermute | solution.py:496
  151.2 4.3 %collective-permute-done.20 = bf16[320,1024]{1,0:T(8,128)(2,1)S(1)} collective-permute-done((bf16[320,1024]{1,0:T(8,128)(2,1)S(1)}, bf16[320,1024]{1,0:T(8,128)(2,1)S(1)}, u32[]{:S(2)}, u32[]{:S(2)}) %collective-permute-start.20) | collective-permute-done | bytes 655392 | tf_op jit(solution)/shard_map/ppermute | solution.py:496
  156.9 5.2 %middle.2 = (f32[640,1024]{1,0:T(8,128)S(1)}, bf16[640,1024]{1,0:T(8,128)(2,1)S(1)}) custom-call(bf16[2,160,1024]{2,1,0:T(8,128)(2,1)S(1)} %copy-done.20, bf16[2,160,1024]{2,1,0:T(8,128)(2,1)} %collective-permute-done.refs_1_, bf16[2,160,1024]{2,1,0:T(8,128)(2,1)} %collective-permute-done.1.refs_2_, bf16[2,160,1024]{2,1,0:T(8,128)(2,1)S(1)} %copy-done.23, ...), custom_call_target="tpu_custom_call" | custom-call | flops 2768399872 | bytes 1024 | tf_op jit(solution)/shard_map/middle/pallas_call | solution.py:229
  163.6 2.3 fusion.67
  166.9 5.4 %middle.3 = (f32[640,1024]{1,0:T(8,128)S(1)}, bf16[640,1024]{1,0:T(8,128)(2,1)S(1)}) custom-call(bf16[2,160,1024]{2,1,0:T(8,128)(2,1)S(1)} %copy-done.20, bf16[2,160,1024]{2,1,0:T(8,128)(2,1)} %collective-permute-done.refs_1_, bf16[2,160,1024]{2,1,0:T(8,128)(2,1)} %collective-permute-done.1.refs_2_, bf16[2,160,1024]{2,1,0:T(8,128)(2,1)S(1)} %copy-done.23, ...), custom_call_target="tpu_custom_call" | custom-call | flops 2768399872 | bytes 1024 | tf_op jit(solution)/shard_map/middle/pallas_call | solution.py:229
  172.3 2.5 multiply_convert_fusion
  174.8 2.3 fusion.66
  178.5 1.8 fusion.81
  181.6 2.0 add_convert_fusion
  183.7 1.7 fusion.9
  185.4 1.7 collective-permute-start.32
  187.1 11.8 %collective-permute-done.38 = bf16[320,1024]{1,0:T(8,128)(2,1)S(1)} collective-permute-done((bf16[320,1024]{1,0:T(8,128)(2,1)S(1)}, bf16[320,1024]{1,0:T(8,128)(2,1)S(1)}, u32[]{:S(2)}, u32[]{:S(2)}) %collective-permute-start.38) | collective-permute-done | bytes 655392 | tf_op jit(solution)/shard_map/ppermute | solution.py:496
  200.1 1.9 fusion.80
  202.0 2.4 add_convert_fusion.1
  204.4 2.5 pad_maximum_fusion
  206.9 5.3 %collective-permute-done.32 = bf16[320,1024]{1,0:T(8,128)(2,1)} collective-permute-done((bf16[320,1024]{1,0:T(8,128)(2,1)}, bf16[320,1024]{1,0:T(8,128)(2,1)}, u32[]{:S(2)}, u32[]{:S(2)}) %collective-permute-start.32) | collective-permute-done | bytes 655392 | tf_op jit(solution)/shard_map/ppermute | solution.py:496
  216.2 5.8 %middle_back.2 = (bf16[640,1024]{1,0:T(8,128)(2,1)S(1)}, f32[160,1024]{1,0:T(8,128)S(1)}, f32[8,1024]{1,0:T(8,128)S(1)}) custom-call(f32[640,1024]{1,0:T(8,128)S(1)} %copy-done.5, bf16[320,1024]{1,0:T(8,128)(2,1)} %add_convert_fusion.2.a_ref, bf16[320,1024]{1,0:T(8,128)(2,1)} %collective-permute-done.39.b_ref, bf16[640,1024]{1,0:T(8,128)(2,1)S(1)} %copy-done.38, ...), custom_call_target="tpu_custom_call" | custom-call | flops 4614000128 | bytes 1024 | tf_op jit(solution)/shard_map/middle_back/pallas_call | solution.py:281
  223.1 6.1 %attn_bwd.5 = (bf16[640,384]{1,0:T(8,128)(2,1)S(1)}, f32[8,128]{1,0:T(8,128)S(1)}) custom-call(bf16[640,384]{1,0:T(8,128)(2,1)S(1)} %copy-done.36, bf16[640,256]{1,0:T(8,128)(2,1)S(1)} %convolution_convert_fusion.7.g_ref, f32[640,128]{1,0:T(8,128)S(1)} %broadcast_in_dim.106.bias_ref), custom_call_target="tpu_custom_call" | custom-call | flops 6920999936 | bytes 1024 | tf_op jit(solution)/shard_map/attn_bwd/pallas_call | solution.py:131
  229.2 6.0 %attn_bwd.4 = (bf16[640,384]{1,0:T(8,128)(2,1)S(1)}, f32[8,128]{1,0:T(8,128)S(1)}) custom-call(bf16[640,384]{1,0:T(8,128)(2,1)S(1)} %copy-done.34, bf16[640,256]{1,0:T(8,128)(2,1)S(1)} %convolution_convert_fusion.7.g_ref, f32[640,128]{1,0:T(8,128)S(1)} %broadcast_in_dim.106.bias_ref), custom_call_target="tpu_custom_call" | custom-call | flops 6920999936 | bytes 1024 | tf_op jit(solution)/shard_map/attn_bwd/pallas_call | solution.py:131
  235.3 2.1 convolution_convert_fusion.2
  237.9 1.7 convolution_convert_fusion.1
  246.1 4.5 %middle_back.3 = (bf16[640,1024]{1,0:T(8,128)(2,1)S(1)}, f32[160,1024]{1,0:T(8,128)S(1)}, f32[8,1024]{1,0:T(8,128)S(1)}) custom-call(f32[640,1024]{1,0:T(8,128)S(1)} %copy-done.7, bf16[320,1024]{1,0:T(8,128)(2,1)S(1)} %add_convert_fusion.3.a_ref, bf16[320,1024]{1,0:T(8,128)(2,1)S(1)} %collective-permute-done.40.b_ref, bf16[640,1024]{1,0:T(8,128)(2,1)S(1)} %copy-done.28, ...), custom_call_target="tpu_custom_call" | custom-call | flops 4614000128 | bytes 1024 | tf_op jit(solution)/shard_map/middle_back/pallas_call | solution.py:281
  251.9 6.0 %attn_bwd.7 = (bf16[640,384]{1,0:T(8,128)(2,1)S(1)}, f32[8,128]{1,0:T(8,128)S(1)}) custom-call(bf16[640,384]{1,0:T(8,128)(2,1)S(1)} %copy-done.32, bf16[640,256]{1,0:T(8,128)(2,1)S(1)} %convolution_convert_fusion.6.g_ref, f32[640,128]{1,0:T(8,128)S(1)} %broadcast_in_dim.108.bias_ref), custom_call_target="tpu_custom_call" | custom-call | flops 6920999936 | bytes 1024 | tf_op jit(solution)/shard_map/attn_bwd/pallas_call | solution.py:131
  258.0 6.0 %attn_bwd.6 = (bf16[640,384]{1,0:T(8,128)(2,1)S(1)}, f32[8,128]{1,0:T(8,128)S(1)}) custom-call(bf16[640,384]{1,0:T(8,128)(2,1)S(1)} %copy-done.30, bf16[640,256]{1,0:T(8,128)(2,1)S(1)} %convolution_convert_fusion.6.g_ref, f32[640,128]{1,0:T(8,128)S(1)} %broadcast_in_dim.108.bias_ref), custom_call_target="tpu_custom_call" | custom-call | flops 6920999936 | bytes 1024 | tf_op jit(solution)/shard_map/attn_bwd/pallas_call | solution.py:131
  264.0 2.8 fusion.10.refs_3_
  270.2 1.8 fusion.4.refs_2_
  278.9 7.9 %collective-permute-done.62 = bf16[4,32,1024]{2,1,0:T(8,128)(2,1)S(1)} collective-permute-done((bf16[4,32,1024]{2,1,0:T(8,128)(2,1)S(1)}, bf16[4,32,1024]{2,1,0:T(8,128)(2,1)S(1)}, u32[]{:S(2)}, u32[]{:S(2)}) %collective-permute-start.62) | collective-permute-done | bytes 262176 | tf_op jit(solution)/shard_map/ppermute | solution.py:496
  287.2 1.8 collective-permute-start.63
  294.3 4.6 %collective-permute-done.50 = bf16[4,128,384]{2,1,0:T(8,128)(2,1)S(1)} collective-permute-done((bf16[4,128,384]{2,1,0:T(8,128)(2,1)S(1)}, bf16[4,128,384]{2,1,0:T(8,128)(2,1)S(1)}, u32[]{:S(2)}, u32[]{:S(2)}) %collective-permute-start.50) | collective-permute-done | bytes 393248 | tf_op jit(solution)/shard_map/ppermute | solution.py:496
  300.5 2.1 collective-permute-start.64
  302.7 2.0 collective-permute-done.51
  304.8 2.6 collective-permute-start.52
  312.0 2.6 collective-permute-start.57
  317.9 3.5 collective-permute-start.54
  323.1 2.3 collective-permute-done.46
  325.4 3.4 collective-permute-start.47
  334.3 2.2 collective-permute-done.58
  337.2 10.7 %collective-permute-done.66.refs_1_ = bf16[288,1024]{1,0:T(8,128)(2,1)S(1)} collective-permute-done((bf16[288,1024]{1,0:T(8,128)(2,1)S(1)}, bf16[288,1024]{1,0:T(8,128)(2,1)S(1)}, u32[]{:S(2)}, u32[]{:S(2)}) %collective-permute-start.66) | collective-permute-done | bytes 589856 | tf_op jit(solution)/shard_map/ppermute | solution.py:496
  351.7 2.6 place_rest.1
  (370 shorter events, 91.3 us)
Async XLA Ops:
  7.2 324.7 %reduce-scatter.2.cloned.1.call-start = ((), (), s32[]{:S(2)}) async-start(), calls=%async_computation.1 | async-start | bytes 4718592 | tf_op jit(solution)/shard_map/reduce_scatter | solution.py:655
  9.6 59.0 %collective-permute-start = (bf16[2,160,1024]{2,1,0:T(8,128)(2,1)S(1)}, bf16[2,160,1024]{2,1,0:T(8,128)(2,1)}, u32[]{:S(2)}, u32[]{:S(2)}) collective-permute-start(bf16[2,160,1024]{2,1,0:T(8,128)(2,1)S(1)} %maximum_maximum_fusion.refs_0_.x_ref), channel_id=1, source_target_pairs={{0,2},{1,3},{2,0},{3,1},{4,6},{5,7},{6,4},{7,5},{8,10},{9,11},{10,... | collective-permute-start | bytes 1966088 | tf_op jit(solution)/shard_map/ppermute | solution.py:496
  12.6 77.0 %collective-permute-start.1 = (bf16[2,160,1024]{2,1,0:T(8,128)(2,1)S(1)}, bf16[2,160,1024]{2,1,0:T(8,128)(2,1)}, u32[]{:S(2)}, u32[]{:S(2)}) collective-permute-start(bf16[2,160,1024]{2,1,0:T(8,128)(2,1)S(1)} %maximum_maximum_fusion.refs_0_.x_ref), channel_id=1, source_target_pairs={{0,1},{1,0},{2,3},{3,2},{4,5},{5,4},{6,7},{7,6},{8,9},{9,8},{10,11... | collective-permute-start | bytes 1966088 | tf_op jit(solution)/shard_map/ppermute | solution.py:496
  13.7 16.9 %collective-permute-start.6 = (bf16[1,128,384]{2,1,0:T(8,128)(2,1)S(1)}, bf16[1,128,384]{2,1,0:T(8,128)(2,1)S(1)}, u32[]{:S(2)}, u32[]{:S(2)}) collective-permute-start(bf16[1,128,384]{2,1,0:T(8,128)(2,1)S(1)} %copy.70.a_ref), channel_id=1, source_target_pairs={{0,16},{1,17},{2,18},{3,19},{4,20},{5,21},{6,22},{7,23},{8,24},{9,... | collective-permute-start | bytes 294920 | tf_op jit(solution)/shard_map/ppermute | solution.py:496
  16.5 17.9 %collective-permute-start.9 = (bf16[1,128,384]{2,1,0:T(8,128)(2,1)S(1)}, bf16[1,128,384]{2,1,0:T(8,128)(2,1)S(1)}, u32[]{:S(2)}, u32[]{:S(2)}) collective-permute-start(bf16[1,128,384]{2,1,0:T(8,128)(2,1)S(1)} %copy.72.a_ref), channel_id=1, source_target_pairs={{0,16},{1,17},{2,18},{3,19},{4,20},{5,21},{6,22},{7,23},{8,24},{9,... | collective-permute-start | bytes 294920 | tf_op jit(solution)/shard_map/ppermute | solution.py:496
  17.0 12.0 %collective-permute-start.3 = (bf16[1,12,128]{2,1,0:T(8,128)(2,1)S(1)}, bf16[1,12,128]{2,1,0:T(8,128)(2,1)S(1)}, u32[]{:S(2)}, u32[]{:S(2)}) collective-permute-start(bf16[1,12,128]{2,1,0:T(8,128)(2,1)S(1)} %bitcast.295), channel_id=1, source_target_pairs={{0,16},{1,17},{2,18},{3,19},{4,20},{5,21},{6,22},{7,23},{8,24},{9,... | collective-permute-start | bytes 9224 | tf_op jit(solution)/shard_map/ppermute | solution.py:496
  30.7 4.2 %collective-permute-start.12 = (bf16[32,1024]{1,0:T(8,128)(2,1)S(1)}, bf16[32,1024]{1,0:T(8,128)(2,1)S(1)}, u32[]{:S(2)}, u32[]{:S(2)}) collective-permute-start(bf16[32,1024]{1,0:T(8,128)(2,1)S(1)} %constant_dynamic-slice_fusion.8), channel_id=1, source_target_pairs={{0,0},{1,4},{2,8},{3,12},{4,16},{5,20},{6,24},{7,28},{8,1},{9,5},{... | collective-permute-start | bytes 196616 | tf_op jit(solution)/shard_map/ppermute | solution.py:584
  32.7 13.4 %collective-permute-start.7 = (bf16[2,128,384]{2,1,0:T(8,128)(2,1)S(1)}, bf16[2,128,384]{2,1,0:T(8,128)(2,1)S(1)}, u32[]{:S(2)}, u32[]{:S(2)}) collective-permute-start(bf16[2,128,384]{2,1,0:T(8,128)(2,1)S(1)} %bitcast.247), channel_id=1, source_target_pairs={{0,8},{1,9},{2,10},{3,11},{4,12},{5,13},{6,14},{7,15},{8,0},{9,1},... | collective-permute-start | bytes 589832 | tf_op jit(solution)/shard_map/ppermute | solution.py:496
  34.4 14.6 %collective-permute-start.10 = (bf16[2,128,384]{2,1,0:T(8,128)(2,1)S(1)}, bf16[2,128,384]{2,1,0:T(8,128)(2,1)S(1)}, u32[]{:S(2)}, u32[]{:S(2)}) collective-permute-start(bf16[2,128,384]{2,1,0:T(8,128)(2,1)S(1)} %bitcast.249), channel_id=1, source_target_pairs={{0,8},{1,9},{2,10},{3,11},{4,12},{5,13},{6,14},{7,15},{8,0},{9,1},... | collective-permute-start | bytes 589832 | tf_op jit(solution)/shard_map/ppermute | solution.py:496
  34.9 9.8 %collective-permute-start.13 = (bf16[1,32,1024]{2,1,0:T(8,128)(2,1)S(1)}, bf16[1,32,1024]{2,1,0:T(8,128)(2,1)S(1)}, u32[]{:S(2)}, u32[]{:S(2)}) collective-permute-start(bf16[1,32,1024]{2,1,0:T(8,128)(2,1)S(1)} %bitcast.253), channel_id=1, source_target_pairs={{0,16},{1,17},{2,18},{3,19},{4,20},{5,21},{6,22},{7,23},{8,24},{9,... | collective-permute-start | bytes 196616 | tf_op jit(solution)/shard_map/ppermute | solution.py:496
  44.7 9.9 %collective-permute-start.5 = (bf16[4,12,128]{2,0,1:T(4,128)(2,1)S(1)}, bf16[4,12,128]{2,0,1:T(4,128)(2,1)S(1)}, u32[]{:S(2)}, u32[]{:S(2)}) collective-permute-start(bf16[4,12,128]{2,0,1:T(4,128)(2,1)S(1)} %bitcast.290), channel_id=1, source_target_pairs={{0,4},{1,5},{2,6},{3,7},{4,0},{5,1},{6,2},{7,3},{8,12},{9,13},{10,... | collective-permute-start | bytes 36872 | tf_op jit(solution)/shard_map/ppermute | solution.py:496
  46.2 6.6 %collective-permute-start.14 = (bf16[2,32,1024]{2,1,0:T(8,128)(2,1)S(1)}, bf16[2,32,1024]{2,1,0:T(8,128)(2,1)S(1)}, u32[]{:S(2)}, u32[]{:S(2)}) collective-permute-start(bf16[2,32,1024]{2,1,0:T(8,128)(2,1)S(1)} %bitcast.251), channel_id=1, source_target_pairs={{0,8},{1,9},{2,10},{3,11},{4,12},{5,13},{6,14},{7,15},{8,0},{9,1},... | collective-permute-start | bytes 393224 | tf_op jit(solution)/shard_map/ppermute | solution.py:496
  49.0 19.9 %collective-permute-start.8 = (bf16[4,128,384]{2,1,0:T(8,128)(2,1)S(1)}, bf16[4,128,384]{2,1,0:T(8,128)(2,1)S(1)}, u32[]{:S(2)}, u32[]{:S(2)}) collective-permute-start(bf16[4,128,384]{2,1,0:T(8,128)(2,1)S(1)} %bitcast.241), channel_id=1, source_target_pairs={{0,4},{1,5},{2,6},{3,7},{4,0},{5,1},{6,2},{7,3},{8,12},{9,13},{10,... | collective-permute-start | bytes 1179656 | tf_op jit(solution)/shard_map/ppermute | solution.py:496
  52.7 14.3 %collective-permute-start.22 = (bf16[1,128,1024]{2,1,0:T(8,128)(2,1)S(1)}, bf16[1,128,1024]{2,1,0:T(8,128)(2,1)S(1)}, u32[]{:S(2)}, u32[]{:S(2)}) collective-permute-start(bf16[1,128,1024]{2,1,0:T(8,128)(2,1)S(1)} %bitcast.235), channel_id=1, source_target_pairs={{0,16},{1,17},{2,18},{3,19},{4,20},{5,21},{6,22},{7,23},{8,24},{9,... | collective-permute-start | bytes 786440 | tf_op jit(solution)/shard_map/ppermute | solution.py:496
  54.6 13.9 %collective-permute-start.15 = (bf16[4,32,1024]{2,1,0:T(8,128)(2,1)S(1)}, bf16[4,32,1024]{2,1,0:T(8,128)(2,1)S(1)}, u32[]{:S(2)}, u32[]{:S(2)}) collective-permute-start(bf16[4,32,1024]{2,1,0:T(8,128)(2,1)S(1)} %bitcast.245), channel_id=1, source_target_pairs={{0,4},{1,5},{2,6},{3,7},{4,0},{5,1},{6,2},{7,3},{8,12},{9,13},{10,... | collective-permute-start | bytes 786440 | tf_op jit(solution)/shard_map/ppermute | solution.py:496
  67.1 10.1 %collective-permute-start.11 = (bf16[4,128,384]{2,1,0:T(8,128)(2,1)S(1)}, bf16[4,128,384]{2,1,0:T(8,128)(2,1)S(1)}, u32[]{:S(2)}, u32[]{:S(2)}) collective-permute-start(bf16[4,128,384]{2,1,0:T(8,128)(2,1)S(1)} %bitcast.243), channel_id=1, source_target_pairs={{0,4},{1,5},{2,6},{3,7},{4,0},{5,1},{6,2},{7,3},{8,12},{9,13},{10,... | collective-permute-start | bytes 1179656 | tf_op jit(solution)/shard_map/ppermute | solution.py:496
  68.5 18.3 %collective-permute-start.23 = (bf16[2,128,1024]{2,1,0:T(8,128)(2,1)S(1)}, bf16[2,128,1024]{2,1,0:T(8,128)(2,1)S(1)}, u32[]{:S(2)}, u32[]{:S(2)}) collective-permute-start(bf16[2,128,1024]{2,1,0:T(8,128)(2,1)S(1)} %bitcast.239), channel_id=1, source_target_pairs={{0,8},{1,9},{2,10},{3,11},{4,12},{5,13},{6,14},{7,15},{8,0},{9,1},... | collective-permute-start | bytes 1572872 | tf_op jit(solution)/shard_map/ppermute | solution.py:496
  68.6 21.6 %collective-permute-start.2 = (bf16[2,160,1024]{2,1,0:T(8,128)(2,1)}, bf16[2,160,1024]{2,1,0:T(8,128)(2,1)S(1)}, u32[]{:S(2)}, u32[]{:S(2)}) collective-permute-start(bf16[2,160,1024]{2,1,0:T(8,128)(2,1)} %collective-permute-done.refs_1_), channel_id=1, source_target_pairs={{0,1},{1,0},{2,3},{3,2},{4,5},{5,4},{6,7},{7,6},{8,9},{9,8},{10,11... | collective-permute-start | bytes 1966088 | tf_op jit(solution)/shard_map/ppermute | solution.py:496
  68.9 15.7 %collective-permute-start.25 = (bf16[1,128,1024]{2,1,0:T(8,128)(2,1)S(1)}, bf16[1,128,1024]{2,1,0:T(8,128)(2,1)S(1)}, u32[]{:S(2)}, u32[]{:S(2)}) collective-permute-start(bf16[1,128,1024]{2,1,0:T(8,128)(2,1)S(1)} %bitcast.233), channel_id=1, source_target_pairs={{0,16},{1,17},{2,18},{3,19},{4,20},{5,21},{6,22},{7,23},{8,24},{9,... | collective-permute-start | bytes 786440 | tf_op jit(solution)/shard_map/ppermute | solution.py:496
  77.2 34.4 %collective-permute-start.28 = (bf16[2,160,1024]{2,1,0:T(8,128)(2,1)}, bf16[2,160,1024]{2,1,0:T(8,128)(2,1)}, u32[]{:S(2)}, u32[]{:S(2)}) collective-permute-start(bf16[2,160,1024]{2,1,0:T(8,128)(2,1)} %pad.9.refs_0_), channel_id=1, source_target_pairs={{0,2},{1,3},{2,0},{3,1},{4,6},{5,7},{6,4},{7,5},{8,10},{9,11},{10,... | collective-permute-start | bytes 1966088 | tf_op jit(solution)/shard_map/ppermute | solution.py:496
  84.7 41.0 %collective-permute-start.29 = (bf16[2,160,1024]{2,1,0:T(8,128)(2,1)}, bf16[2,160,1024]{2,1,0:T(8,128)(2,1)}, u32[]{:S(2)}, u32[]{:S(2)}) collective-permute-start(bf16[2,160,1024]{2,1,0:T(8,128)(2,1)} %pad.9.refs_0_), channel_id=1, source_target_pairs={{0,1},{1,0},{2,3},{3,2},{4,5},{5,4},{6,7},{7,6},{8,9},{9,8},{10,11... | collective-permute-start | bytes 1966088 | tf_op jit(solution)/shard_map/ppermute | solution.py:496
  86.9 37.2 %collective-permute-start.26 = (bf16[2,128,1024]{2,1,0:T(8,128)(2,1)}, bf16[2,128,1024]{2,1,0:T(8,128)(2,1)}, u32[]{:S(2)}, u32[]{:S(2)}) collective-permute-start(bf16[2,128,1024]{2,1,0:T(8,128)(2,1)} %bitcast.37.a_ref), channel_id=1, source_target_pairs={{0,8},{1,9},{2,10},{3,11},{4,12},{5,13},{6,14},{7,15},{8,0},{9,1},... | collective-permute-start | bytes 1572872 | tf_op jit(solution)/shard_map/ppermute | solution.py:496
  89.6 39.7 %collective-permute-start.24 = (bf16[4,128,1024]{2,1,0:T(8,128)(2,1)}, bf16[4,128,1024]{2,1,0:T(8,128)(2,1)}, u32[]{:S(2)}, u32[]{:S(2)}) collective-permute-start(bf16[4,128,1024]{2,1,0:T(8,128)(2,1)} %bitcast.33.a_ref), channel_id=1, source_target_pairs={{0,4},{1,5},{2,6},{3,7},{4,0},{5,1},{6,2},{7,3},{8,12},{9,13},{10,... | collective-permute-start | bytes 3145736 | tf_op jit(solution)/shard_map/ppermute | solution.py:496
  110.7 6.5 %collective-permute-start.16 = (bf16[320,1024]{1,0:T(8,128)(2,1)S(1)}, bf16[320,1024]{1,0:T(8,128)(2,1)S(1)}, u32[]{:S(2)}, u32[]{:S(2)}) collective-permute-start(bf16[320,1024]{1,0:T(8,128)(2,1)S(1)} %convolution_convert_fusion.5), channel_id=1, source_target_pairs={{0,1},{1,0},{2,3},{3,2},{4,5},{5,4},{6,7},{7,6},{8,9},{9,8},{10,11... | collective-permute-start | bytes 1966088 | tf_op jit(solution)/shard_map/ppermute | solution.py:496
  111.6 15.8 %collective-permute-start.30 = (bf16[2,160,1024]{2,1,0:T(8,128)(2,1)}, bf16[2,160,1024]{2,1,0:T(8,128)(2,1)}, u32[]{:S(2)}, u32[]{:S(2)}) collective-permute-start(bf16[2,160,1024]{2,1,0:T(8,128)(2,1)} %collective-permute-done.28.refs_1_), channel_id=1, source_target_pairs={{0,1},{1,0},{2,3},{3,2},{4,5},{5,4},{6,7},{7,6},{8,9},{9,8},{10,11... | collective-permute-start | bytes 1966088 | tf_op jit(solution)/shard_map/ppermute | solution.py:496
  124.0 8.0 %collective-permute-start.19 = (bf16[320,1024]{1,0:T(8,128)(2,1)}, bf16[320,1024]{1,0:T(8,128)(2,1)}, u32[]{:S(2)}, u32[]{:S(2)}) collective-permute-start(bf16[320,1024]{1,0:T(8,128)(2,1)} %convolution_convert_fusion.4), channel_id=1, source_target_pairs={{0,1},{1,0},{2,3},{3,2},{4,5},{5,4},{6,7},{7,6},{8,9},{9,8},{10,11... | collective-permute-start | bytes 1966088 | tf_op jit(solution)/shard_map/ppermute | solution.py:496
  124.1 17.8 %collective-permute-start.17 = (bf16[320,1024]{1,0:T(8,128)(2,1)}, bf16[320,1024]{1,0:T(8,128)(2,1)S(1)}, u32[]{:S(2)}, u32[]{:S(2)}) collective-permute-start(bf16[320,1024]{1,0:T(8,128)(2,1)} %fusion.6), channel_id=1, source_target_pairs={{0,2},{1,3},{2,0},{3,1},{4,6},{5,7},{6,4},{7,5},{8,10},{9,11},{10,... | collective-permute-start | bytes 1966088 | tf_op jit(solution)/shard_map/ppermute | solution.py:496
  125.6 25.4 %collective-permute-start.27 = (bf16[4,128,1024]{2,1,0:T(8,128)(2,1)S(1)}, bf16[4,128,1024]{2,1,0:T(8,128)(2,1)S(1)}, u32[]{:S(2)}, u32[]{:S(2)}) collective-permute-start(bf16[4,128,1024]{2,1,0:T(8,128)(2,1)S(1)} %bitcast.237), channel_id=1, source_target_pairs={{0,4},{1,5},{2,6},{3,7},{4,0},{5,1},{6,2},{7,3},{8,12},{9,13},{10,... | collective-permute-start | bytes 3145736 | tf_op jit(solution)/shard_map/ppermute | solution.py:496
  133.6 22.0 %collective-permute-start.20 = (bf16[320,1024]{1,0:T(8,128)(2,1)S(1)}, bf16[320,1024]{1,0:T(8,128)(2,1)S(1)}, u32[]{:S(2)}, u32[]{:S(2)}) collective-permute-start(bf16[320,1024]{1,0:T(8,128)(2,1)S(1)} %fusion.7), channel_id=1, source_target_pairs={{0,2},{1,3},{2,0},{3,1},{4,6},{5,7},{6,4},{7,5},{8,10},{9,11},{10,... | collective-permute-start | bytes 1966088 | tf_op jit(solution)/shard_map/ppermute | solution.py:496
  142.2 13.7 %collective-permute-start.18 = (bf16[320,1024]{1,0:T(8,128)(2,1)S(1)}, bf16[320,1024]{1,0:T(8,128)(2,1)S(1)}, u32[]{:S(2)}, u32[]{:S(2)}) collective-permute-start(bf16[320,1024]{1,0:T(8,128)(2,1)S(1)} %add_convert_fusion.5.refs_4_), channel_id=1, source_target_pairs={{0,1},{1,0},{2,3},{3,2},{4,5},{5,4},{6,7},{7,6},{8,9},{9,8},{10,11... | collective-permute-start | bytes 1966088 | tf_op jit(solution)/shard_map/ppermute | solution.py:496
  155.8 11.0 %collective-permute-start.21 = (bf16[320,1024]{1,0:T(8,128)(2,1)S(1)}, bf16[320,1024]{1,0:T(8,128)(2,1)S(1)}, u32[]{:S(2)}, u32[]{:S(2)}) collective-permute-start(bf16[320,1024]{1,0:T(8,128)(2,1)S(1)} %add_convert_fusion.4.refs_4_), channel_id=1, source_target_pairs={{0,1},{1,0},{2,3},{3,2},{4,5},{5,4},{6,7},{7,6},{8,9},{9,8},{10,11... | collective-permute-start | bytes 1966088 | tf_op jit(solution)/shard_map/ppermute | solution.py:496
  166.8 13.6 %collective-permute-start.37 = (bf16[320,1024]{1,0:T(8,128)(2,1)S(1)}, bf16[320,1024]{1,0:T(8,128)(2,1)S(1)}, u32[]{:S(2)}, u32[]{:S(2)}) collective-permute-start(bf16[320,1024]{1,0:T(8,128)(2,1)S(1)} %convolution_convert_fusion), channel_id=1, source_target_pairs={{0,1},{1,0},{2,3},{3,2},{4,5},{5,4},{6,7},{7,6},{8,9},{9,8},{10,11... | collective-permute-start | bytes 1966088 | tf_op jit(solution)/shard_map/ppermute | solution.py:496
  178.0 5.7 %collective-permute-start.31 = (bf16[320,1024]{1,0:T(8,128)(2,1)S(1)}, bf16[320,1024]{1,0:T(8,128)(2,1)S(1)}, u32[]{:S(2)}, u32[]{:S(2)}) collective-permute-start(bf16[320,1024]{1,0:T(8,128)(2,1)S(1)} %convolution_convert_fusion.3), channel_id=1, source_target_pairs={{0,1},{1,0},{2,3},{3,2},{4,5},{5,4},{6,7},{7,6},{8,9},{9,8},{10,11... | collective-permute-start | bytes 1966088 | tf_op jit(solution)/shard_map/ppermute | solution.py:496
  181.3 17.7 %collective-permute-start.38 = (bf16[320,1024]{1,0:T(8,128)(2,1)S(1)}, bf16[320,1024]{1,0:T(8,128)(2,1)S(1)}, u32[]{:S(2)}, u32[]{:S(2)}) collective-permute-start(bf16[320,1024]{1,0:T(8,128)(2,1)S(1)} %fusion.11), channel_id=1, source_target_pairs={{0,2},{1,3},{2,0},{3,1},{4,6},{5,7},{6,4},{7,5},{8,10},{9,11},{10,... | collective-permute-start | bytes 1966088 | tf_op jit(solution)/shard_map/ppermute | solution.py:496
  185.4 26.7 %collective-permute-start.32 = (bf16[320,1024]{1,0:T(8,128)(2,1)}, bf16[320,1024]{1,0:T(8,128)(2,1)}, u32[]{:S(2)}, u32[]{:S(2)}) collective-permute-start(bf16[320,1024]{1,0:T(8,128)(2,1)} %fusion.9), channel_id=1, source_target_pairs={{0,2},{1,3},{2,0},{3,1},{4,6},{5,7},{6,4},{7,5},{8,10},{9,11},{10,... | collective-permute-start | bytes 1966088 | tf_op jit(solution)/shard_map/ppermute | solution.py:496
  200.1 14.8 %collective-permute-start.39 = (bf16[320,1024]{1,0:T(8,128)(2,1)}, bf16[320,1024]{1,0:T(8,128)(2,1)}, u32[]{:S(2)}, u32[]{:S(2)}) collective-permute-start(bf16[320,1024]{1,0:T(8,128)(2,1)} %add_convert_fusion.2.a_ref), channel_id=1, source_target_pairs={{0,1},{1,0},{2,3},{3,2},{4,5},{5,4},{6,7},{7,6},{8,9},{9,8},{10,11... | collective-permute-start | bytes 1966088 | tf_op jit(solution)/shard_map/ppermute | solution.py:496
  214.8 31.1 %collective-permute-start.40 = (bf16[320,1024]{1,0:T(8,128)(2,1)S(1)}, bf16[320,1024]{1,0:T(8,128)(2,1)S(1)}, u32[]{:S(2)}, u32[]{:S(2)}) collective-permute-start(bf16[320,1024]{1,0:T(8,128)(2,1)S(1)} %add_convert_fusion.3.a_ref), channel_id=1, source_target_pairs={{0,1},{1,0},{2,3},{3,2},{4,5},{5,4},{6,7},{7,6},{8,9},{9,8},{10,11... | collective-permute-start | bytes 1966088 | tf_op jit(solution)/shard_map/ppermute | solution.py:496
  237.3 6.5 %collective-permute-start.33 = (bf16[320,1024]{1,0:T(8,128)(2,1)S(1)}, bf16[320,1024]{1,0:T(8,128)(2,1)S(1)}, u32[]{:S(2)}, u32[]{:S(2)}) collective-permute-start(bf16[320,1024]{1,0:T(8,128)(2,1)S(1)} %convolution_convert_fusion.2), channel_id=1, source_target_pairs={{0,1},{1,0},{2,3},{3,2},{4,5},{5,4},{6,7},{7,6},{8,9},{9,8},{10,11... | collective-permute-start | bytes 1966088 | tf_op jit(solution)/shard_map/ppermute | solution.py:496
  239.6 24.4 %collective-permute-start.34 = (bf16[320,1024]{1,0:T(8,128)(2,1)}, bf16[320,1024]{1,0:T(8,128)(2,1)}, u32[]{:S(2)}, u32[]{:S(2)}) collective-permute-start(bf16[320,1024]{1,0:T(8,128)(2,1)} %convolution_convert_fusion.1), channel_id=1, source_target_pairs={{0,1},{1,0},{2,3},{3,2},{4,5},{5,4},{6,7},{7,6},{8,9},{9,8},{10,11... | collective-permute-start | bytes 1966088 | tf_op jit(solution)/shard_map/ppermute | solution.py:496
  241.7 27.8 %collective-permute-start.41 = (bf16[320,1024]{1,0:T(8,128)(2,1)}, bf16[320,1024]{1,0:T(8,128)(2,1)}, u32[]{:S(2)}, u32[]{:S(2)}) collective-permute-start(bf16[320,1024]{1,0:T(8,128)(2,1)} %fusion.2), channel_id=1, source_target_pairs={{0,1},{1,0},{2,3},{3,2},{4,5},{5,4},{6,7},{7,6},{8,9},{9,8},{10,11... | collective-permute-start | bytes 1966088 | tf_op jit(solution)/shard_map/ppermute | solution.py:496
  245.5 41.7 %collective-permute-start.35 = (bf16[160,1024]{1,0:T(8,128)(2,1)}, bf16[160,1024]{1,0:T(8,128)(2,1)S(1)}, u32[]{:S(2)}, u32[]{:S(2)}) collective-permute-start(bf16[160,1024]{1,0:T(8,128)(2,1)} %slice.216), channel_id=1, source_target_pairs={{0,2},{1,3},{2,0},{3,1},{4,6},{5,7},{6,4},{7,5},{8,10},{9,11},{10,... | collective-permute-start | bytes 983048 | tf_op jit(solution)/shard_map/ppermute | solution.py:496
  266.9 22.1 %collective-permute-start.36 = (bf16[160,1024]{1,0:T(8,128)(2,1)S(1)}, bf16[160,1024]{1,0:T(8,128)(2,1)S(1)}, u32[]{:S(2)}, u32[]{:S(2)}) collective-permute-start(bf16[160,1024]{1,0:T(8,128)(2,1)S(1)} %slice.217), channel_id=1, source_target_pairs={{0,2},{1,3},{2,0},{3,1},{4,6},{5,7},{6,4},{7,5},{8,10},{9,11},{10,... | collective-permute-start | bytes 983048 | tf_op jit(solution)/shard_map/ppermute | solution.py:496
  269.5 37.9 %collective-permute-start.42 = (bf16[320,1024]{1,0:T(8,128)(2,1)S(1)}, bf16[320,1024]{1,0:T(8,128)(2,1)S(1)}, u32[]{:S(2)}, u32[]{:S(2)}) collective-permute-start(bf16[320,1024]{1,0:T(8,128)(2,1)S(1)} %fusion.3), channel_id=1, source_target_pairs={{0,1},{1,0},{2,3},{3,2},{4,5},{5,4},{6,7},{7,6},{8,9},{9,8},{10,11... | collective-permute-start | bytes 1966088 | tf_op jit(solution)/shard_map/ppermute | solution.py:496
  272.1 42.6 %collective-permute-start.43 = (bf16[160,1024]{1,0:T(8,128)(2,1)S(1)}, bf16[160,1024]{1,0:T(8,128)(2,1)S(1)}, u32[]{:S(2)}, u32[]{:S(2)}) collective-permute-start(bf16[160,1024]{1,0:T(8,128)(2,1)S(1)} %slice.222), channel_id=1, source_target_pairs={{0,2},{1,3},{2,0},{3,1},{4,6},{5,7},{6,4},{7,5},{8,10},{9,11},{10,... | collective-permute-start | bytes 983048 | tf_op jit(solution)/shard_map/ppermute | solution.py:496
  274.7 12.1 %collective-permute-start.62 = (bf16[4,32,1024]{2,1,0:T(8,128)(2,1)S(1)}, bf16[4,32,1024]{2,1,0:T(8,128)(2,1)S(1)}, u32[]{:S(2)}, u32[]{:S(2)}) collective-permute-start(bf16[4,32,1024]{2,1,0:T(8,128)(2,1)S(1)} %fusion.27), channel_id=1, source_target_pairs={{0,4},{1,5},{2,6},{3,7},{4,0},{5,1},{6,2},{7,3},{8,12},{9,13},{10,... | collective-permute-start | bytes 786440 | tf_op jit(solution)/shard_map/ppermute | solution.py:496
  286.8 12.0 %collective-permute-start.50 = (bf16[4,128,384]{2,1,0:T(8,128)(2,1)S(1)}, bf16[4,128,384]{2,1,0:T(8,128)(2,1)S(1)}, u32[]{:S(2)}, u32[]{:S(2)}) collective-permute-start(bf16[4,128,384]{2,1,0:T(8,128)(2,1)S(1)} %fusion.24), channel_id=1, source_target_pairs={{0,4},{1,5},{2,6},{3,7},{4,0},{5,1},{6,2},{7,3},{8,12},{9,13},{10,... | collective-permute-start | bytes 1179656 | tf_op jit(solution)/shard_map/ppermute | solution.py:496
  287.2 13.3 %collective-permute-start.63 = (bf16[2,32,1024]{2,1,0:T(8,128)(2,1)S(1)}, bf16[2,32,1024]{2,1,0:T(8,128)(2,1)S(1)}, u32[]{:S(2)}, u32[]{:S(2)}) collective-permute-start(bf16[2,32,1024]{2,1,0:T(8,128)(2,1)S(1)} %fusion.50), channel_id=1, source_target_pairs={{0,8},{1,9},{2,10},{3,11},{4,12},{5,13},{6,14},{7,15},{8,0},{9,1},... | collective-permute-start | bytes 393224 | tf_op jit(solution)/shard_map/ppermute | solution.py:496
  292.7 19.2 %collective-permute-start.56 = (bf16[4,128,384]{2,1,0:T(8,128)(2,1)S(1)}, bf16[4,128,384]{2,1,0:T(8,128)(2,1)S(1)}, u32[]{:S(2)}, u32[]{:S(2)}) collective-permute-start(bf16[4,128,384]{2,1,0:T(8,128)(2,1)S(1)} %fusion.25), channel_id=1, source_target_pairs={{0,4},{1,5},{2,6},{3,7},{4,0},{5,1},{6,2},{7,3},{8,12},{9,13},{10,... | collective-permute-start | bytes 1179656 | tf_op jit(solution)/shard_map/ppermute | solution.py:496
  299.0 5.7 %collective-permute-start.51 = (bf16[2,128,384]{2,1,0:T(8,128)(2,1)S(1)}, bf16[2,128,384]{2,1,0:T(8,128)(2,1)S(1)}, u32[]{:S(2)}, u32[]{:S(2)}) collective-permute-start(bf16[2,128,384]{2,1,0:T(8,128)(2,1)S(1)} %fusion.40), channel_id=1, source_target_pairs={{0,8},{1,9},{2,10},{3,11},{4,12},{5,13},{6,14},{7,15},{8,0},{9,1},... | collective-permute-start | bytes 589832 | tf_op jit(solution)/shard_map/ppermute | solution.py:496
  300.5 16.7 %collective-permute-start.64 = (bf16[1,32,1024]{2,1,0:T(8,128)(2,1)S(1)}, bf16[1,32,1024]{2,1,0:T(8,128)(2,1)S(1)}, u32[]{:S(2)}, u32[]{:S(2)}) collective-permute-start(bf16[1,32,1024]{2,1,0:T(8,128)(2,1)S(1)} %dynamic-slice_convert_fusion.2), channel_id=1, source_target_pairs={{0,16},{1,17},{2,18},{3,19},{4,20},{5,21},{6,22},{7,23},{8,24},{9,... | collective-permute-start | bytes 196616 | tf_op jit(solution)/shard_map/ppermute | solution.py:496
  304.8 5.6 %collective-permute-start.52 = (bf16[1,128,384]{2,1,0:T(8,128)(2,1)S(1)}, bf16[1,128,384]{2,1,0:T(8,128)(2,1)S(1)}, u32[]{:S(2)}, u32[]{:S(2)}) collective-permute-start(bf16[1,128,384]{2,1,0:T(8,128)(2,1)S(1)} %dynamic-slice_convert_fusion.1), channel_id=1, source_target_pairs={{0,16},{1,17},{2,18},{3,19},{4,20},{5,21},{6,22},{7,23},{8,24},{9,... | collective-permute-start | bytes 294920 | tf_op jit(solution)/shard_map/ppermute | solution.py:496
  308.0 7.6 %collective-permute-start.44 = (bf16[160,1024]{1,0:T(8,128)(2,1)S(1)}, bf16[160,1024]{1,0:T(8,128)(2,1)S(1)}, u32[]{:S(2)}, u32[]{:S(2)}) collective-permute-start(bf16[160,1024]{1,0:T(8,128)(2,1)S(1)} %slice.223), channel_id=1, source_target_pairs={{0,2},{1,3},{2,0},{3,1},{4,6},{5,7},{6,4},{7,5},{8,10},{9,11},{10,... | collective-permute-start | bytes 983048 | tf_op jit(solution)/shard_map/ppermute | solution.py:496
  310.4 11.0 %collective-permute-start.53 = (bf16[128,384]{1,0:T(8,128)(2,1)S(1)}, bf16[128,384]{1,0:T(8,128)(2,1)S(1)}, u32[]{:S(2)}, u32[]{:S(2)}) collective-permute-start(bf16[128,384]{1,0:T(8,128)(2,1)S(1)} %fusion.51.refs_0_), channel_id=1, source_target_pairs={{0,2},{1,3},{2,0},{3,1},{4,6},{5,7},{6,4},{7,5},{8,10},{9,11},{10,... | collective-permute-start | bytes 294920 | tf_op jit(solution)/shard_map/ppermute | solution.py:496
  312.0 11.0 %collective-permute-start.57 = (bf16[2,128,384]{2,1,0:T(8,128)(2,1)S(1)}, bf16[2,128,384]{2,1,0:T(8,128)(2,1)S(1)}, u32[]{:S(2)}, u32[]{:S(2)}) collective-permute-start(bf16[2,128,384]{2,1,0:T(8,128)(2,1)S(1)} %fusion.41), channel_id=1, source_target_pairs={{0,8},{1,9},{2,10},{3,11},{4,12},{5,13},{6,14},{7,15},{8,0},{9,1},... | collective-permute-start | bytes 589832 | tf_op jit(solution)/shard_map/ppermute | solution.py:496
  317.0 4.5 %collective-permute-start.45 = (f32[4,12,128]{2,0,1:T(4,128)S(1)}, f32[4,12,128]{2,0,1:T(4,128)S(1)}, u32[]{:S(2)}, u32[]{:S(2)}) collective-permute-start(f32[4,12,128]{2,0,1:T(4,128)S(1)} %bitcast.294), channel_id=1, source_target_pairs={{0,4},{1,5},{2,6},{3,7},{4,0},{5,1},{6,2},{7,3},{8,12},{9,13},{10,... | collective-permute-start | bytes 73736 | tf_op jit(solution)/shard_map/ppermute | solution.py:496
  317.2 15.7 %collective-permute-start.65 = (bf16[32,1024]{1,0:T(8,128)(2,1)S(1)}, bf16[32,1024]{1,0:T(8,128)(2,1)S(1)}, u32[]{:S(2)}, u32[]{:S(2)}) collective-permute-start(bf16[32,1024]{1,0:T(8,128)(2,1)S(1)} %fusion.53), channel_id=1, source_target_pairs={{0,0},{4,1},{8,2},{12,3},{16,4},{20,5},{24,6},{28,7},{1,8},{5,9},{... | collective-permute-start | bytes 196616 | tf_op jit(solution)/shard_map/ppermute | solution.py:678
  317.9 30.6 %collective-permute-start.54 = (bf16[128,384]{1,0:T(8,128)(2,1)S(1)}, bf16[128,384]{1,0:T(8,128)(2,1)S(1)}, u32[]{:S(2)}, u32[]{:S(2)}) collective-permute-start(bf16[128,384]{1,0:T(8,128)(2,1)S(1)} %fusion.51.refs_0_), channel_id=1, source_target_pairs={{0,1},{1,0},{2,3},{3,2},{4,5},{5,4},{6,7},{7,6},{8,9},{9,8},{10,11... | collective-permute-start | bytes 294920 | tf_op jit(solution)/shard_map/ppermute | solution.py:496
  321.4 28.2 %collective-permute-start.55 = (bf16[128,384]{1,0:T(8,128)(2,1)S(1)}, bf16[128,384]{1,0:T(8,128)(2,1)S(1)}, u32[]{:S(2)}, u32[]{:S(2)}) collective-permute-start(bf16[128,384]{1,0:T(8,128)(2,1)S(1)} %collective-permute-done.53.refs_1_), channel_id=1, source_target_pairs={{0,1},{1,0},{2,3},{3,2},{4,5},{5,4},{6,7},{7,6},{8,9},{9,8},{10,11... | collective-permute-start | bytes 294920 | tf_op jit(solution)/shard_map/ppermute | solution.py:496
  321.5 3.9 %collective-permute-start.46 = (f32[2,12,128]{2,0,1:T(2,128)S(1)}, f32[2,12,128]{2,0,1:T(2,128)S(1)}, u32[]{:S(2)}, u32[]{:S(2)}) collective-permute-start(f32[2,12,128]{2,0,1:T(2,128)S(1)} %bitcast.296), channel_id=1, source_target_pairs={{0,8},{1,9},{2,10},{3,11},{4,12},{5,13},{6,14},{7,15},{8,0},{9,1},... | collective-permute-start | bytes 36872 | tf_op jit(solution)/shard_map/ppermute | solution.py:496
  325.4 5.1 %collective-permute-start.47 = (f32[1,12,128]{2,0,1:T(1,128)S(1)}, f32[1,12,128]{2,0,1:T(1,128)S(1)}, u32[]{:S(2)}, u32[]{:S(2)}) collective-permute-start(f32[1,12,128]{2,0,1:T(1,128)S(1)} %constant_dynamic-slice_fusion), channel_id=1, source_target_pairs={{0,16},{1,17},{2,18},{3,19},{4,20},{5,21},{6,22},{7,23},{8,24},{9,... | collective-permute-start | bytes 18440 | tf_op jit(solution)/shard_map/ppermute | solution.py:496
  328.9 7.6 %collective-permute-start.58 = (bf16[1,128,384]{2,1,0:T(8,128)(2,1)S(1)}, bf16[1,128,384]{2,1,0:T(8,128)(2,1)S(1)}, u32[]{:S(2)}, u32[]{:S(2)}) collective-permute-start(bf16[1,128,384]{2,1,0:T(8,128)(2,1)S(1)} %dynamic-slice_convert_fusion), channel_id=1, source_target_pairs={{0,16},{1,17},{2,18},{3,19},{4,20},{5,21},{6,22},{7,23},{8,24},{9,... | collective-permute-start | bytes 294920 | tf_op jit(solution)/shard_map/ppermute | solution.py:496
  333.0 14.9 %collective-permute-start.66 = (bf16[288,1024]{1,0:T(8,128)(2,1)S(1)}, bf16[288,1024]{1,0:T(8,128)(2,1)S(1)}, u32[]{:S(2)}, u32[]{:S(2)}) collective-permute-start(bf16[288,1024]{1,0:T(8,128)(2,1)S(1)} %pad_maximum_fusion.1.refs_0_), channel_id=1, source_target_pairs={{0,2},{1,3},{2,0},{3,1},{4,6},{5,7},{6,4},{7,5},{8,10},{9,11},{10,... | collective-permute-start | bytes 1769480 | tf_op jit(solution)/shard_map/ppermute | solution.py:496
  336.5 12.5 %collective-permute-start.59 = (bf16[128,384]{1,0:T(8,128)(2,1)S(1)}, bf16[128,384]{1,0:T(8,128)(2,1)S(1)}, u32[]{:S(2)}, u32[]{:S(2)}) collective-permute-start(bf16[128,384]{1,0:T(8,128)(2,1)S(1)} %fusion.52.refs_4_), channel_id=1, source_target_pairs={{0,2},{1,3},{2,0},{3,1},{4,6},{5,7},{6,4},{7,5},{8,10},{9,11},{10,... | collective-permute-start | bytes 294920 | tf_op jit(solution)/shard_map/ppermute | solution.py:496
  337.2 14.5 %collective-permute-start.67 = (bf16[288,1024]{1,0:T(8,128)(2,1)S(1)}, bf16[288,1024]{1,0:T(8,128)(2,1)S(1)}, u32[]{:S(2)}, u32[]{:S(2)}) collective-permute-start(bf16[288,1024]{1,0:T(8,128)(2,1)S(1)} %pad_maximum_fusion.1.refs_0_), channel_id=1, source_target_pairs={{0,1},{1,0},{2,3},{3,2},{4,5},{5,4},{6,7},{7,6},{8,9},{9,8},{10,11... | collective-permute-start | bytes 1769480 | tf_op jit(solution)/shard_map/ppermute | solution.py:496
  (62 other events, 446.6 us)
Sparse Core Ops, SparseCore 0:
  207.0 93.0 reduce-scatter.1
